TPU v7x, 32 devices: a whole 2x2x4 slice. The times are simulated.
32 devices in a mesh: blk: 8 (over z, core), tenant: 4 (over y, x).
Axes of the slice: x: 2, y: 2, z: 4, core: 2. Of those that a mesh axis runs over, the one named last changes fastest.
Arguments:
- history_u: bfloat16 [4, 1024, 4096], P('tenant', 'blk'), may hold values from -6 to 6
- span_gate: bfloat16 [4, 64, 4096], P('tenant', 'blk'), may hold values from -6 to 6
- span_key: bfloat16 [4, 64, 4096], P('tenant', 'blk'), may hold values from -6 to 6
- span_value: bfloat16 [4, 64, 4096], P('tenant', 'blk'), may hold values from -6 to 6
- filter_taps: bfloat16 [1088, 256], P(('blk', 'tenant'))
- skip_bias: bfloat16 [4096], P(('blk', 'tenant')), may hold values from -6 to 6
- lengths: int32 [4], P('tenant'), may hold values from 1 to 1024, as said below
- page_owner: int32 [4, 8, 1], P('tenant'), may hold values from 0 to 7; in each aligned block of 8 rows (0 to 7, 8 to 15, ..., all dimensions but the last counted through in order) at most 2 rows name the same one
Outputs:
- mixed: bfloat16 [4, 64, 4096], P('tenant', 'blk')
- new_pool: bfloat16 [4, 128, 4096], P('tenant', 'blk')
Inputs may be any that keep to these rules, and one draw needn't show every extreme that they name: `lengths`: lengths are at least 1, and some tenant uses all 1024 cached positions in every draw. `page_owner`: among the 8 pages of one tenant no device is named more than 2 times, and some device is named exactly 2 times.
All inputs are finite; a program needn't handle non-finite values.
Results may differ from a plain program's by a relative error of at most 0.0044.
Values may be sent and summed in bfloat16 or wider, within the bound.
No kernel may reach another device: no remote copies, remote signals or barrier semaphores. Data moves between devices by JAX's collectives and lax.ppermute only.
A program may use at most 128 MiB of HBM per device.

v0:
```python
import jax
import jax.numpy as jnp
from jax import lax
from jax.sharding import PartitionSpec as P

PAGE = 8
PAGES_DEV = 1
MOST = 2


def toeplitz(window, tile_rows, groups):
    reversed_taps = jnp.transpose(window[::-1])
    repeated = jnp.tile(reversed_taps, (1, tile_rows))
    trimmed = repeated[:, tile_rows - 1 : tile_rows - 1 + tile_rows * (2 * tile_rows - 2)]
    return trimmed.reshape(groups, tile_rows, 2 * tile_rows - 2)[:, :, :tile_rows]


def tile_table(padded_filter, starts, tile_rows, groups):

    def one_window(start):
        window = lax.dynamic_slice_in_dim(padded_filter, start, 2 * tile_rows - 1, 0)
        return toeplitz(window, tile_rows, groups)

    return jax.vmap(one_window)(starts)


def blocked_convolution(table, sources_reversed, target_blocks, source_blocks):

    def per_target(target_index):
        tiles = lax.dynamic_slice_in_dim(table, target_index, source_blocks, 0)
        return jnp.einsum(
            "mgab,mbgc->agc", tiles, sources_reversed, preferred_element_type=jnp.float32
        )

    return lax.map(per_target, jnp.arange(target_blocks, dtype=jnp.int32))


def per_device(
    history_u, span_gate, span_key, span_value, filter_taps, skip_bias, lengths, page_owner
):
    cycle_size = lax.axis_size("blk")
    own_index = lax.axis_index("blk")
    history = history_u[0]
    gate_rows = span_gate[0]
    history_rows, width = history.shape
    span_rows = gate_rows.shape[0]
    span_total = span_rows * cycle_size
    groups = filter_taps.shape[1]
    group_size = width // groups
    taps_all, bias_all = (
        lax.all_gather(filter_taps, ("blk", "tenant"), axis=0, tiled=True),
        lax.all_gather(skip_bias, ("blk", "tenant"), axis=0, tiled=True),
    )
    length = lengths[0]
    own_rows = (span_key[0].astype(jnp.float32) * span_value[0].astype(jnp.float32)).astype(
        jnp.bfloat16
    )
    tile_rows = min(32, history_rows, span_total)
    target_blocks = span_total // tile_rows
    column_history, column_span = (
        lax.all_to_all(history, "blk", split_axis=1, concat_axis=0, tiled=True),
        lax.all_to_all(own_rows, "blk", split_axis=1, concat_axis=0, tiled=True),
    )
    column_width = width // cycle_size
    local_groups = column_width // group_size
    full_rows = column_history.shape[0]
    filter_rows_all = full_rows + span_total
    taps_local = lax.dynamic_slice_in_dim(taps_all, own_index * local_groups, local_groups, 1)
    masked_columns = jnp.where(
        jnp.arange(full_rows, dtype=jnp.int32)[:, None] < length,
        column_history,
        jnp.zeros_like(column_history),
    )
    sequence = jnp.concatenate(
        [masked_columns, jnp.zeros((span_total, column_width), jnp.bfloat16)], axis=0
    )
    sequence = lax.dynamic_update_slice(sequence, column_span, (length, jnp.int32(0)))
    source_blocks = filter_rows_all // tile_rows
    padded_filter = jnp.concatenate(
        [jnp.zeros((filter_rows_all, local_groups), jnp.bfloat16), taps_local], axis=0
    )
    offsets = jnp.arange(target_blocks + source_blocks - 1, dtype=jnp.int32) - (source_blocks - 1)
    starts = length + offsets * tile_rows - (tile_rows - 1) + filter_rows_all
    table = tile_table(padded_filter, starts, tile_rows, local_groups)
    sources_reversed = sequence.reshape(source_blocks, tile_rows, local_groups, group_size)[::-1]
    column_out = blocked_convolution(table, sources_reversed, target_blocks, source_blocks).reshape(
        span_total, column_width
    )
    convolved = lax.all_to_all(column_out, "blk", split_axis=0, concat_axis=1, tiled=True)
    mixed = (
        gate_rows.astype(jnp.float32)
        * (convolved + bias_all.astype(jnp.float32)[None, :] * own_rows.astype(jnp.float32))
    ).astype(jnp.bfloat16)
    owners = page_owner[0, :, 0]
    page_count = owners.shape[0]
    onehot = (owners[:, None] == jnp.arange(cycle_size, dtype=jnp.int32)[None, :]).astype(jnp.int32)
    before = jnp.cumsum(onehot, axis=0) - onehot
    slot_rank = jnp.sum(before * onehot, axis=1)
    selector = (
        (owners[None, :] == own_index)
        & (slot_rank[None, :] == jnp.arange(MOST, dtype=jnp.int32)[:, None])
    ).astype(jnp.bfloat16)
    local_pages = own_rows.reshape(PAGES_DEV, PAGE * width)
    targets_of = lax.dynamic_slice_in_dim(owners, own_index * PAGES_DEV, PAGES_DEV, 0)
    send_mask = targets_of[None, :] == jnp.arange(cycle_size, dtype=jnp.int32)[:, None]
    outgoing = jnp.where(
        send_mask[:, :, None], local_pages[None, :, :], jnp.zeros((), jnp.bfloat16)
    )
    incoming = lax.all_to_all(outgoing, "blk", split_axis=0, concat_axis=0, tiled=True)
    arrived = incoming.reshape(page_count, PAGE * width)
    new_pool = jnp.dot(selector, arrived, preferred_element_type=jnp.float32).astype(jnp.bfloat16)
    return (mixed[None], new_pool.reshape(MOST * PAGE, width)[None])


def solution(mesh):
    return jax.shard_map(
        per_device,
        mesh=mesh,
        in_specs=(
            P("tenant", "blk", None),
            P("tenant", "blk", None),
            P("tenant", "blk", None),
            P("tenant", "blk", None),
            P(("blk", "tenant"), None),
            P(("blk", "tenant")),
            P("tenant"),
            P("tenant", None, None),
        ),
        out_specs=(P("tenant", "blk", None), P("tenant", "blk", None)),
        check_vma=False,
    )
```

profile of v0, /device:TPU:0, one launch (start us, length us, event | category | flops | bytes accessed | tf_op | source)
XLA Modules:
  0.0 384.6 jit_solution(1890351494734139457)
XLA Ops:
  0.6 1.3 constant_dynamic-slice_fusion.1
  2.6 1.5 multiply_convert_fusion.1
  6.5 3.8 reduce
  11.4 6.3 %all-to-all-start.3 = ((bf16[8,2,16384]{2,1,0:T(2,128)(2,1)}), bf16[8,2,16384]{2,1,0:T(2,128)(2,1)S(1)}, u32[]{:S(2)}, u32[]{:S(2)}) async-start(bf16[8,2,16384]{2,1,0:T(2,128)(2,1)} %reshape.183), calls=%async_computation.3 | async-start | bytes 1048576 | tf_op jit(solution)/shard_map/all_to_all | solution.py:109
  17.8 74.8 %all-gather = bf16[32,34,256]{2,1,0:T(8,128)(2,1)S(1)} all-gather(bf16[1,34,256]{2,1,0:T(8,128)(2,1)} %bitcast.67), channel_id=1, replica_groups=mesh['blk'=8,'tenant'=4] {'blk','tenant'}, dimensions={0}, use_global_device_ids=true | all-gather | bytes 574464 | tf_op jit(solution)/shard_map/all_gather | solution.py:51
  93.4 1.3 copy.31
  95.0 3.7 all-to-all-start
  98.8 65.2 %while.12 = (s32[]{:T(128)}, bf16[2176,32]{1,0:T(8,128)(2,1)S(1)}, s32[35,2]{0,1:T(2,128)S(1)}, bf16[35,63,32]{2,1,0:T(8,128)(2,1)}, s32[]{:T(128)}) while((s32[]{:T(128)}, bf16[2176,32]{1,0:T(8,128)(2,1)S(1)}, s32[35,2]{0,1:T(2,128)S(1)}, bf16[35,63,32]{2,1,0:T(8,128)(2,1)}, s32[]{:T(128)}) %tuple.37), condition=%wide.while_cond, body=%wide.while_body.sunk | while | flops 2 | bytes 21529 | solution.py:21
  106.8 1.3 bitcast_dynamic-update-slice_fusion.2
  112.4 1.3 bitcast_dynamic-update-slice_fusion.2
  119.9 1.3 bitcast_dynamic-update-slice_fusion.2
  127.3 1.3 bitcast_dynamic-update-slice_fusion.2
  149.7 1.3 bitcast_dynamic-update-slice_fusion.2
  164.0 2.3 rev.6
  166.6 4.7 %tile.4 = bf16[35,32,32,63]{3,2,1,0:T(8,128)(2,1)} broadcast(bf16[35,32,63]{2,1,0:T(8,128)(2,1)S(1)} %copy.30), dimensions={0,1,3} | broadcast | bytes 4656960 | tf_op jit(solution)/shard_map/vmap()/tile | solution.py:13
  171.3 16.1 %tile.10 = bf16[35,32,2016]{2,1,0:T(8,128)(2,1)} reshape(bf16[35,32,32,63]{3,2,1,0:T(8,128)(2,1)} %tile.4) | data formatting | bytes 9031680 | tf_op jit(solution)/shard_map/vmap()/tile | solution.py:13
  187.4 6.9 %slice.19 = bf16[35,32,1984]{2,1,0:T(8,128)(2,1)} slice(bf16[35,32,2016]{2,1,0:T(8,128)(2,1)} %tile.10), slice={[0:35], [0:32], [31:2015]} | slice | bytes 8888320 | tf_op jit(solution)/shard_map/vmap()/slice | solution.py:14
  194.4 31.4 %reshape.155 = bf16[35,32,32,62]{3,2,1,0:T(8,128)(2,1)} reshape(bf16[35,32,1984]{2,1,0:T(8,128)(2,1)} %slice.19) | data formatting | bytes 8888320 | tf_op jit(solution)/shard_map/vmap()/reshape | solution.py:15
  225.8 14.3 %copy.34 = bf16[35,32,32,32]{0,2,3,1:T(8,128)(2,1)} copy(bf16[35,32,32,32]{3,2,1,0:T(8,128)(2,1)} %bitcast.60) | data formatting | bytes 4587520 | tf_op jit(solution)/shard_map/while | solution.py:35
  240.1 66.1 %all-gather.1 = bf16[32,1,128]{2,1,0:T(2,128)(2,1)S(1)} all-gather(bf16[1,1,128]{2,1,0:T(2,128)(2,1)S(1)} %bitcast.70), channel_id=1, replica_groups=mesh['blk'=8,'tenant'=4] {'blk','tenant'}, dimensions={0}, use_global_device_ids=true | all-gather | bytes 8448 | tf_op jit(solution)/shard_map/all_gather | solution.py:52
  307.1 3.6 all-to-all-start.1
  311.5 4.8 %all-to-all-done.1 = bf16[8,8,512]{2,0,1:T(8,128)(2,1)S(1)} async-done(((bf16[8,8,512]{2,0,1:T(8,128)(2,1)}), bf16[8,8,512]{2,0,1:T(8,128)(2,1)S(1)}, u32[]{:S(2)}, u32[]{:S(2)}) %all-to-all-start.1) | async-done | bytes 65568 | tf_op jit(solution)/shard_map/all_to_all | solution.py:62
  317.5 4.8 %reshape.156 = bf16[34,32,32,16]{1,0,3,2:T(8,128)(2,1)} reshape(bf16[1088,512]{0,1:T(8,128)(2,1)S(1)} %copy.33) | data formatting | bytes 2228224 | tf_op jit(solution)/shard_map/reshape | solution.py:85
  322.3 20.3 %rev.7 = bf16[34,32,32,16]{1,0,3,2:T(8,128)(2,1)} reverse(bf16[34,32,32,16]{1,0,3,2:T(8,128)(2,1)} %reshape.156), dimensions={0} | reverse | bytes 2228224 | tf_op jit(solution)/shard_map/rev | solution.py:85
  342.6 8.7 %copy.35 = bf16[34,32,32,16]{0,3,1,2:T(8,128)(2,1)} copy(bf16[34,32,32,16]{1,0,3,2:T(8,128)(2,1)} %rev.7) | data formatting | bytes 2228224 | tf_op jit(solution)/shard_map/while | solution.py:35
  351.4 19.5 %while.11 = (s32[]{:T(128)}, f32[2,32,32,16]{1,3,2,0:T(8,128)S(1)}, s32[2]{0:T(128)S(1)}, bf16[35,32,32,32]{0,2,3,1:T(8,128)(2,1)}, bf16[34,32,32,16]{0,3,1,2:T(8,128)(2,1)}, /*index=5*/s32[]{:T(128)}, s32[]{:T(128)}, s32[]{:T(128)}) while((s32[]{:T(128)}, f32[2,32,32,16]{1,3,2,0:T(8,128)S(1)}, s32[2]{0:T(128)S(1)}, ...), condition=%wide.region_1.2_spmd, body=%wide.region_0.1_spmd.sunk | while | flops 35651588 | bytes 3670155 | solution.py:35
  354.1 7.0 %fusion.23 = f32[2,32,32,16]{1,3,2,0:T(8,128)S(1)} fusion(f32[2,32,32,16]{1,3,2,0:T(8,128)S(1)} %get-tuple-element.156, s32[]{:T(128)} %get-tuple-element.155, bf16[34,32,32,16]{0,3,1,2:T(8,128)(2,1)} %get-tuple-element.167, bf16[35,32,32,32]{0,2,3,1:T(8,128)(2,1)} %get-tuple-element.166, s32[]{:T(128)S(6)} %select_n.48), kind=kOutput, calls=%fused_computation.3.clone.1 | convolution fusion | flops 35651584 | bytes 3670024 | tf_op jit(solution)/shard_map/while/body/eval_jaxpr/mgab,mbgc->agc/dot_general | solution.py:31
  363.9 7.0 %fusion.23 = f32[2,32,32,16]{1,3,2,0:T(8,128)S(1)} fusion(f32[2,32,32,16]{1,3,2,0:T(8,128)S(1)} %get-tuple-element.156, s32[]{:T(128)} %get-tuple-element.155, bf16[34,32,32,16]{0,3,1,2:T(8,128)(2,1)} %get-tuple-element.167, bf16[35,32,32,32]{0,2,3,1:T(8,128)(2,1)} %get-tuple-element.166, s32[]{:T(128)S(6)} %select_n.48), kind=kOutput, calls=%fused_computation.3.clone.1 | convolution fusion | flops 35651584 | bytes 3670024 | tf_op jit(solution)/shard_map/while/body/eval_jaxpr/mgab,mbgc->agc/dot_general | solution.py:31
  371.8 1.3 all_to_all.50
  373.1 3.4 all-to-all-start.2
  377.8 5.3 %all-to-all-done.2 = f32[8,8,512]{2,1,0:T(8,128)S(1)} async-done(((f32[8,8,512]{2,1,0:T(8,128)}), f32[8,8,512]{2,1,0:T(8,128)S(1)}, u32[]{:S(2)}, u32[]{:S(2)}) %all-to-all-start.2) | async-done | bytes 131104 | tf_op jit(solution)/shard_map/all_to_all | solution.py:89
  383.1 1.5 multiply_convert_fusion
  (143 shorter events, 70.3 us)
Async XLA Ops:
  0.6 92.8 %copy-start = (bf16[1,128,4096]{2,1,0:T(8,128)(2,1)S(1)}, bf16[1,128,4096]{2,1,0:T(8,128)(2,1)}, u32[]{:S(2)}) copy-start(bf16[1,128,4096]{2,1,0:T(8,128)(2,1)} %param.10) | copy-start | bytes 3145732
  11.4 83.6 %all-to-all-start.3 = ((bf16[8,2,16384]{2,1,0:T(2,128)(2,1)}), bf16[8,2,16384]{2,1,0:T(2,128)(2,1)S(1)}, u32[]{:S(2)}, u32[]{:S(2)}) async-start(bf16[8,2,16384]{2,1,0:T(2,128)(2,1)} %reshape.183), calls=%async_computation.3 | async-start | bytes 1048576 | tf_op jit(solution)/shard_map/all_to_all | solution.py:109
  95.0 212.0 %all-to-all-start = ((bf16[128,8,512]{0,2,1:T(8,128)(2,1)}), bf16[128,8,512]{0,2,1:T(8,128)(2,1)S(1)}, u32[]{:S(2)}, u32[]{:S(2)}) async-start(bf16[128,8,512]{0,2,1:T(8,128)(2,1)} %bitcast.8), calls=%async_computation | async-start | bytes 2097152 | tf_op jit(solution)/shard_map/all_to_all | solution.py:61
  225.8 14.3 %copy-start.4 = (bf16[128]{0:T(256)(128)(2,1)S(1)}, bf16[128]{0:T(256)(128)(2,1)}, u32[]{:S(2)}) copy-start(bf16[128]{0:T(256)(128)(2,1)} %param.15) | copy-start | bytes 772
  225.8 80.4 %copy-start.3 = (s32[1,8,1]{1,2,0:T(1,128)S(1)}, s32[1,8,1]{1,2,0:T(1,128)}, u32[]{:S(2)}) copy-start(s32[1,8,1]{1,2,0:T(1,128)} %param.17) | copy-start | bytes 100
  307.1 9.2 %all-to-all-start.1 = ((bf16[8,8,512]{2,0,1:T(8,128)(2,1)}), bf16[8,8,512]{2,0,1:T(8,128)(2,1)S(1)}, u32[]{:S(2)}, u32[]{:S(2)}) async-start(bf16[8,8,512]{2,0,1:T(8,128)(2,1)} %bitcast.11), calls=%async_computation.1 | async-start | bytes 131072 | tf_op jit(solution)/shard_map/all_to_all | solution.py:62
  342.6 8.7 %copy-start.1 = (f32[2,32,32,16]{1,3,2,0:T(8,128)S(1)}, f32[2,32,32,16]{1,3,2,0:T(8,128)}, u32[]{:S(2)}) copy-start(f32[2,32,32,16]{1,3,2,0:T(8,128)} %custom-call) | copy-start | bytes 393220
  351.4 31.8 %copy-start.2 = (bf16[1,8,4096]{2,1,0:T(8,128)(2,1)S(1)}, bf16[1,8,4096]{2,1,0:T(8,128)(2,1)}, u32[]{:S(2)}) copy-start(bf16[1,8,4096]{2,1,0:T(8,128)(2,1)} %param.11) | copy-start | bytes 196612
  373.1 10.1 %all-to-all-start.2 = ((f32[8,8,512]{2,1,0:T(8,128)}), f32[8,8,512]{2,1,0:T(8,128)S(1)}, u32[]{:S(2)}, u32[]{:S(2)}) async-start(f32[8,8,512]{2,1,0:T(8,128)} %all_to_all.50), calls=%async_computation.2 | async-start | bytes 262144 | tf_op jit(solution)/shard_map/all_to_all | solution.py:89
where the time goes:
time: 387 us; the launch traced here: 385 us
  local copies, waits for them, and re-layouts  187 us (48%)
  blocking collectives  141 us (36%)
  starting transfers between devices  17 us (4%)
  matrix products  14.7 us (4%)
  waiting for transfers between devices  10.1 us (3%)
  other arithmetic  8.95 us (2%)
  loops' own time  4.23 us (1%)
    all_gather x1, blocking collectives, per_device(): lax.all_gather(filter_taps, ('blk', 'tenant'), axis=0, tiled=True)  74.8 us
    all_gather x1, blocking collectives, per_device(): lax.all_gather(skip_bias, ('blk', 'tenant'), axis=0, tiled=True)  66.1 us
    gather x105, local copies, waits for them, and re-layouts  65.1 us
    reshape x1, local copies, waits for them, and re-layouts, toeplitz(): trimmed.reshape(groups, tile_rows, 2 * tile_rows - 2)[:, :, :tile_rows]  31.4 us
    while x3, local copies, waits for them, and re-layouts, blocked_convolution(): return lax.map(per_target, jnp.arange(target_blocks, dtype=jnp.int32))  23.9 us
    another operation x2, local copies, waits for them, and re-layouts, toeplitz(): repeated = jnp.tile(reversed_taps, (1, tile_rows))  20.8 us
    rev x1, local copies, waits for them, and re-layouts, per_device(): sequence.reshape(source_blocks, tile_rows, local_groups, group_size)[::-1]  20.3 us
    dot_general x2, matrix products, per_target(): jnp.einsum('mgab,mbgc->agc', tiles, sources_reversed, preferred_element_t...  14 us
  transfers between devices with their start and end apart: 4, of which 2 were waited for; matrix products, arithmetic and copies ran while one was open for 38% of the time, Pallas kernels for 0%

commit v1 on v0

v1 whole, which is shorter than its diff:
```python
import functools

import jax
import jax.numpy as jnp
from jax import lax
from jax.experimental import pallas as pl
from jax.experimental.pallas import tpu as pltpu
from jax.sharding import PartitionSpec as P

PAGE = 8
MOST = 2
LANES = 128

bf16 = jnp.bfloat16
f32 = jnp.float32


def round_up(value, step):
    return -(-value // step) * step


def pack_kernel(n_ten, taps_ref, bias_ref, key_ref, value_ref, send_ref, input_ref):
    n_dev, padded, lanes = send_ref.shape
    rows = taps_ref.shape[0]
    bias = bias_ref[...].astype(f32)
    if bias.shape[1] < lanes:
        bias = jnp.concatenate([bias, jnp.zeros((1, lanes - bias.shape[1]), f32)], axis=1)
    blocks = []
    for half in range(2):
        taps = taps_ref[:, half * lanes : (half + 1) * lanes].astype(f32)
        parts = [taps, bias]
        if padded > rows + 1:
            parts.append(jnp.zeros((padded - rows - 1, lanes), f32))
        blocks.append(jnp.concatenate(parts, axis=0).astype(bf16))
    for dest in range(n_dev):
        send_ref[dest] = blocks[(dest // n_ten) % 2]
    input_ref[...] = (key_ref[...].astype(f32) * value_ref[...].astype(f32)).astype(bf16)


def source_kernel(len_ref, own_ref, peer_ref, own_in_ref, peer_in_ref, out_ref):
    blk = lax.axis_index("blk")
    core = lax.rem(blk, 2)
    rows, width = own_ref.shape
    new = own_in_ref.shape[0]
    start = (blk - core) * rows
    length = len_ref[0]

    def masked(value, first):
        index = first + lax.broadcasted_iota(jnp.int32, (rows, width), 0)
        return jnp.where(index < length, value.astype(f32), 0.0).astype(bf16)

    own_at = pl.multiple_of(core * rows, rows)
    peer_at = pl.multiple_of((1 - core) * rows, rows)
    out_ref[pl.ds(own_at, rows), :] = masked(own_ref[...], start + core * rows)
    out_ref[pl.ds(peer_at, rows), :] = masked(peer_ref[...], start + (1 - core) * rows)
    own_new = own_in_ref[...].astype(f32)
    peer_new = peer_in_ref[...].astype(f32)
    first = jnp.where(core == 0, own_new, peer_new)
    second = jnp.where(core == 0, peer_new, own_new)
    rest = jnp.zeros((LANES - 2 * new, width), f32)
    out_ref[2 * rows :, :] = jnp.concatenate([first, second, rest], axis=0).astype(bf16)


def conv_kernel(fr, span, gsize, len_ref, taps_ref, source_ref, out_ref, history_taps, new_taps):
    n_dev, padded, groups = taps_ref.shape
    rows = source_ref.shape[0] - LANES
    new = 2 * PAGE
    chip = lax.div(lax.axis_index("blk"), 2)
    length = len_ref[0]

    def reversed_taps(top_lag, low_lag, blocks, lanes):
        first = jnp.clip(lax.div(jnp.maximum(low_lag, 0), fr), 0, n_dev - blocks)
        window = taps_ref[pl.ds(first, blocks)].reshape(blocks * padded, groups)
        shape = (blocks, padded, lanes)
        block = lax.broadcasted_iota(jnp.int32, shape, 0)
        row = lax.broadcasted_iota(jnp.int32, shape, 1)
        lane = lax.broadcasted_iota(jnp.int32, shape, 2)
        lag = (first + block) * fr + row
        pick = jnp.where((row < fr) & (lag + lane == top_lag), 1.0, 0.0)
        pick = pick.reshape(blocks * padded, lanes).astype(bf16)
        return lax.dot_general(
            window, pick, (((0,), (0,)), ((), ())), preferred_element_type=f32
        )

    lanes = history_taps.shape[1]
    base = length - chip * rows
    blocks = min(n_dev, -(-(fr - 1 + rows + span - 1) // fr))
    history_taps[...] = reversed_taps(base + span - 1, base - rows + 1, blocks, lanes)
    new_lanes = new_taps.shape[1]
    new_blocks = min(n_dev, -(-span // fr))
    new_taps[...] = reversed_taps(span - 1 - chip * new, 0, new_blocks, new_lanes)

    per = LANES // gsize
    lane_group = lax.broadcasted_iota(jnp.int32, (span, LANES), 1) // gsize

    def chunk(index, carry):
        tiles = []
        for g in range(per):
            at = index * per + g
            line = history_taps[pl.ds(at, 1), :]
            line = jnp.broadcast_to(line, (span, lanes))
            line = pltpu.roll(line, lanes - (span - 1), 1, stride=1, stride_axis=0)
            fresh = new_taps[pl.ds(at, 1), :]
            fresh = jnp.broadcast_to(fresh, (span, new_lanes))
            fresh = pltpu.roll(fresh, new_lanes - (span - 1), 1, stride=1, stride_axis=0)
            tiles.append(
                jnp.concatenate([line[:, :rows], fresh[:, :LANES]], axis=1).astype(bf16)
            )
        toeplitz = jnp.concatenate(tiles, axis=0)
        column = pl.multiple_of(index * LANES, LANES)
        product = jnp.dot(
            toeplitz, source_ref[:, pl.ds(column, LANES)], preferred_element_type=f32
        )
        total = product[:span]
        for g in range(1, per):
            total = jnp.where(lane_group == g, product[g * span : (g + 1) * span], total)
        out_ref[:, pl.ds(column, LANES)] = total.astype(bf16)
        return carry

    lax.fori_loop(0, groups // per, chunk, 0)


def select_kernel(owner_ref, *refs):
    pages, (own_ref, peer_ref) = refs[:-2], refs[-2:]
    blk = lax.axis_index("blk")
    core = lax.rem(blk, 2)
    chip = lax.div(blk, 2)
    n_chip = len(pages)
    own_ref[...] = jnp.zeros_like(own_ref)
    peer_ref[...] = jnp.zeros_like(peer_ref)
    for step, page in enumerate(pages):
        number = 2 * lax.rem(chip + n_chip - step, n_chip) + core
        owner = owner_ref[number]
        rank = jnp.int32(0)
        for other in range(2 * n_chip):
            earlier = (owner_ref[other] == owner) & (other < number)
            rank = rank + earlier.astype(jnp.int32)
        for target, device in ((own_ref, blk), (peer_ref, blk + 1 - 2 * core)):

            @pl.when(owner == device)
            def _(target=target, page=page, rank=rank):
                target[rank] = page[...]


def finish_kernel(parts_ref, gate_ref, input_ref, bias_ref, own_ref, peer_ref, mixed_ref, pool_ref):
    n_blk, _, half = parts_ref.shape
    for core in range(2):
        columns = slice(core * half, (core + 1) * half)
        total = parts_ref[core].astype(f32)
        for chip in range(1, n_blk // 2):
            total = total + parts_ref[2 * chip + core].astype(f32)
        skip = bias_ref[:, columns].astype(f32) * input_ref[:, columns].astype(f32)
        gate = gate_ref[:, columns].astype(f32)
        mixed_ref[:, columns] = (gate * (total + skip)).astype(bf16)
    pool_ref[...] = own_ref[...] + peer_ref[...]


def whole(memory=pltpu.VMEM):
    return pl.BlockSpec(memory_space=memory)


def per_device(
    history_u, span_gate, span_key, span_value, filter_taps, skip_bias, lengths, page_owner
):
    n_blk, n_ten = lax.axis_size("blk"), lax.axis_size("tenant")
    n_dev, n_chip = n_blk * n_ten, n_blk // 2
    history = history_u[0]
    rows, width = history.shape
    half = width // 2
    span_rows = span_key.shape[1]
    span = span_rows * n_blk
    fr, groups = filter_taps.shape
    gsize = width // groups
    padded = round_up(fr + 1, 8)
    bias_width = skip_bias.shape[0]
    swap = [(i, i ^ 1) for i in range(n_blk)]

    send, inputs = pl.pallas_call(
        functools.partial(pack_kernel, n_ten),
        out_shape=(
            jax.ShapeDtypeStruct((n_dev, padded, groups // 2), bf16),
            jax.ShapeDtypeStruct((span_rows, width), bf16),
        ),
        in_specs=[whole()] * 4,
        out_specs=(whole(), whole()),
        name="pack",
    )(filter_taps, skip_bias.reshape(1, bias_width), span_key[0], span_value[0])

    taps = lax.all_to_all(send, ("blk", "tenant"), split_axis=0, concat_axis=0, tiled=True)
    peer_history = lax.ppermute(history, "blk", swap)
    peer_inputs = lax.ppermute(inputs, "blk", swap)
    pages = [inputs]
    for step in range(1, n_chip):
        turn = [(i, (i + 2 * step) % n_blk) for i in range(n_blk)]
        pages.append(lax.ppermute(inputs, "blk", turn))

    def half_block(count):
        return pl.BlockSpec((count, half), lambda i, n: (0, lax.rem(lax.axis_index("blk"), 2)))

    source = pl.pallas_call(
        source_kernel,
        grid_spec=pltpu.PrefetchScalarGridSpec(
            num_scalar_prefetch=1,
            grid=(1,),
            in_specs=[
                half_block(rows),
                half_block(rows),
                half_block(span_rows),
                half_block(span_rows),
            ],
            out_specs=pl.BlockSpec((2 * rows + LANES, half), lambda i, n: (0, 0)),
        ),
        out_shape=jax.ShapeDtypeStruct((2 * rows + LANES, half), bf16),
        name="source",
    )(lengths, history, peer_history, inputs, peer_inputs)

    partial = pl.pallas_call(
        functools.partial(conv_kernel, fr, span, gsize),
        out_shape=jax.ShapeDtypeStruct((span, half), bf16),
        in_specs=[whole(pltpu.SMEM), whole(), whole()],
        out_specs=whole(),
        scratch_shapes=[
            pltpu.VMEM((groups // 2, round_up(2 * rows + span - 1, LANES)), f32),
            pltpu.VMEM((groups // 2, round_up(2 * PAGE + span - 1, LANES)), f32),
        ],
        name="conv",
    )(lengths, taps, source)

    parts = lax.all_to_all(
        partial.reshape(n_blk, span_rows, half), "blk", split_axis=0, concat_axis=0, tiled=True
    )

    slots = jax.ShapeDtypeStruct((MOST, PAGE, width), bf16)
    own_slots, peer_slots = pl.pallas_call(
        select_kernel,
        out_shape=(slots, slots),
        in_specs=[whole(pltpu.SMEM)] + [whole()] * n_chip,
        out_specs=(whole(), whole()),
        name="select",
    )(page_owner.reshape(n_blk), *pages)
    peer_slots = lax.ppermute(peer_slots, "blk", swap)
    bias = taps[:, fr, :bias_width].reshape(1, width)

    mixed, pool = pl.pallas_call(
        finish_kernel,
        out_shape=(jax.ShapeDtypeStruct((span_rows, width), bf16), slots),
        in_specs=[whole()] * 6,
        out_specs=(whole(), whole()),
        name="finish",
    )(parts, span_gate[0], inputs, bias, own_slots, peer_slots)
    return mixed[None], pool.reshape(1, MOST * PAGE, width)


def solution(mesh):
    return jax.shard_map(
        per_device,
        mesh=mesh,
        in_specs=(
            P("tenant", "blk", None),
            P("tenant", "blk", None),
            P("tenant", "blk", None),
            P("tenant", "blk", None),
            P(("blk", "tenant"), None),
            P(("blk", "tenant")),
            P("tenant"),
            P("tenant", None, None),
        ),
        out_specs=(P("tenant", "blk", None), P("tenant", "blk", None)),
        check_vma=False,
    )
```

time: 387 us -> 57.2 us (0.15)
  local copies, waits for them, and re-layouts: 187 us -> 5.13 us
  blocking collectives: 141 us -> 0 us
  Pallas kernels: 0 us -> 16 us
  matrix products: 14.7 us -> 0 us
  other arithmetic: 8.95 us -> 0 us
  waiting for transfers between devices: 10.1 us -> 17.5 us
  loops' own time: 4.23 us -> 0 us
    all_gather x2 -> x0, blocking collectives: 141 us -> none  [the longest x1 74.8 us: per_device(): lax.all_gather(filter_taps, ('blk', 'tenant'), axis=0, tiled=True)]
    gather x105 -> x0, local copies, waits for them, and re-layouts: 65.1 us -> none
    reshape x2 -> x0, local copies, waits for them, and re-layouts: 36.2 us -> none  [the longest x1 31.4 us: toeplitz(): trimmed.reshape(groups, tile_rows, 2 * tile_rows - 2)[:, :, :tile_rows]]
    while x3 -> x0, local copies, waits for them, and re-layouts: 23.9 us -> none  [blocked_convolution(): return lax.map(per_target, jnp.arange(target_blocks, dtype=jnp.int32))]
    rev x2 -> x0, local copies, waits for them, and re-layouts: 22.6 us -> none  [the longest x1 20.3 us: per_device(): sequence.reshape(source_blocks, tile_rows, local_groups, group_size)[::-1]]
    another operation x3 -> x1, local copies, waits for them, and re-layouts: 21.6 us -> 1.45 us  [per_device(): bias = taps[:, fr, :bias_width].reshape(1, width)]
    pallas_call x0 -> x5, Pallas kernels: none -> 16 us  [the longest x1 8.03 us: per_device(): pl.pallas_call(functools.partial(conv_kernel, fr, span, gsize), out_shape...]
    dot_general x3 -> x0, matrix products: 14.7 us -> none  [the longest x2 14 us: per_target(): jnp.einsum('mgab,mbgc->agc', tiles, sources_reversed, preferred_element_t...]
  transfers between devices with their start and end apart: 4 -> 8, of which waited for: 2 -> 3; matrix products, arithmetic and copies ran while one was open for 38% -> 3% of each run, Pallas kernels for 0% -> 25%
where the time goes in v1:
time: 57.2 us; the launch traced here: 56.7 us
  waiting for transfers between devices  17.5 us (31%)
  starting transfers between devices  16.8 us (29%)
  Pallas kernels  16 us (28%)
  local copies, waits for them, and re-layouts  5.13 us (9%)
  between operations  1.33 us (2%)
    ppermute x3, waiting for transfers between devices, per_device(): pages.append(lax.ppermute(inputs, 'blk', turn))  9.17 us
    all_to_all x1, waiting for transfers between devices, per_device(): lax.all_to_all(partial.reshape(n_blk, span_rows, half), 'blk', split_axis...  8.28 us
    pallas_call x1, Pallas kernels, per_device(): pl.pallas_call(functools.partial(conv_kernel, fr, span, gsize), out_shape...  8.03 us
    all_to_all x1, starting transfers between devices, per_device(): lax.all_to_all(send, ('blk', 'tenant'), split_axis=0, concat_axis=0, tile...  6.96 us
    ppermute x3, starting transfers between devices, per_device(): pages.append(lax.ppermute(inputs, 'blk', turn))  5.65 us
    all_to_all x1, starting transfers between devices, per_device(): lax.all_to_all(partial.reshape(n_blk, span_rows, half), 'blk', split_axis...  3.67 us
    unnamed x16, local copies, waits for them, and re-layouts  3.67 us
    pallas_call x1, Pallas kernels, per_device(): pl.pallas_call(source_kernel, grid_spec=pltpu.PrefetchScalarGridSpec(num_...  2.61 us
  transfers between devices with their start and end apart: 8, of which 3 were waited for; matrix products, arithmetic and copies ran while one was open for 3% of the time, Pallas kernels for 25%

profile of v1, /device:TPU:0, one launch (start us, length us, event | category | flops | bytes accessed | tf_op | source)
XLA Modules:
  0.0 56.7 jit_solution(17846432325176459848)
XLA Ops:
  0.6 0.5 collective-permute-start
  1.1 1.7 %pack.1 = (bf16[32,40,128]{2,1,0:T(8,128)(2,1)}, bf16[8,4096]{1,0:T(8,128)(2,1)}) custom-call(bf16[34,256]{1,0:T(8,128)(2,1)} %taps_ref.1, bf16[1,128]{1,0:T(2,128)(2,1)} %bitcast.17, bf16[8,4096]{1,0:T(8,128)(2,1)} %bitcast.14, bf16[8,4096]{1,0:T(8,128)(2,1)} %bitcast.15), custom_call_target="tpu_custom_call" | custom-call | tf_op jit(solution)/shard_map/pack/pallas_call | solution.py:178
  2.9 7.0 %all-to-all-start = ((bf16[32,40,128]{2,1,0:T(8,128)(2,1)}), bf16[32,40,128]{2,1,0:T(8,128)(2,1)S(1)}, u32[]{:S(2)}, u32[]{:S(2)}) async-start(bf16[32,40,128]{2,1,0:T(8,128)(2,1)} %get-tuple-element.8), calls=%async_computation | async-start | bytes 655360 | tf_op jit(solution)/shard_map/all_to_all | solution.py:189
  9.8 1.8 %collective-permute-start.2 = (bf16[8,4096]{1,0:T(8,128)(2,1)}, bf16[8,4096]{1,0:T(8,128)(2,1)S(1)}, u32[]{:S(2)}, u32[]{:S(2)}) collective-permute-start(bf16[8,4096]{1,0:T(8,128)(2,1)} %get-tuple-element.9.own_in_ref.refs_0_.input_ref), channel_id=1, source_target_pairs={{0,8},{4,12},{8,16},{12,20},{16,24},{20,28},{24,0},{28,4},{1,9},{5... | collective-permute-start | bytes 196616 | tf_op jit(solution)/shard_map/ppermute | solution.py:195
  11.6 2.4 %collective-permute-start.3 = (bf16[8,4096]{1,0:T(8,128)(2,1)}, bf16[8,4096]{1,0:T(8,128)(2,1)S(1)}, u32[]{:S(2)}, u32[]{:S(2)}) collective-permute-start(bf16[8,4096]{1,0:T(8,128)(2,1)} %get-tuple-element.9.own_in_ref.refs_0_.input_ref), channel_id=1, source_target_pairs={{0,16},{4,20},{8,24},{12,28},{16,0},{20,4},{24,8},{28,12},{1,17},{... | collective-permute-start | bytes 196616 | tf_op jit(solution)/shard_map/ppermute | solution.py:195
  14.1 1.4 %collective-permute-start.4 = (bf16[8,4096]{1,0:T(8,128)(2,1)}, bf16[8,4096]{1,0:T(8,128)(2,1)S(1)}, u32[]{:S(2)}, u32[]{:S(2)}) collective-permute-start(bf16[8,4096]{1,0:T(8,128)(2,1)} %get-tuple-element.9.own_in_ref.refs_0_.input_ref), channel_id=1, source_target_pairs={{0,24},{4,28},{8,0},{12,4},{16,8},{20,12},{24,16},{28,20},{1,25},{... | collective-permute-start | bytes 196616 | tf_op jit(solution)/shard_map/ppermute | solution.py:195
  15.5 0.0 collective-permute-start.1
  16.1 5.6 %collective-permute-done.2.refs_1_ = bf16[8,4096]{1,0:T(8,128)(2,1)S(1)} collective-permute-done((bf16[8,4096]{1,0:T(8,128)(2,1)}, bf16[8,4096]{1,0:T(8,128)(2,1)S(1)}, u32[]{:S(2)}, u32[]{:S(2)}) %collective-permute-start.2) | collective-permute-done | bytes 65568 | tf_op jit(solution)/shard_map/ppermute | solution.py:195
  21.7 0.0 copy-start.5
  21.7 3.6 %collective-permute-done.3.refs_2_ = bf16[8,4096]{1,0:T(8,128)(2,1)S(1)} collective-permute-done((bf16[8,4096]{1,0:T(8,128)(2,1)}, bf16[8,4096]{1,0:T(8,128)(2,1)S(1)}, u32[]{:S(2)}, u32[]{:S(2)}) %collective-permute-start.3) | collective-permute-done | bytes 65568 | tf_op jit(solution)/shard_map/ppermute | solution.py:195
  25.3 0.0 collective-permute-done.4.refs_3_
  25.3 0.0 copy-done.5
  25.3 0.6 %copy-done.6 = bf16[8,4096]{1,0:T(8,128)(2,1)} copy-done((bf16[8,4096]{1,0:T(8,128)(2,1)}, bf16[8,4096]{1,0:T(8,128)(2,1)S(1)}, u32[]{:S(2)}) %copy-start.6) | copy-done | bytes 65560
  25.9 0.0 copy-done.7
  25.9 1.8 %select.1 = (bf16[2,8,4096]{2,1,0:T(8,128)(2,1)}, bf16[2,8,4096]{2,1,0:T(8,128)(2,1)}) custom-call(s32[8]{0:T(128)} %bitcast.18, bf16[8,4096]{1,0:T(8,128)(2,1)} %get-tuple-element.9.own_in_ref.refs_0_.input_ref, bf16[8,4096]{1,0:T(8,128)(2,1)} %copy-done.5, bf16[8,4096]{1,0:T(8,128)(2,1)} %copy-done.6, bf16[8,4096]{1,0:T(8,128)(2,1)} %copy-done.7), custom_call_target="tpu_custom_call" | custom-call | tf_op jit(solution)/shard_map/select/pallas_call | solution.py:234
  27.7 0.0 collective-permute-start.5
  27.7 0.0 collective-permute-done.1.peer_in_ref
  27.7 0.0 copy-start.4
  27.7 0.0 collective-permute-done.peer_ref
  27.7 0.6 %copy-done.4 = bf16[8,4096]{1,0:T(8,128)(2,1)} copy-done((bf16[8,4096]{1,0:T(8,128)(2,1)}, bf16[8,4096]{1,0:T(8,128)(2,1)S(1)}, u32[]{:S(2)}) %copy-start.4) | copy-done | bytes 65560
  28.4 1.0 %copy-done.2 = bf16[128,4096]{1,0:T(8,128)(2,1)} copy-done((bf16[128,4096]{1,0:T(8,128)(2,1)}, bf16[128,4096]{1,0:T(8,128)(2,1)S(1)}, u32[]{:S(2)}) %copy-start.2) | copy-done | bytes 1048600
  29.3 2.6 %source.1.source_ref = bf16[384,2048]{1,0:T(8,128)(2,1)} custom-call(s32[1]{0:T(128)S(6)} %copy.10.len_ref, bf16[128,4096]{1,0:T(8,128)(2,1)} %bitcast.13, bf16[128,4096]{1,0:T(8,128)(2,1)} %copy-done.2, bf16[8,4096]{1,0:T(8,128)(2,1)} %get-tuple-element.9.own_in_ref.refs_0_.input_ref, bf16[8,4096]{1,0:T(8,128)(2,1)} %copy-done.4), custom_call_target="tpu_custom_call" | custom-call | tf_op jit(solution)/shard_map/source/pallas_call | solution.py:200
  31.9 0.0 all-to-all-done.taps_ref
  31.9 0.7 %copy-done = bf16[32,40,128]{2,1,0:T(8,128)(2,1)} copy-done((bf16[32,40,128]{2,1,0:T(8,128)(2,1)}, bf16[32,40,128]{2,1,0:T(8,128)(2,1)S(1)}, u32[]{:S(2)}) %copy-start) | copy-done | bytes 327704
  32.7 8.0 %conv.1 = bf16[64,2048]{1,0:T(8,128)(2,1)} custom-call(s32[1]{0:T(128)S(6)} %copy.10.len_ref, bf16[32,40,128]{2,1,0:T(8,128)(2,1)} %copy-done, bf16[384,2048]{1,0:T(8,128)(2,1)} %source.1.source_ref), custom_call_target="tpu_custom_call" | custom-call | tf_op jit(solution)/shard_map/conv/pallas_call | solution.py:217
  40.7 3.7 %all-to-all-start.1 = ((bf16[8,8,2048]{2,1,0:T(8,128)(2,1)}), bf16[8,8,2048]{2,1,0:T(8,128)(2,1)S(1)}, u32[]{:S(2)}, u32[]{:S(2)}) async-start(bf16[8,8,2048]{2,1,0:T(8,128)(2,1)} %bitcast.11), calls=%async_computation.1 | async-start | bytes 524288 | tf_op jit(solution)/shard_map/all_to_all | solution.py:229
  44.4 1.5 %slice_bitcast_fusion.bias_ref = bf16[1,4096]{1,0:T(2,128)(2,1)} fusion(bf16[32,40,128]{2,1,0:T(8,128)(2,1)} %copy-done), kind=kLoop, calls=%fused_computation | loop fusion | bytes 16384 | tf_op jit(solution)/shard_map/reshape;squeeze | solution.py:242
  45.8 0.0 collective-permute-done.5.peer_ref
  45.8 8.3 %all-to-all-done.1.parts_ref = bf16[8,8,2048]{2,1,0:T(8,128)(2,1)S(1)} async-done(((bf16[8,8,2048]{2,1,0:T(8,128)(2,1)}), bf16[8,8,2048]{2,1,0:T(8,128)(2,1)S(1)}, u32[]{:S(2)}, u32[]{:S(2)}) %all-to-all-start.1) | async-done | bytes 262176 | tf_op jit(solution)/shard_map/all_to_all | solution.py:229
  54.1 0.0 copy-done.3
  54.1 0.7 %copy-done.1 = bf16[8,8,2048]{2,1,0:T(8,128)(2,1)} copy-done((bf16[8,8,2048]{2,1,0:T(8,128)(2,1)}, bf16[8,8,2048]{2,1,0:T(8,128)(2,1)S(1)}, u32[]{:S(2)}) %copy-start.1) | copy-done | bytes 262168
  54.8 1.9 %finish.1 = (bf16[8,4096]{1,0:T(8,128)(2,1)}, bf16[2,8,4096]{2,1,0:T(8,128)(2,1)}) custom-call(bf16[8,8,2048]{2,1,0:T(8,128)(2,1)} %copy-done.1, bf16[8,4096]{1,0:T(8,128)(2,1)} %bitcast.16, bf16[8,4096]{1,0:T(8,128)(2,1)} %get-tuple-element.9.own_in_ref.refs_0_.input_ref, bf16[1,4096]{1,0:T(2,128)(2,1)} %slice_bitcast_fusion.bias_ref, ...), custom_call_target="tpu_custom_call" | custom-call | tf_op jit(solution)/shard_map/finish/pallas_call | solution.py:244
  (6 shorter events, 0.0 us)
Async XLA Ops:
  0.6 27.1 %collective-permute-start = (bf16[128,4096]{1,0:T(8,128)(2,1)}, bf16[128,4096]{1,0:T(8,128)(2,1)S(1)}, u32[]{:S(2)}, u32[]{:S(2)}) collective-permute-start(bf16[128,4096]{1,0:T(8,128)(2,1)} %bitcast.12), channel_id=1, source_target_pairs={{0,4},{4,0},{8,12},{12,8},{16,20},{20,16},{24,28},{28,24},{1,5},{5... | collective-permute-start | bytes 3145736 | tf_op jit(solution)/shard_map/ppermute | solution.py:190
  2.9 29.1 %all-to-all-start = ((bf16[32,40,128]{2,1,0:T(8,128)(2,1)}), bf16[32,40,128]{2,1,0:T(8,128)(2,1)S(1)}, u32[]{:S(2)}, u32[]{:S(2)}) async-start(bf16[32,40,128]{2,1,0:T(8,128)(2,1)} %get-tuple-element.8), calls=%async_computation | async-start | bytes 655360 | tf_op jit(solution)/shard_map/all_to_all | solution.py:189
  9.8 11.9 %collective-permute-start.2 = (bf16[8,4096]{1,0:T(8,128)(2,1)}, bf16[8,4096]{1,0:T(8,128)(2,1)S(1)}, u32[]{:S(2)}, u32[]{:S(2)}) collective-permute-start(bf16[8,4096]{1,0:T(8,128)(2,1)} %get-tuple-element.9.own_in_ref.refs_0_.input_ref), channel_id=1, source_target_pairs={{0,8},{4,12},{8,16},{12,20},{16,24},{20,28},{24,0},{28,4},{1,9},{5... | collective-permute-start | bytes 196616 | tf_op jit(solution)/shard_map/ppermute | solution.py:195
  11.6 13.7 %collective-permute-start.3 = (bf16[8,4096]{1,0:T(8,128)(2,1)}, bf16[8,4096]{1,0:T(8,128)(2,1)S(1)}, u32[]{:S(2)}, u32[]{:S(2)}) collective-permute-start(bf16[8,4096]{1,0:T(8,128)(2,1)} %get-tuple-element.9.own_in_ref.refs_0_.input_ref), channel_id=1, source_target_pairs={{0,16},{4,20},{8,24},{12,28},{16,0},{20,4},{24,8},{28,12},{1,17},{... | collective-permute-start | bytes 196616 | tf_op jit(solution)/shard_map/ppermute | solution.py:195
  14.1 11.2 %collective-permute-start.4 = (bf16[8,4096]{1,0:T(8,128)(2,1)}, bf16[8,4096]{1,0:T(8,128)(2,1)S(1)}, u32[]{:S(2)}, u32[]{:S(2)}) collective-permute-start(bf16[8,4096]{1,0:T(8,128)(2,1)} %get-tuple-element.9.own_in_ref.refs_0_.input_ref), channel_id=1, source_target_pairs={{0,24},{4,28},{8,0},{12,4},{16,8},{20,12},{24,16},{28,20},{1,25},{... | collective-permute-start | bytes 196616 | tf_op jit(solution)/shard_map/ppermute | solution.py:195
  15.5 12.2 %collective-permute-start.1 = (bf16[8,4096]{1,0:T(8,128)(2,1)}, bf16[8,4096]{1,0:T(8,128)(2,1)S(1)}, u32[]{:S(2)}, u32[]{:S(2)}) collective-permute-start(bf16[8,4096]{1,0:T(8,128)(2,1)} %get-tuple-element.9.own_in_ref.refs_0_.input_ref), channel_id=1, source_target_pairs={{0,4},{4,0},{8,12},{12,8},{16,20},{20,16},{24,28},{28,24},{1,5},{5... | collective-permute-start | bytes 196616 | tf_op jit(solution)/shard_map/ppermute | solution.py:191
  21.7 3.6 %copy-start.5 = (bf16[8,4096]{1,0:T(8,128)(2,1)}, bf16[8,4096]{1,0:T(8,128)(2,1)S(1)}, u32[]{:S(2)}) copy-start(bf16[8,4096]{1,0:T(8,128)(2,1)S(1)} %collective-permute-done.2.refs_1_) | copy-start | bytes 196612
  25.3 0.6 %copy-start.6 = (bf16[8,4096]{1,0:T(8,128)(2,1)}, bf16[8,4096]{1,0:T(8,128)(2,1)S(1)}, u32[]{:S(2)}) copy-start(bf16[8,4096]{1,0:T(8,128)(2,1)S(1)} %collective-permute-done.3.refs_2_) | copy-start | bytes 196612
  25.3 0.6 %copy-start.7 = (bf16[8,4096]{1,0:T(8,128)(2,1)}, bf16[8,4096]{1,0:T(8,128)(2,1)S(1)}, u32[]{:S(2)}) copy-start(bf16[8,4096]{1,0:T(8,128)(2,1)S(1)} %collective-permute-done.4.refs_3_) | copy-start | bytes 196612
  27.7 18.1 %collective-permute-start.5 = (bf16[2,8,4096]{2,1,0:T(8,128)(2,1)}, bf16[2,8,4096]{2,1,0:T(8,128)(2,1)S(1)}, u32[]{:S(2)}, u32[]{:S(2)}) collective-permute-start(bf16[2,8,4096]{2,1,0:T(8,128)(2,1)} %get-tuple-element.11), channel_id=1, source_target_pairs={{0,4},{4,0},{8,12},{12,8},{16,20},{20,16},{24,28},{28,24},{1,5},{5... | collective-permute-start | bytes 393224 | tf_op jit(solution)/shard_map/ppermute | solution.py:241
  27.7 0.6 %copy-start.4 = (bf16[8,4096]{1,0:T(8,128)(2,1)}, bf16[8,4096]{1,0:T(8,128)(2,1)S(1)}, u32[]{:S(2)}) copy-start(bf16[8,4096]{1,0:T(8,128)(2,1)S(1)} %collective-permute-done.1.peer_in_ref) | copy-start | bytes 196612
  28.4 1.0 %copy-start.2 = (bf16[128,4096]{1,0:T(8,128)(2,1)}, bf16[128,4096]{1,0:T(8,128)(2,1)S(1)}, u32[]{:S(2)}) copy-start(bf16[128,4096]{1,0:T(8,128)(2,1)S(1)} %collective-permute-done.peer_ref) | copy-start | bytes 3145732
  31.9 0.7 %copy-start = (bf16[32,40,128]{2,1,0:T(8,128)(2,1)}, bf16[32,40,128]{2,1,0:T(8,128)(2,1)S(1)}, u32[]{:S(2)}) copy-start(bf16[32,40,128]{2,1,0:T(8,128)(2,1)S(1)} %all-to-all-done.taps_ref) | copy-start | bytes 983044
  40.7 13.4 %all-to-all-start.1 = ((bf16[8,8,2048]{2,1,0:T(8,128)(2,1)}), bf16[8,8,2048]{2,1,0:T(8,128)(2,1)S(1)}, u32[]{:S(2)}, u32[]{:S(2)}) async-start(bf16[8,8,2048]{2,1,0:T(8,128)(2,1)} %bitcast.11), calls=%async_computation.1 | async-start | bytes 524288 | tf_op jit(solution)/shard_map/all_to_all | solution.py:229
  45.8 8.3 %copy-start.3 = (bf16[2,8,4096]{2,1,0:T(8,128)(2,1)}, bf16[2,8,4096]{2,1,0:T(8,128)(2,1)S(1)}, u32[]{:S(2)}) copy-start(bf16[2,8,4096]{2,1,0:T(8,128)(2,1)S(1)} %collective-permute-done.5.peer_ref) | copy-start | bytes 393220
  54.1 0.7 %copy-start.1 = (bf16[8,8,2048]{2,1,0:T(8,128)(2,1)}, bf16[8,8,2048]{2,1,0:T(8,128)(2,1)S(1)}, u32[]{:S(2)}) copy-start(bf16[8,8,2048]{2,1,0:T(8,128)(2,1)S(1)} %all-to-all-done.1.parts_ref) | copy-start | bytes 786436

commit v2 on v1

v2 whole, which is shorter than its diff:
```python
import functools

import jax
import jax.numpy as jnp
from jax import lax
from jax.experimental import pallas as pl
from jax.experimental.pallas import tpu as pltpu
from jax.sharding import PartitionSpec as P

PAGE = 8
MOST = 2
LANES = 128

bf16 = jnp.bfloat16
f32 = jnp.float32


def round_up(value, step):
    return -(-value // step) * step


def pack_kernel(n_ten, taps_ref, bias_ref, key_ref, value_ref, send_ref, input_ref):
    n_dev, padded, lanes = send_ref.shape
    rows = taps_ref.shape[0]
    bias = bias_ref[...].astype(f32)
    if bias.shape[1] < lanes:
        bias = jnp.concatenate([bias, jnp.zeros((1, lanes - bias.shape[1]), f32)], axis=1)
    blocks = []
    for half in range(2):
        taps = taps_ref[:, half * lanes : (half + 1) * lanes].astype(f32)
        parts = [taps, bias]
        if padded > rows + 1:
            parts.append(jnp.zeros((padded - rows - 1, lanes), f32))
        blocks.append(jnp.concatenate(parts, axis=0).astype(bf16))
    for dest in range(n_dev):
        send_ref[dest] = blocks[(dest // n_ten) % 2]
    input_ref[...] = (key_ref[...].astype(f32) * value_ref[...].astype(f32)).astype(bf16)


def source_kernel(len_ref, own_ref, peer_ref, out_ref):
    blk = lax.axis_index("blk")
    core = lax.rem(blk, 2)
    rows, width = own_ref.shape
    start = (blk - core) * rows
    length = len_ref[0]

    def masked(value, first):
        index = first + lax.broadcasted_iota(jnp.int32, (rows, width), 0)
        return jnp.where(index < length, value.astype(f32), 0.0).astype(bf16)

    own_at = pl.multiple_of(core * rows, rows)
    peer_at = pl.multiple_of((1 - core) * rows, rows)
    out_ref[pl.ds(own_at, rows), :] = masked(own_ref[...], start + core * rows)
    out_ref[pl.ds(peer_at, rows), :] = masked(peer_ref[...], start + (1 - core) * rows)


def reversed_taps(window, first, fr, top_lag, lanes):
    blocks, padded, groups = window.shape
    shape = (blocks, padded, lanes)
    block = lax.broadcasted_iota(jnp.int32, shape, 0)
    row = lax.broadcasted_iota(jnp.int32, shape, 1)
    lane = lax.broadcasted_iota(jnp.int32, shape, 2)
    lag = (first + block) * fr + row
    pick = jnp.where((row < fr) & (lag + lane == top_lag), 1.0, 0.0)
    pick = pick.reshape(blocks * padded, lanes).astype(bf16)
    return lax.dot_general(
        window.reshape(blocks * padded, groups),
        pick,
        (((0,), (0,)), ((), ())),
        preferred_element_type=f32,
    )


def toeplitz_product(taps_ref, first_group, gsize, outputs, depth, source):
    per = LANES // gsize
    lanes = taps_ref.shape[1]
    tiles = []
    for g in range(per):
        line = jnp.broadcast_to(taps_ref[pl.ds(first_group + g, 1), :], (outputs, lanes))
        line = pltpu.roll(line, lanes - (outputs - 1), 1, stride=1, stride_axis=0)
        tiles.append(line[:, :depth])
    matrix = jnp.concatenate(tiles, axis=0).astype(bf16)
    product = jnp.dot(matrix, source, preferred_element_type=f32)
    group = lax.broadcasted_iota(jnp.int32, (outputs, LANES), 1) // gsize
    total = product[:outputs]
    for g in range(1, per):
        total = jnp.where(group == g, product[g * outputs : (g + 1) * outputs], total)
    return total


def conv_kernel(fr, span, gsize, len_ref, taps_ref, source_ref, out_ref, line_ref):
    n_dev, _, groups = taps_ref.shape
    rows = source_ref.shape[0]
    base = len_ref[0] - lax.div(lax.axis_index("blk"), 2) * rows
    blocks = min(n_dev, -(-(fr - 1 + rows + span - 1) // fr))
    low = jnp.maximum(base - rows + 1, 0)
    first = jnp.clip(lax.div(low, fr), 0, n_dev - blocks)
    line_ref[...] = reversed_taps(
        taps_ref[pl.ds(first, blocks)], first, fr, base + span - 1, line_ref.shape[1]
    )
    per = LANES // gsize
    for index in range(groups // per):
        columns = slice(index * LANES, (index + 1) * LANES)
        total = toeplitz_product(
            line_ref, index * per, gsize, span, rows, source_ref[:, columns]
        )
        out_ref[:, columns] = total.astype(bf16)


def gather_kernel(fr, bias_width, _, taps_ref, *refs):
    pages, (stack_ref, head_ref, bias_ref) = refs[:-3], refs[-3:]
    chip = lax.div(lax.axis_index("blk"), 2)
    n_chip = len(pages)
    for step, page in enumerate(pages):
        stack_ref[lax.rem(chip + n_chip - step, n_chip)] = page[...]
    head_ref[...] = taps_ref[: head_ref.shape[0]]
    each = LANES // bias_width
    for index in range(taps_ref.shape[0] // each):
        row = [
            taps_ref[index * each + i, fr : fr + 1, :bias_width].astype(f32) for i in range(each)
        ]
        row = row[0] if each == 1 else jnp.concatenate(row, axis=1)
        bias_ref[:, index * LANES : (index + 1) * LANES] = row


def span_kernel(
    fr,
    gsize,
    owner_ref,
    own_stack_ref,
    peer_stack_ref,
    own_head_ref,
    peer_head_ref,
    input_ref,
    bias_ref,
    extra_ref,
    pool_ref,
    line_ref,
    source_ref,
):
    blk = lax.axis_index("blk")
    core = lax.rem(blk, 2)
    n_chip, page, width = own_stack_ref.shape
    n_blk = 2 * n_chip
    pool_ref[...] = jnp.zeros_like(pool_ref)
    for chip in range(n_chip):
        for stack, side in ((own_stack_ref, core), (peer_stack_ref, 1 - core)):
            number = 2 * chip + side
            value = stack[chip]
            source_ref[number] = value
            owner = owner_ref[number]
            rank = jnp.int32(0)
            for other in range(n_blk):
                earlier = (owner_ref[other] == owner) & (other < number)
                rank = rank + earlier.astype(jnp.int32)

            @pl.when(owner == blk)
            def _(value=value, rank=rank):
                pool_ref[rank] = value

    groups = own_head_ref.shape[2]
    lanes = line_ref.shape[1]
    top_lag = blk * page + page - 1
    for head, side in ((own_head_ref, core), (peer_head_ref, 1 - core)):
        at = pl.multiple_of(side * groups, groups)
        line_ref[pl.ds(at, groups), :] = reversed_taps(head[...], 0, fr, top_lag, lanes)
    per = LANES // gsize
    for index in range(width // LANES):
        columns = slice(index * LANES, (index + 1) * LANES)
        source = source_ref[:, :, columns].reshape(n_blk * page, LANES)
        total = toeplitz_product(line_ref, index * per, gsize, page, n_blk * page, source)
        skip = bias_ref[:, columns] * input_ref[:, columns].astype(f32)
        extra_ref[:, columns] = total + skip


def finish_kernel(parts_ref, gate_ref, extra_ref, mixed_ref):
    n_blk, _, half = parts_ref.shape
    for core in range(2):
        columns = slice(core * half, (core + 1) * half)
        total = extra_ref[:, columns]
        for chip in range(n_blk // 2):
            total = total + parts_ref[2 * chip + core].astype(f32)
        gate = gate_ref[:, columns].astype(f32)
        mixed_ref[:, columns] = (gate * total).astype(bf16)


def whole(memory=pltpu.VMEM):
    return pl.BlockSpec(memory_space=memory)


def limit(mebibytes):
    return pltpu.CompilerParams(vmem_limit_bytes=mebibytes << 20)


def per_device(
    history_u, span_gate, span_key, span_value, filter_taps, skip_bias, lengths, page_owner
):
    n_blk, n_ten = lax.axis_size("blk"), lax.axis_size("tenant")
    n_dev, n_chip = n_blk * n_ten, n_blk // 2
    history = history_u[0]
    rows, width = history.shape
    half = width // 2
    span_rows = span_key.shape[1]
    span = span_rows * n_blk
    fr, groups = filter_taps.shape
    gsize = width // groups
    padded = round_up(fr + 1, 8)
    bias_width = skip_bias.shape[0]
    swap = [(i, i ^ 1) for i in range(n_blk)]

    send, inputs = pl.pallas_call(
        functools.partial(pack_kernel, n_ten),
        out_shape=(
            jax.ShapeDtypeStruct((n_dev, padded, groups // 2), bf16),
            jax.ShapeDtypeStruct((span_rows, width), bf16),
        ),
        in_specs=[whole()] * 4,
        out_specs=(whole(), whole()),
        compiler_params=limit(8),
        name="pack",
    )(filter_taps, skip_bias.reshape(1, bias_width), span_key[0], span_value[0])

    taps = lax.all_to_all(send, ("blk", "tenant"), split_axis=0, concat_axis=0, tiled=True)
    history, inputs = lax.optimization_barrier((history, inputs))
    peer_history = lax.ppermute(history, "blk", swap)
    pages = [inputs]
    for step in range(1, n_chip):
        turn = [(i, (i + 2 * step) % n_blk) for i in range(n_blk)]
        pages.append(lax.ppermute(inputs, "blk", turn))

    def half_block(count):
        return pl.BlockSpec((count, half), lambda i, n: (0, lax.rem(lax.axis_index("blk"), 2)))

    source = pl.pallas_call(
        source_kernel,
        grid_spec=pltpu.PrefetchScalarGridSpec(
            num_scalar_prefetch=1,
            grid=(1,),
            in_specs=[half_block(rows), half_block(rows)],
            out_specs=pl.BlockSpec((2 * rows, half), lambda i, n: (0, 0)),
        ),
        out_shape=jax.ShapeDtypeStruct((2 * rows, half), bf16),
        compiler_params=limit(8),
        name="source",
    )(lengths, history, peer_history)

    partial = pl.pallas_call(
        functools.partial(conv_kernel, fr, span, gsize),
        out_shape=jax.ShapeDtypeStruct((span, half), bf16),
        in_specs=[whole(pltpu.SMEM), whole(), whole()],
        out_specs=whole(),
        scratch_shapes=[pltpu.VMEM((groups // 2, round_up(2 * rows + span - 1, LANES)), f32)],
        compiler_params=limit(16),
        name="conv",
    )(lengths, taps, source)

    parts = lax.all_to_all(
        partial.reshape(n_blk, span_rows, half), "blk", split_axis=0, concat_axis=0, tiled=True
    )

    stack = jax.ShapeDtypeStruct((n_chip, span_rows, width), bf16)
    head = jax.ShapeDtypeStruct((min(n_dev, -(-span // fr)), padded, groups // 2), bf16)
    own_stack, own_head, bias = pl.pallas_call(
        functools.partial(gather_kernel, fr, bias_width),
        out_shape=(stack, head, jax.ShapeDtypeStruct((1, width), f32)),
        in_specs=[whole(pl.ANY)] + [whole()] * (1 + n_chip),
        out_specs=(whole(),) * 3,
        compiler_params=limit(8),
        name="gather",
    )(partial, taps, *pages)
    peer_stack = lax.ppermute(own_stack, "blk", swap)
    peer_head = lax.ppermute(own_head, "blk", swap)

    extra, pool = pl.pallas_call(
        functools.partial(span_kernel, fr, gsize),
        out_shape=(
            jax.ShapeDtypeStruct((span_rows, width), f32),
            jax.ShapeDtypeStruct((MOST, PAGE, width), bf16),
        ),
        in_specs=[whole(pltpu.SMEM)] + [whole()] * 6,
        out_specs=(whole(), whole()),
        scratch_shapes=[
            pltpu.VMEM((groups, round_up(span + PAGE - 1, LANES)), f32),
            pltpu.VMEM((n_blk, span_rows, width), bf16),
        ],
        compiler_params=limit(8),
        name="span",
    )(page_owner.reshape(n_blk), own_stack, peer_stack, own_head, peer_head, inputs, bias)

    mixed = pl.pallas_call(
        finish_kernel,
        out_shape=jax.ShapeDtypeStruct((span_rows, width), bf16),
        in_specs=[whole()] * 3,
        out_specs=whole(),
        compiler_params=limit(8),
        name="finish",
    )(parts, span_gate[0], extra)
    return mixed[None], pool.reshape(1, MOST * PAGE, width)


def solution(mesh):
    return jax.shard_map(
        per_device,
        mesh=mesh,
        in_specs=(
            P("tenant", "blk", None),
            P("tenant", "blk", None),
            P("tenant", "blk", None),
            P("tenant", "blk", None),
            P(("blk", "tenant"), None),
            P(("blk", "tenant")),
            P("tenant"),
            P("tenant", None, None),
        ),
        out_specs=(P("tenant", "blk", None), P("tenant", "blk", None)),
        check_vma=False,
    )
```

time: 57.2 us -> 49.6 us (0.87)
  Pallas kernels: 16 us -> 5.81 us
  waiting for transfers between devices: 17.5 us -> 19.9 us
    all_to_all x1, waiting for transfers between devices: 0.01 us -> 10.2 us  [per_device(): lax.all_to_all(send, ('blk', 'tenant'), split_axis=0, concat_axis=0, tile...]
    all_to_all x1, waiting for transfers between devices: 8.28 us -> 0.01 us  [per_device(): lax.all_to_all(partial.reshape(n_blk, span_rows, half), 'blk', split_axis...]
    pallas_call x1, Pallas kernels: 8.03 us -> 2.83 us  [per_device(): pl.pallas_call(functools.partial(conv_kernel, fr, span, gsize), out_shape...]
    pallas_call x1, Pallas kernels: 2.61 us -> 0.18 us  [per_device(): pl.pallas_call(source_kernel, grid_spec=pltpu.PrefetchScalarGridSpec(num_...]
    pallas_call x2 -> x3, Pallas kernels: 3.64 us -> 2.02 us  [the longest x1 1.31 us: per_device(): pl.pallas_call(functools.partial(span_kernel, fr, gsize), out_shape=(jax....]
    another operation x1 -> x0, local copies, waits for them, and re-layouts: 1.45 us -> none  [per_device(): bias = taps[:, fr, :bias_width].reshape(1, width)]
    unnamed x16 -> x14, local copies, waits for them, and re-layouts: 3.67 us -> 4.93 us
    ppermute x2, waiting for transfers between devices: 0.01 us -> 1.06 us  [the longest x1 1.05 us: per_device(): peer_head = lax.ppermute(own_head, 'blk', swap)]
  transfers between devices with their start and end apart: 8 -> 8, of which waited for: 3 -> 4; matrix products, arithmetic and copies ran while one was open for 3% -> 0% of each run, Pallas kernels for 25% -> 3%
where the time goes in v2:
time: 49.6 us; the launch traced here: 49.1 us
  waiting for transfers between devices  19.9 us (40%)
  starting transfers between devices  17.2 us (35%)
  Pallas kernels  5.81 us (12%)
  local copies, waits for them, and re-layouts  4.93 us (10%)
  between operations  1.35 us (3%)
    all_to_all x1, waiting for transfers between devices, per_device(): lax.all_to_all(send, ('blk', 'tenant'), split_axis=0, concat_axis=0, tile...  10.2 us
    ppermute x3, waiting for transfers between devices, per_device(): pages.append(lax.ppermute(inputs, 'blk', turn))  8.58 us
    all_to_all x1, starting transfers between devices, per_device(): lax.all_to_all(send, ('blk', 'tenant'), split_axis=0, concat_axis=0, tile...  6.96 us
    ppermute x3, starting transfers between devices, per_device(): pages.append(lax.ppermute(inputs, 'blk', turn))  5.76 us
    unnamed x14, local copies, waits for them, and re-layouts  4.93 us
    all_to_all x1, starting transfers between devices, per_device(): lax.all_to_all(partial.reshape(n_blk, span_rows, half), 'blk', split_axis...  3.41 us
    pallas_call x1, Pallas kernels, per_device(): pl.pallas_call(functools.partial(conv_kernel, fr, span, gsize), out_shape...  2.83 us
    pallas_call x1, Pallas kernels, per_device(): pl.pallas_call(functools.partial(span_kernel, fr, gsize), out_shape=(jax....  1.31 us
  transfers between devices with their start and end apart: 8, of which 4 were waited for; matrix products, arithmetic and copies ran while one was open for 0% of the time, Pallas kernels for 3%

profile of v2, /device:TPU:0, one launch (start us, length us, event | category | flops | bytes accessed | tf_op | source)
XLA Modules:
  0.0 49.1 jit_solution(2308908152978804184)
XLA Ops:
  0.6 0.0 copy-start.5
  0.6 0.6 %copy-done.5 = bf16[128]{0:T(256)(128)(2,1)S(1)} copy-done((bf16[128]{0:T(256)(128)(2,1)S(1)}, bf16[128]{0:T(256)(128)(2,1)}, u32[]{:S(2)}) %copy-start.5) | copy-done | bytes 280
  1.3 0.0 copy-start.1
  1.3 0.8 %copy-done.1 = bf16[1,8,4096]{2,1,0:T(8,128)(2,1)S(1)} copy-done((bf16[1,8,4096]{2,1,0:T(8,128)(2,1)S(1)}, bf16[1,8,4096]{2,1,0:T(8,128)(2,1)}, u32[]{:S(2)}) %copy-start.1) | copy-done | bytes 65560
  2.1 0.0 copy-start.2
  2.1 0.8 %copy-done.2 = bf16[1,8,4096]{2,1,0:T(8,128)(2,1)S(1)} copy-done((bf16[1,8,4096]{2,1,0:T(8,128)(2,1)S(1)}, bf16[1,8,4096]{2,1,0:T(8,128)(2,1)}, u32[]{:S(2)}) %copy-start.2) | copy-done | bytes 65560
  3.0 0.7 %copy-done.4 = bf16[34,256]{1,0:T(8,128)(2,1)S(1)} copy-done((bf16[34,256]{1,0:T(8,128)(2,1)S(1)}, bf16[34,256]{1,0:T(8,128)(2,1)}, u32[]{:S(2)}) %copy-start.4) | copy-done | bytes 17432
  3.7 0.8 %pack.1 = (bf16[32,40,128]{2,1,0:T(8,128)(2,1)}, bf16[8,4096]{1,0:T(8,128)(2,1)S(1)}) custom-call(bf16[34,256]{1,0:T(8,128)(2,1)S(1)} %copy-done.4, bf16[1,128]{1,0:T(2,128)(2,1)S(1)} %bitcast.14, bf16[8,4096]{1,0:T(8,128)(2,1)S(1)} %bitcast.11, bf16[8,4096]{1,0:T(8,128)(2,1)S(1)} %bitcast.12), custom_call_target="tpu_custom_call" | custom-call | tf_op jit(solution)/shard_map/pack/pallas_call | solution.py:211
  4.5 0.5 collective-permute-start
  4.9 7.0 %all-to-all-start = ((bf16[32,40,128]{2,1,0:T(8,128)(2,1)}), bf16[32,40,128]{2,1,0:T(8,128)(2,1)S(1)}, u32[]{:S(2)}, u32[]{:S(2)}) async-start(bf16[32,40,128]{2,1,0:T(8,128)(2,1)} %get-tuple-element.11), calls=%async_computation | async-start | bytes 655360 | tf_op jit(solution)/shard_map/all_to_all | solution.py:223
  12.5 0.0 collective-permute-done.peer_ref
  12.5 0.0 copy-start
  12.6 1.2 %copy-done = bf16[1,128,4096]{2,1,0:T(8,128)(2,1)S(1)} copy-done((bf16[1,128,4096]{2,1,0:T(8,128)(2,1)S(1)}, bf16[1,128,4096]{2,1,0:T(8,128)(2,1)}, u32[]{:S(2)}) %copy-start) | copy-done | bytes 1048600
  13.8 0.2 source.1.source_ref
  14.0 10.2 %all-to-all-done.taps_ref = bf16[32,40,128]{2,1,0:T(8,128)(2,1)S(1)} async-done(((bf16[32,40,128]{2,1,0:T(8,128)(2,1)}), bf16[32,40,128]{2,1,0:T(8,128)(2,1)S(1)}, u32[]{:S(2)}, u32[]{:S(2)}) %all-to-all-start) | async-done | bytes 327712 | tf_op jit(solution)/shard_map/all_to_all | solution.py:223
  24.2 2.8 %conv.1._ = bf16[64,2048]{1,0:T(8,128)(2,1)} custom-call(s32[1]{0:T(128)S(6)} %copy.10.len_ref, bf16[32,40,128]{2,1,0:T(8,128)(2,1)S(1)} %all-to-all-done.taps_ref, bf16[256,2048]{1,0:T(8,128)(2,1)S(1)} %source.1.source_ref), custom_call_target="tpu_custom_call" | custom-call | tf_op jit(solution)/shard_map/conv/pallas_call | solution.py:247
  27.0 3.4 %all-to-all-start.1 = ((bf16[8,8,2048]{2,1,0:T(8,128)(2,1)}), bf16[8,8,2048]{2,1,0:T(8,128)(2,1)S(1)}, u32[]{:S(2)}, u32[]{:S(2)}) async-start(bf16[8,8,2048]{2,1,0:T(8,128)(2,1)} %bitcast.4), calls=%async_computation.1 | async-start | bytes 524288 | tf_op jit(solution)/shard_map/all_to_all | solution.py:257
  30.4 1.9 %collective-permute-start.1 = (bf16[8,4096]{1,0:T(8,128)(2,1)S(1)}, bf16[8,4096]{1,0:T(8,128)(2,1)S(1)}, u32[]{:S(2)}, u32[]{:S(2)}) collective-permute-start(bf16[8,4096]{1,0:T(8,128)(2,1)S(1)} %get-tuple-element.14.refs_0_.input_ref), channel_id=1, source_target_pairs={{0,8},{4,12},{8,16},{12,20},{16,24},{20,28},{24,0},{28,4},{1,9},{5... | collective-permute-start | bytes 196616 | tf_op jit(solution)/shard_map/ppermute | solution.py:229
  32.4 2.4 %collective-permute-start.2 = (bf16[8,4096]{1,0:T(8,128)(2,1)S(1)}, bf16[8,4096]{1,0:T(8,128)(2,1)S(1)}, u32[]{:S(2)}, u32[]{:S(2)}) collective-permute-start(bf16[8,4096]{1,0:T(8,128)(2,1)S(1)} %get-tuple-element.14.refs_0_.input_ref), channel_id=1, source_target_pairs={{0,16},{4,20},{8,24},{12,28},{16,0},{20,4},{24,8},{28,12},{1,17},{... | collective-permute-start | bytes 196616 | tf_op jit(solution)/shard_map/ppermute | solution.py:229
  34.7 1.4 %collective-permute-start.3 = (bf16[8,4096]{1,0:T(8,128)(2,1)S(1)}, bf16[8,4096]{1,0:T(8,128)(2,1)S(1)}, u32[]{:S(2)}, u32[]{:S(2)}) collective-permute-start(bf16[8,4096]{1,0:T(8,128)(2,1)S(1)} %get-tuple-element.14.refs_0_.input_ref), channel_id=1, source_target_pairs={{0,24},{4,28},{8,0},{12,4},{16,8},{20,12},{24,16},{28,20},{1,25},{... | collective-permute-start | bytes 196616 | tf_op jit(solution)/shard_map/ppermute | solution.py:229
  36.2 5.4 %collective-permute-done.1.refs_1_ = bf16[8,4096]{1,0:T(8,128)(2,1)S(1)} collective-permute-done((bf16[8,4096]{1,0:T(8,128)(2,1)S(1)}, bf16[8,4096]{1,0:T(8,128)(2,1)S(1)}, u32[]{:S(2)}, u32[]{:S(2)}) %collective-permute-start.1) | collective-permute-done | bytes 65568 | tf_op jit(solution)/shard_map/ppermute | solution.py:229
  41.6 3.2 %collective-permute-done.2.refs_2_ = bf16[8,4096]{1,0:T(8,128)(2,1)S(1)} collective-permute-done((bf16[8,4096]{1,0:T(8,128)(2,1)S(1)}, bf16[8,4096]{1,0:T(8,128)(2,1)S(1)}, u32[]{:S(2)}, u32[]{:S(2)}) %collective-permute-start.2) | collective-permute-done | bytes 65568 | tf_op jit(solution)/shard_map/ppermute | solution.py:229
  44.8 0.0 collective-permute-done.3.refs_3_
  44.8 0.1 collective-permute-start.4
  44.9 0.5 %collective-permute-start.5 = (bf16[2,40,128]{2,1,0:T(8,128)(2,1)S(1)}, bf16[2,40,128]{2,1,0:T(8,128)(2,1)S(1)}, u32[]{:S(2)}, u32[]{:S(2)}) collective-permute-start(bf16[2,40,128]{2,1,0:T(8,128)(2,1)S(1)} %get-tuple-element.16.own_head_ref), channel_id=1, source_target_pairs={{0,4},{4,0},{8,12},{12,8},{16,20},{20,16},{24,28},{28,24},{1,5},{5... | collective-permute-start | bytes 61448 | tf_op jit(solution)/shard_map/ppermute | solution.py:272
  45.4 1.1 %collective-permute-done.5.peer_head_ref = bf16[2,40,128]{2,1,0:T(8,128)(2,1)S(1)} collective-permute-done((bf16[2,40,128]{2,1,0:T(8,128)(2,1)S(1)}, bf16[2,40,128]{2,1,0:T(8,128)(2,1)S(1)}, u32[]{:S(2)}, u32[]{:S(2)}) %collective-permute-start.5) | collective-permute-done | bytes 20512 | tf_op jit(solution)/shard_map/ppermute | solution.py:272
  46.5 0.0 collective-permute-done.4.peer_stack_ref
  46.5 0.7 %copy-done.6 = s32[1,8,1]{1,2,0:T(1,128)S(1)} copy-done((s32[1,8,1]{1,2,0:T(1,128)S(1)}, s32[1,8,1]{1,2,0:T(1,128)}, u32[]{:S(2)}) %copy-start.6) | copy-done | bytes 56
  47.1 1.3 %span.1 = (f32[8,4096]{1,0:T(8,128)S(1)}, bf16[2,8,4096]{2,1,0:T(8,128)(2,1)}) custom-call(s32[8]{0:T(128)S(1)} %bitcast.15, bf16[4,8,4096]{2,1,0:T(8,128)(2,1)S(1)} %get-tuple-element.15.own_stack_ref, bf16[4,8,4096]{2,1,0:T(8,128)(2,1)S(1)} %collective-permute-done.4.peer_stack_ref, bf16[2,40,128]{2,1,0:T(8,128)(2,1)S(1)} %get-tuple-element.16.own_head_ref, ...), custom_call_target="tpu_custom_call" | custom-call | tf_op jit(solution)/shard_map/span/pallas_call | solution.py:274
  48.4 0.0 all-to-all-done.1.parts_ref
  48.4 0.0 copy-done.3
  48.4 0.7 %finish.1 = bf16[8,4096]{1,0:T(8,128)(2,1)} custom-call(bf16[8,8,2048]{2,1,0:T(8,128)(2,1)S(1)} %all-to-all-done.1.parts_ref, bf16[8,4096]{1,0:T(8,128)(2,1)S(1)} %bitcast.13, f32[8,4096]{1,0:T(8,128)S(1)} %get-tuple-element.18.extra_ref), custom_call_target="tpu_custom_call" | custom-call | tf_op jit(solution)/shard_map/finish/pallas_call | solution.py:290
  (4 shorter events, 0.0 us)
Async XLA Ops:
  0.6 0.7 %copy-start.5 = (bf16[128]{0:T(256)(128)(2,1)S(1)}, bf16[128]{0:T(256)(128)(2,1)}, u32[]{:S(2)}) copy-start(bf16[128]{0:T(256)(128)(2,1)} %param.13) | copy-start | bytes 772
  1.3 0.8 %copy-start.1 = (bf16[1,8,4096]{2,1,0:T(8,128)(2,1)S(1)}, bf16[1,8,4096]{2,1,0:T(8,128)(2,1)}, u32[]{:S(2)}) copy-start(bf16[1,8,4096]{2,1,0:T(8,128)(2,1)} %param.10) | copy-start | bytes 196612
  2.1 0.8 %copy-start.2 = (bf16[1,8,4096]{2,1,0:T(8,128)(2,1)S(1)}, bf16[1,8,4096]{2,1,0:T(8,128)(2,1)}, u32[]{:S(2)}) copy-start(bf16[1,8,4096]{2,1,0:T(8,128)(2,1)} %param.11) | copy-start | bytes 196612
  3.0 0.7 %copy-start.4 = (bf16[34,256]{1,0:T(8,128)(2,1)S(1)}, bf16[34,256]{1,0:T(8,128)(2,1)}, u32[]{:S(2)}) copy-start(bf16[34,256]{1,0:T(8,128)(2,1)} %taps_ref.1) | copy-start | bytes 52228
  4.5 8.1 %collective-permute-start = (bf16[128,4096]{1,0:T(8,128)(2,1)}, bf16[128,4096]{1,0:T(8,128)(2,1)S(1)}, u32[]{:S(2)}, u32[]{:S(2)}) collective-permute-start(bf16[128,4096]{1,0:T(8,128)(2,1)} %bitcast.9), channel_id=1, source_target_pairs={{0,4},{4,0},{8,12},{12,8},{16,20},{20,16},{24,28},{28,24},{1,5},{5... | collective-permute-start | bytes 3145736 | tf_op jit(solution)/shard_map/ppermute | solution.py:225
  4.9 19.3 %all-to-all-start = ((bf16[32,40,128]{2,1,0:T(8,128)(2,1)}), bf16[32,40,128]{2,1,0:T(8,128)(2,1)S(1)}, u32[]{:S(2)}, u32[]{:S(2)}) async-start(bf16[32,40,128]{2,1,0:T(8,128)(2,1)} %get-tuple-element.11), calls=%async_computation | async-start | bytes 655360 | tf_op jit(solution)/shard_map/all_to_all | solution.py:223
  12.5 1.2 %copy-start = (bf16[1,128,4096]{2,1,0:T(8,128)(2,1)S(1)}, bf16[1,128,4096]{2,1,0:T(8,128)(2,1)}, u32[]{:S(2)}) copy-start(bf16[1,128,4096]{2,1,0:T(8,128)(2,1)} %param.8) | copy-start | bytes 3145732
  27.0 21.4 %all-to-all-start.1 = ((bf16[8,8,2048]{2,1,0:T(8,128)(2,1)}), bf16[8,8,2048]{2,1,0:T(8,128)(2,1)S(1)}, u32[]{:S(2)}, u32[]{:S(2)}) async-start(bf16[8,8,2048]{2,1,0:T(8,128)(2,1)} %bitcast.4), calls=%async_computation.1 | async-start | bytes 524288 | tf_op jit(solution)/shard_map/all_to_all | solution.py:257
  30.4 11.1 %collective-permute-start.1 = (bf16[8,4096]{1,0:T(8,128)(2,1)S(1)}, bf16[8,4096]{1,0:T(8,128)(2,1)S(1)}, u32[]{:S(2)}, u32[]{:S(2)}) collective-permute-start(bf16[8,4096]{1,0:T(8,128)(2,1)S(1)} %get-tuple-element.14.refs_0_.input_ref), channel_id=1, source_target_pairs={{0,8},{4,12},{8,16},{12,20},{16,24},{20,28},{24,0},{28,4},{1,9},{5... | collective-permute-start | bytes 196616 | tf_op jit(solution)/shard_map/ppermute | solution.py:229
  32.4 12.4 %collective-permute-start.2 = (bf16[8,4096]{1,0:T(8,128)(2,1)S(1)}, bf16[8,4096]{1,0:T(8,128)(2,1)S(1)}, u32[]{:S(2)}, u32[]{:S(2)}) collective-permute-start(bf16[8,4096]{1,0:T(8,128)(2,1)S(1)} %get-tuple-element.14.refs_0_.input_ref), channel_id=1, source_target_pairs={{0,16},{4,20},{8,24},{12,28},{16,0},{20,4},{24,8},{28,12},{1,17},{... | collective-permute-start | bytes 196616 | tf_op jit(solution)/shard_map/ppermute | solution.py:229
  34.7 10.0 %collective-permute-start.3 = (bf16[8,4096]{1,0:T(8,128)(2,1)S(1)}, bf16[8,4096]{1,0:T(8,128)(2,1)S(1)}, u32[]{:S(2)}, u32[]{:S(2)}) collective-permute-start(bf16[8,4096]{1,0:T(8,128)(2,1)S(1)} %get-tuple-element.14.refs_0_.input_ref), channel_id=1, source_target_pairs={{0,24},{4,28},{8,0},{12,4},{16,8},{20,12},{24,16},{28,20},{1,25},{... | collective-permute-start | bytes 196616 | tf_op jit(solution)/shard_map/ppermute | solution.py:229
  44.8 1.6 %collective-permute-start.4 = (bf16[4,8,4096]{2,1,0:T(8,128)(2,1)S(1)}, bf16[4,8,4096]{2,1,0:T(8,128)(2,1)S(1)}, u32[]{:S(2)}, u32[]{:S(2)}) collective-permute-start(bf16[4,8,4096]{2,1,0:T(8,128)(2,1)S(1)} %get-tuple-element.15.own_stack_ref), channel_id=1, source_target_pairs={{0,4},{4,0},{8,12},{12,8},{16,20},{20,16},{24,28},{28,24},{1,5},{5... | collective-permute-start | bytes 786440 | tf_op jit(solution)/shard_map/ppermute | solution.py:271
  44.9 1.6 %collective-permute-start.5 = (bf16[2,40,128]{2,1,0:T(8,128)(2,1)S(1)}, bf16[2,40,128]{2,1,0:T(8,128)(2,1)S(1)}, u32[]{:S(2)}, u32[]{:S(2)}) collective-permute-start(bf16[2,40,128]{2,1,0:T(8,128)(2,1)S(1)} %get-tuple-element.16.own_head_ref), channel_id=1, source_target_pairs={{0,4},{4,0},{8,12},{12,8},{16,20},{20,16},{24,28},{28,24},{1,5},{5... | collective-permute-start | bytes 61448 | tf_op jit(solution)/shard_map/ppermute | solution.py:272
  46.5 0.7 %copy-start.6 = (s32[1,8,1]{1,2,0:T(1,128)S(1)}, s32[1,8,1]{1,2,0:T(1,128)}, u32[]{:S(2)}) copy-start(s32[1,8,1]{1,2,0:T(1,128)} %param.15) | copy-start | bytes 100
  47.1 1.3 %copy-start.3 = (bf16[1,8,4096]{2,1,0:T(8,128)(2,1)S(1)}, bf16[1,8,4096]{2,1,0:T(8,128)(2,1)}, u32[]{:S(2)}) copy-start(bf16[1,8,4096]{2,1,0:T(8,128)(2,1)} %param.9) | copy-start | bytes 196612

commit v3 on v2

--- a/solution.py
+++ b/solution.py
@@ -19,7 +19,19 @@
     return -(-value // step) * step
 
 
-def pack_kernel(n_ten, taps_ref, bias_ref, key_ref, value_ref, send_ref, input_ref):
+def pack_kernel(n_ten, taps_hbm, bias_hbm, key_hbm, value_hbm, send_ref, input_ref, *scratch):
+    held, sems = scratch[:-1], scratch[-1]
+    copies = [
+        pltpu.make_async_copy(source, target, sems.at[i])
+        for i, (source, target) in enumerate(
+            zip((taps_hbm, bias_hbm, key_hbm, value_hbm), held, strict=True)
+        )
+    ]
+    for copy in copies:
+        copy.start()
+    for copy in copies:
+        copy.wait()
+    taps_ref, bias_ref, key_ref, value_ref = held
     n_dev, padded, lanes = send_ref.shape
     rows = taps_ref.shape[0]
     bias = bias_ref[...].astype(f32)
@@ -214,9 +226,16 @@
             jax.ShapeDtypeStruct((n_dev, padded, groups // 2), bf16),
             jax.ShapeDtypeStruct((span_rows, width), bf16),
         ),
-        in_specs=[whole()] * 4,
+        in_specs=[whole(pltpu.HBM)] * 4,
         out_specs=(whole(), whole()),
-        compiler_params=limit(8),
+        scratch_shapes=[
+            pltpu.VMEM((fr, groups), bf16),
+            pltpu.VMEM((1, bias_width), bf16),
+            pltpu.VMEM((span_rows, width), bf16),
+            pltpu.VMEM((span_rows, width), bf16),
+            pltpu.SemaphoreType.DMA((4,)),
+        ],
+        compiler_params=limit(58),
         name="pack",
     )(filter_taps, skip_bias.reshape(1, bias_width), span_key[0], span_value[0])
 
@@ -244,6 +263,7 @@
         name="source",
     )(lengths, history, peer_history)
 
+    taps, source, *pages = lax.optimization_barrier((taps, source, *pages))
     partial = pl.pallas_call(
         functools.partial(conv_kernel, fr, span, gsize),
         out_shape=jax.ShapeDtypeStruct((span, half), bf16),

time: 49.6 us -> 42.6 us (0.86)
  waiting for transfers between devices: 19.9 us -> 14.8 us
  local copies, waits for them, and re-layouts: 4.93 us -> 1.88 us
  Pallas kernels: 5.81 us -> 6.78 us
    all_to_all x1, waiting for transfers between devices: 10.2 us -> 0.01 us  [per_device(): lax.all_to_all(send, ('blk', 'tenant'), split_axis=0, concat_axis=0, tile...]
    all_to_all x1, waiting for transfers between devices: 0.01 us -> 5.96 us  [per_device(): lax.all_to_all(partial.reshape(n_blk, span_rows, half), 'blk', split_axis...]
    unnamed x14 -> x8, local copies, waits for them, and re-layouts: 4.93 us -> 1.88 us
    pallas_call x1, Pallas kernels: 0.77 us -> 1.72 us  [per_device(): pl.pallas_call(functools.partial(pack_kernel, n_ten), out_shape=(jax.Shap...]
    ppermute x3, waiting for transfers between devices: 8.58 us -> 7.74 us  [per_device(): pages.append(lax.ppermute(inputs, 'blk', turn))]
    ppermute x1, starting transfers between devices: 0.07 us -> 0.57 us  [per_device(): peer_stack = lax.ppermute(own_stack, 'blk', swap)]
  transfers between devices with their start and end apart: 8 -> 8, of which waited for: 4 -> 4; matrix products, arithmetic and copies ran while one was open for 0% -> 0% of each run, Pallas kernels for 3% -> 4%
where the time goes in v3:
time: 42.6 us; the launch traced here: 42.2 us
  starting transfers between devices  17.4 us (41%)
  waiting for transfers between devices  14.8 us (35%)
  Pallas kernels  6.78 us (16%)
  local copies, waits for them, and re-layouts  1.88 us (4%)
  between operations  1.34 us (3%)
    ppermute x3, waiting for transfers between devices, per_device(): pages.append(lax.ppermute(inputs, 'blk', turn))  7.74 us
    all_to_all x1, starting transfers between devices, per_device(): lax.all_to_all(send, ('blk', 'tenant'), split_axis=0, concat_axis=0, tile...  6.96 us
    all_to_all x1, waiting for transfers between devices, per_device(): lax.all_to_all(partial.reshape(n_blk, span_rows, half), 'blk', split_axis...  5.96 us
    ppermute x3, starting transfers between devices, per_device(): pages.append(lax.ppermute(inputs, 'blk', turn))  5.65 us
    all_to_all x1, starting transfers between devices, per_device(): lax.all_to_all(partial.reshape(n_blk, span_rows, half), 'blk', split_axis...  3.58 us
    pallas_call x1, Pallas kernels, per_device(): pl.pallas_call(functools.partial(conv_kernel, fr, span, gsize), out_shape...  2.85 us
    unnamed x8, local copies, waits for them, and re-layouts  1.88 us
    pallas_call x1, Pallas kernels, per_device(): pl.pallas_call(functools.partial(pack_kernel, n_ten), out_shape=(jax.Shap...  1.72 us
  transfers between devices with their start and end apart: 8, of which 4 were waited for; matrix products, arithmetic and copies ran while one was open for 0% of the time, Pallas kernels for 4%

profile of v3, /device:TPU:0, one launch (start us, length us, event | category | flops | bytes accessed | tf_op | source)
XLA Modules:
  0.0 42.2 jit_solution(13041850119551824405)
XLA Ops:
  0.6 1.7 %pack.1 = (bf16[32,40,128]{2,1,0:T(8,128)(2,1)}, bf16[8,4096]{1,0:T(8,128)(2,1)}) custom-call(bf16[34,256]{1,0:T(8,128)(2,1)} %taps_hbm.1, bf16[1,128]{1,0:T(2,128)(2,1)} %bitcast.16, bf16[8,4096]{1,0:T(8,128)(2,1)} %bitcast.13, bf16[8,4096]{1,0:T(8,128)(2,1)} %bitcast.14), custom_call_target="tpu_custom_call" | custom-call | tf_op jit(solution)/shard_map/pack/pallas_call | solution.py:223
  2.4 0.5 %collective-permute-start = (bf16[128,4096]{1,0:T(8,128)(2,1)}, bf16[128,4096]{1,0:T(8,128)(2,1)S(1)}, u32[]{:S(2)}, u32[]{:S(2)}) collective-permute-start(bf16[128,4096]{1,0:T(8,128)(2,1)} %bitcast.9), channel_id=1, source_target_pairs={{0,4},{4,0},{8,12},{12,8},{16,20},{20,16},{24,28},{28,24},{1,5},{5... | collective-permute-start | bytes 3145736 | tf_op jit(solution)/shard_map/ppermute | solution.py:244
  2.9 0.0 copy-start.1
  2.9 7.0 %all-to-all-start = ((bf16[32,40,128]{2,1,0:T(8,128)(2,1)}), bf16[32,40,128]{2,1,0:T(8,128)(2,1)S(1)}, u32[]{:S(2)}, u32[]{:S(2)}) async-start(bf16[32,40,128]{2,1,0:T(8,128)(2,1)} %get-tuple-element.17), calls=%async_computation | async-start | bytes 655360 | tf_op jit(solution)/shard_map/all_to_all | solution.py:242
  9.8 0.0 copy-done.1
  9.9 1.8 %collective-permute-start.1 = (bf16[8,4096]{1,0:T(8,128)(2,1)S(1)}, bf16[8,4096]{1,0:T(8,128)(2,1)S(1)}, u32[]{:S(2)}, u32[]{:S(2)}) collective-permute-start(bf16[8,4096]{1,0:T(8,128)(2,1)S(1)} %copy-done.1), channel_id=1, source_target_pairs={{0,8},{4,12},{8,16},{12,20},{16,24},{20,28},{24,0},{28,4},{1,9},{5... | collective-permute-start | bytes 196616 | tf_op jit(solution)/shard_map/ppermute | solution.py:248
  11.7 2.4 %collective-permute-start.2 = (bf16[8,4096]{1,0:T(8,128)(2,1)S(1)}, bf16[8,4096]{1,0:T(8,128)(2,1)S(1)}, u32[]{:S(2)}, u32[]{:S(2)}) collective-permute-start(bf16[8,4096]{1,0:T(8,128)(2,1)S(1)} %copy-done.1), channel_id=1, source_target_pairs={{0,16},{4,20},{8,24},{12,28},{16,0},{20,4},{24,8},{28,12},{1,17},{... | collective-permute-start | bytes 196616 | tf_op jit(solution)/shard_map/ppermute | solution.py:248
  14.1 1.4 %collective-permute-start.3 = (bf16[8,4096]{1,0:T(8,128)(2,1)S(1)}, bf16[8,4096]{1,0:T(8,128)(2,1)S(1)}, u32[]{:S(2)}, u32[]{:S(2)}) collective-permute-start(bf16[8,4096]{1,0:T(8,128)(2,1)S(1)} %copy-done.1), channel_id=1, source_target_pairs={{0,24},{4,28},{8,0},{12,4},{16,8},{20,12},{24,16},{28,20},{1,25},{... | collective-permute-start | bytes 196616 | tf_op jit(solution)/shard_map/ppermute | solution.py:248
  16.2 0.0 collective-permute-done.peer_ref
  16.2 0.0 copy-start
  16.2 1.2 %copy-done = bf16[1,128,4096]{2,1,0:T(8,128)(2,1)S(1)} copy-done((bf16[1,128,4096]{2,1,0:T(8,128)(2,1)S(1)}, bf16[1,128,4096]{2,1,0:T(8,128)(2,1)}, u32[]{:S(2)}) %copy-start) | copy-done | bytes 1048600
  17.4 0.2 source.1.source_ref
  17.6 4.1 %collective-permute-done.1.refs_1_ = bf16[8,4096]{1,0:T(8,128)(2,1)S(1)} collective-permute-done((bf16[8,4096]{1,0:T(8,128)(2,1)S(1)}, bf16[8,4096]{1,0:T(8,128)(2,1)S(1)}, u32[]{:S(2)}, u32[]{:S(2)}) %collective-permute-start.1) | collective-permute-done | bytes 65568 | tf_op jit(solution)/shard_map/ppermute | solution.py:248
  21.7 3.6 %collective-permute-done.2.refs_2_ = bf16[8,4096]{1,0:T(8,128)(2,1)S(1)} collective-permute-done((bf16[8,4096]{1,0:T(8,128)(2,1)S(1)}, bf16[8,4096]{1,0:T(8,128)(2,1)S(1)}, u32[]{:S(2)}, u32[]{:S(2)}) %collective-permute-start.2) | collective-permute-done | bytes 65568 | tf_op jit(solution)/shard_map/ppermute | solution.py:248
  25.3 0.0 collective-permute-done.3.refs_3_
  25.3 0.0 all-to-all-done.taps_ref
  25.3 2.8 %conv.1._ = bf16[64,2048]{1,0:T(8,128)(2,1)} custom-call(s32[1]{0:T(128)S(6)} %copy.10.len_ref, bf16[32,40,128]{2,1,0:T(8,128)(2,1)S(1)} %all-to-all-done.taps_ref, bf16[256,2048]{1,0:T(8,128)(2,1)S(1)} %source.1.source_ref), custom_call_target="tpu_custom_call" | custom-call | tf_op jit(solution)/shard_map/conv/pallas_call | solution.py:267
  28.2 3.6 %all-to-all-start.1 = ((bf16[8,8,2048]{2,1,0:T(8,128)(2,1)}), bf16[8,8,2048]{2,1,0:T(8,128)(2,1)S(1)}, u32[]{:S(2)}, u32[]{:S(2)}) async-start(bf16[8,8,2048]{2,1,0:T(8,128)(2,1)} %bitcast.4), calls=%async_computation.1 | async-start | bytes 524288 | tf_op jit(solution)/shard_map/all_to_all | solution.py:277
  31.8 0.6 %collective-permute-start.4 = (bf16[4,8,4096]{2,1,0:T(8,128)(2,1)S(1)}, bf16[4,8,4096]{2,1,0:T(8,128)(2,1)S(1)}, u32[]{:S(2)}, u32[]{:S(2)}) collective-permute-start(bf16[4,8,4096]{2,1,0:T(8,128)(2,1)S(1)} %get-tuple-element.27.own_stack_ref), channel_id=1, source_target_pairs={{0,4},{4,0},{8,12},{12,8},{16,20},{20,16},{24,28},{28,24},{1,5},{5... | collective-permute-start | bytes 786440 | tf_op jit(solution)/shard_map/ppermute | solution.py:291
  32.4 0.1 collective-permute-start.5
  32.4 1.1 %collective-permute-done.5.peer_head_ref = bf16[2,40,128]{2,1,0:T(8,128)(2,1)S(1)} collective-permute-done((bf16[2,40,128]{2,1,0:T(8,128)(2,1)S(1)}, bf16[2,40,128]{2,1,0:T(8,128)(2,1)S(1)}, u32[]{:S(2)}, u32[]{:S(2)}) %collective-permute-start.5) | collective-permute-done | bytes 20512 | tf_op jit(solution)/shard_map/ppermute | solution.py:292
  33.6 0.0 collective-permute-done.4.peer_stack_ref
  33.6 0.0 copy-start.3
  33.6 0.7 %copy-done.3 = s32[1,8,1]{1,2,0:T(1,128)S(1)} copy-done((s32[1,8,1]{1,2,0:T(1,128)S(1)}, s32[1,8,1]{1,2,0:T(1,128)}, u32[]{:S(2)}) %copy-start.3) | copy-done | bytes 56
  34.2 0.0 copy-start.2
  34.2 1.3 %span.1 = (f32[8,4096]{1,0:T(8,128)S(1)}, bf16[2,8,4096]{2,1,0:T(8,128)(2,1)}) custom-call(s32[8]{0:T(128)S(1)} %bitcast.12, bf16[4,8,4096]{2,1,0:T(8,128)(2,1)S(1)} %get-tuple-element.27.own_stack_ref, bf16[4,8,4096]{2,1,0:T(8,128)(2,1)S(1)} %collective-permute-done.4.peer_stack_ref, bf16[2,40,128]{2,1,0:T(8,128)(2,1)S(1)} %get-tuple-element.28.own_head_ref, ...), custom_call_target="tpu_custom_call" | custom-call | tf_op jit(solution)/shard_map/span/pallas_call | solution.py:294
  35.5 6.0 %all-to-all-done.1.parts_ref = bf16[8,8,2048]{2,1,0:T(8,128)(2,1)S(1)} async-done(((bf16[8,8,2048]{2,1,0:T(8,128)(2,1)}), bf16[8,8,2048]{2,1,0:T(8,128)(2,1)S(1)}, u32[]{:S(2)}, u32[]{:S(2)}) %all-to-all-start.1) | async-done | bytes 262176 | tf_op jit(solution)/shard_map/all_to_all | solution.py:277
  41.5 0.0 copy-done.2
  41.5 0.7 %finish.1 = bf16[8,4096]{1,0:T(8,128)(2,1)} custom-call(bf16[8,8,2048]{2,1,0:T(8,128)(2,1)S(1)} %all-to-all-done.1.parts_ref, bf16[8,4096]{1,0:T(8,128)(2,1)S(1)} %bitcast.11, f32[8,4096]{1,0:T(8,128)S(1)} %get-tuple-element.30.extra_ref), custom_call_target="tpu_custom_call" | custom-call | tf_op jit(solution)/shard_map/finish/pallas_call | solution.py:310
  (1 shorter events, 0.0 us)
Async XLA Ops:
  2.4 13.8 %collective-permute-start = (bf16[128,4096]{1,0:T(8,128)(2,1)}, bf16[128,4096]{1,0:T(8,128)(2,1)S(1)}, u32[]{:S(2)}, u32[]{:S(2)}) collective-permute-start(bf16[128,4096]{1,0:T(8,128)(2,1)} %bitcast.9), channel_id=1, source_target_pairs={{0,4},{4,0},{8,12},{12,8},{16,20},{20,16},{24,28},{28,24},{1,5},{5... | collective-permute-start | bytes 3145736 | tf_op jit(solution)/shard_map/ppermute | solution.py:244
  2.9 7.0 %copy-start.1 = (bf16[8,4096]{1,0:T(8,128)(2,1)S(1)}, bf16[8,4096]{1,0:T(8,128)(2,1)}, u32[]{:S(2)}) copy-start(bf16[8,4096]{1,0:T(8,128)(2,1)} %get-tuple-element.23.refs_0_.input_ref) | copy-start | bytes 196612
  2.9 22.4 %all-to-all-start = ((bf16[32,40,128]{2,1,0:T(8,128)(2,1)}), bf16[32,40,128]{2,1,0:T(8,128)(2,1)S(1)}, u32[]{:S(2)}, u32[]{:S(2)}) async-start(bf16[32,40,128]{2,1,0:T(8,128)(2,1)} %get-tuple-element.17), calls=%async_computation | async-start | bytes 655360 | tf_op jit(solution)/shard_map/all_to_all | solution.py:242
  9.9 11.8 %collective-permute-start.1 = (bf16[8,4096]{1,0:T(8,128)(2,1)S(1)}, bf16[8,4096]{1,0:T(8,128)(2,1)S(1)}, u32[]{:S(2)}, u32[]{:S(2)}) collective-permute-start(bf16[8,4096]{1,0:T(8,128)(2,1)S(1)} %copy-done.1), channel_id=1, source_target_pairs={{0,8},{4,12},{8,16},{12,20},{16,24},{20,28},{24,0},{28,4},{1,9},{5... | collective-permute-start | bytes 196616 | tf_op jit(solution)/shard_map/ppermute | solution.py:248
  11.7 13.6 %collective-permute-start.2 = (bf16[8,4096]{1,0:T(8,128)(2,1)S(1)}, bf16[8,4096]{1,0:T(8,128)(2,1)S(1)}, u32[]{:S(2)}, u32[]{:S(2)}) collective-permute-start(bf16[8,4096]{1,0:T(8,128)(2,1)S(1)} %copy-done.1), channel_id=1, source_target_pairs={{0,16},{4,20},{8,24},{12,28},{16,0},{20,4},{24,8},{28,12},{1,17},{... | collective-permute-start | bytes 196616 | tf_op jit(solution)/shard_map/ppermute | solution.py:248
  14.1 11.2 %collective-permute-start.3 = (bf16[8,4096]{1,0:T(8,128)(2,1)S(1)}, bf16[8,4096]{1,0:T(8,128)(2,1)S(1)}, u32[]{:S(2)}, u32[]{:S(2)}) collective-permute-start(bf16[8,4096]{1,0:T(8,128)(2,1)S(1)} %copy-done.1), channel_id=1, source_target_pairs={{0,24},{4,28},{8,0},{12,4},{16,8},{20,12},{24,16},{28,20},{1,25},{... | collective-permute-start | bytes 196616 | tf_op jit(solution)/shard_map/ppermute | solution.py:248
  16.2 1.2 %copy-start = (bf16[1,128,4096]{2,1,0:T(8,128)(2,1)S(1)}, bf16[1,128,4096]{2,1,0:T(8,128)(2,1)}, u32[]{:S(2)}) copy-start(bf16[1,128,4096]{2,1,0:T(8,128)(2,1)} %param.8) | copy-start | bytes 3145732
  28.2 13.3 %all-to-all-start.1 = ((bf16[8,8,2048]{2,1,0:T(8,128)(2,1)}), bf16[8,8,2048]{2,1,0:T(8,128)(2,1)S(1)}, u32[]{:S(2)}, u32[]{:S(2)}) async-start(bf16[8,8,2048]{2,1,0:T(8,128)(2,1)} %bitcast.4), calls=%async_computation.1 | async-start | bytes 524288 | tf_op jit(solution)/shard_map/all_to_all | solution.py:277
  31.8 1.8 %collective-permute-start.4 = (bf16[4,8,4096]{2,1,0:T(8,128)(2,1)S(1)}, bf16[4,8,4096]{2,1,0:T(8,128)(2,1)S(1)}, u32[]{:S(2)}, u32[]{:S(2)}) collective-permute-start(bf16[4,8,4096]{2,1,0:T(8,128)(2,1)S(1)} %get-tuple-element.27.own_stack_ref), channel_id=1, source_target_pairs={{0,4},{4,0},{8,12},{12,8},{16,20},{20,16},{24,28},{28,24},{1,5},{5... | collective-permute-start | bytes 786440 | tf_op jit(solution)/shard_map/ppermute | solution.py:291
  32.4 1.2 %collective-permute-start.5 = (bf16[2,40,128]{2,1,0:T(8,128)(2,1)S(1)}, bf16[2,40,128]{2,1,0:T(8,128)(2,1)S(1)}, u32[]{:S(2)}, u32[]{:S(2)}) collective-permute-start(bf16[2,40,128]{2,1,0:T(8,128)(2,1)S(1)} %get-tuple-element.28.own_head_ref), channel_id=1, source_target_pairs={{0,4},{4,0},{8,12},{12,8},{16,20},{20,16},{24,28},{28,24},{1,5},{5... | collective-permute-start | bytes 61448 | tf_op jit(solution)/shard_map/ppermute | solution.py:292
  33.6 0.7 %copy-start.3 = (s32[1,8,1]{1,2,0:T(1,128)S(1)}, s32[1,8,1]{1,2,0:T(1,128)}, u32[]{:S(2)}) copy-start(s32[1,8,1]{1,2,0:T(1,128)} %param.15) | copy-start | bytes 100
  34.2 7.3 %copy-start.2 = (bf16[1,8,4096]{2,1,0:T(8,128)(2,1)S(1)}, bf16[1,8,4096]{2,1,0:T(8,128)(2,1)}, u32[]{:S(2)}) copy-start(bf16[1,8,4096]{2,1,0:T(8,128)(2,1)} %param.9) | copy-start | bytes 196612

commit v4 on v3

--- a/solution.py
+++ b/solution.py
@@ -240,12 +240,7 @@
     )(filter_taps, skip_bias.reshape(1, bias_width), span_key[0], span_value[0])
 
     taps = lax.all_to_all(send, ("blk", "tenant"), split_axis=0, concat_axis=0, tiled=True)
-    history, inputs = lax.optimization_barrier((history, inputs))
     peer_history = lax.ppermute(history, "blk", swap)
-    pages = [inputs]
-    for step in range(1, n_chip):
-        turn = [(i, (i + 2 * step) % n_blk) for i in range(n_blk)]
-        pages.append(lax.ppermute(inputs, "blk", turn))
 
     def half_block(count):
         return pl.BlockSpec((count, half), lambda i, n: (0, lax.rem(lax.axis_index("blk"), 2)))
@@ -263,7 +258,11 @@
         name="source",
     )(lengths, history, peer_history)
 
-    taps, source, *pages = lax.optimization_barrier((taps, source, *pages))
+    source, inputs = lax.optimization_barrier((source, inputs))
+    pages = [inputs]
+    for step in range(1, n_chip):
+        turn = [(i, (i + 2 * step) % n_blk) for i in range(n_blk)]
+        pages.append(lax.ppermute(inputs, "blk", turn))
     partial = pl.pallas_call(
         functools.partial(conv_kernel, fr, span, gsize),
         out_shape=jax.ShapeDtypeStruct((span, half), bf16),
@@ -274,6 +273,7 @@
         name="conv",
     )(lengths, taps, source)
 
+    partial, *pages = lax.optimization_barrier((partial, *pages))
     parts = lax.all_to_all(
         partial.reshape(n_blk, span_rows, half), "blk", split_axis=0, concat_axis=0, tiled=True
     )

time: 42.6 us -> 42.2 us (level)
  waiting for transfers between devices: 14.8 us -> 14 us
  local copies, waits for them, and re-layouts: 1.88 us -> 2.53 us
    ppermute x3, waiting for transfers between devices: 7.74 us -> 0.01 us  [per_device(): pages.append(lax.ppermute(inputs, 'blk', turn))]
    all_to_all x1, waiting for transfers between devices: 0.01 us -> 6.91 us  [per_device(): lax.all_to_all(send, ('blk', 'tenant'), split_axis=0, concat_axis=0, tile...]
    unnamed x8, local copies, waits for them, and re-layouts: 1.88 us -> 2.53 us
  transfers between devices with their start and end apart: 8 -> 8, of which waited for: 4 -> 3; matrix products, arithmetic and copies ran while one was open for 0% -> 0% of each run, Pallas kernels for 4% -> 15%
where the time goes in v4:
time: 42.2 us; the launch traced here: 41.7 us
  starting transfers between devices  17.1 us (41%)
  waiting for transfers between devices  14 us (33%)
  Pallas kernels  6.77 us (16%)
  local copies, waits for them, and re-layouts  2.53 us (6%)
  between operations  1.34 us (3%)
    all_to_all x1, starting transfers between devices, per_device(): lax.all_to_all(send, ('blk', 'tenant'), split_axis=0, concat_axis=0, tile...  6.97 us
    all_to_all x1, waiting for transfers between devices, per_device(): lax.all_to_all(send, ('blk', 'tenant'), split_axis=0, concat_axis=0, tile...  6.91 us
    all_to_all x1, waiting for transfers between devices, per_device(): lax.all_to_all(partial.reshape(n_blk, span_rows, half), 'blk', split_axis...  5.99 us
    ppermute x3, starting transfers between devices, per_device(): pages.append(lax.ppermute(inputs, 'blk', turn))  5.6 us
    all_to_all x1, starting transfers between devices, per_device(): lax.all_to_all(partial.reshape(n_blk, span_rows, half), 'blk', split_axis...  3.42 us
    pallas_call x1, Pallas kernels, per_device(): pl.pallas_call(functools.partial(conv_kernel, fr, span, gsize), out_shape...  2.84 us
    unnamed x8, local copies, waits for them, and re-layouts  2.53 us
    pallas_call x1, Pallas kernels, per_device(): pl.pallas_call(functools.partial(pack_kernel, n_ten), out_shape=(jax.Shap...  1.72 us
  transfers between devices with their start and end apart: 8, of which 3 were waited for; matrix products, arithmetic and copies ran while one was open for 0% of the time, Pallas kernels for 15%

profile of v4, /device:TPU:0, one launch (start us, length us, event | category | flops | bytes accessed | tf_op | source)
XLA Modules:
  0.0 41.7 jit_solution(12092924131578414841)
XLA Ops:
  0.6 0.5 %collective-permute-start = (bf16[128,4096]{1,0:T(8,128)(2,1)}, bf16[128,4096]{1,0:T(8,128)(2,1)S(1)}, u32[]{:S(2)}, u32[]{:S(2)}) collective-permute-start(bf16[128,4096]{1,0:T(8,128)(2,1)} %bitcast.9), channel_id=1, source_target_pairs={{0,4},{4,0},{8,12},{12,8},{16,20},{20,16},{24,28},{28,24},{1,5},{5... | collective-permute-start | bytes 3145736 | tf_op jit(solution)/shard_map/ppermute | solution.py:243
  1.1 1.7 %pack.1 = (bf16[32,40,128]{2,1,0:T(8,128)(2,1)}, bf16[8,4096]{1,0:T(8,128)(2,1)}) custom-call(bf16[34,256]{1,0:T(8,128)(2,1)} %taps_hbm.1, bf16[1,128]{1,0:T(2,128)(2,1)} %bitcast.16, bf16[8,4096]{1,0:T(8,128)(2,1)} %bitcast.13, bf16[8,4096]{1,0:T(8,128)(2,1)} %bitcast.14), custom_call_target="tpu_custom_call" | custom-call | tf_op jit(solution)/shard_map/pack/pallas_call | solution.py:223
  2.9 7.0 %all-to-all-start = ((bf16[32,40,128]{2,1,0:T(8,128)(2,1)}), bf16[32,40,128]{2,1,0:T(8,128)(2,1)S(1)}, u32[]{:S(2)}, u32[]{:S(2)}) async-start(bf16[32,40,128]{2,1,0:T(8,128)(2,1)} %get-tuple-element.16), calls=%async_computation | async-start | bytes 655360 | tf_op jit(solution)/shard_map/all_to_all | solution.py:242
  10.5 0.0 collective-permute-done.peer_ref
  10.5 0.0 copy-start
  10.5 1.2 %copy-done = bf16[1,128,4096]{2,1,0:T(8,128)(2,1)S(1)} copy-done((bf16[1,128,4096]{2,1,0:T(8,128)(2,1)S(1)}, bf16[1,128,4096]{2,1,0:T(8,128)(2,1)}, u32[]{:S(2)}) %copy-start) | copy-done | bytes 1048600
  11.7 0.0 copy-start.1
  11.7 0.2 source.1.source_ref
  11.9 0.7 %copy-done.1 = bf16[8,4096]{1,0:T(8,128)(2,1)S(1)} copy-done((bf16[8,4096]{1,0:T(8,128)(2,1)S(1)}, bf16[8,4096]{1,0:T(8,128)(2,1)}, u32[]{:S(2)}) %copy-start.1) | copy-done | bytes 65560
  12.6 1.8 %collective-permute-start.1 = (bf16[8,4096]{1,0:T(8,128)(2,1)S(1)}, bf16[8,4096]{1,0:T(8,128)(2,1)S(1)}, u32[]{:S(2)}, u32[]{:S(2)}) collective-permute-start(bf16[8,4096]{1,0:T(8,128)(2,1)S(1)} %copy-done.1), channel_id=1, source_target_pairs={{0,8},{4,12},{8,16},{12,20},{16,24},{20,28},{24,0},{28,4},{1,9},{5... | collective-permute-start | bytes 196616 | tf_op jit(solution)/shard_map/ppermute | solution.py:265
  14.3 2.4 %collective-permute-start.2 = (bf16[8,4096]{1,0:T(8,128)(2,1)S(1)}, bf16[8,4096]{1,0:T(8,128)(2,1)S(1)}, u32[]{:S(2)}, u32[]{:S(2)}) collective-permute-start(bf16[8,4096]{1,0:T(8,128)(2,1)S(1)} %copy-done.1), channel_id=1, source_target_pairs={{0,16},{4,20},{8,24},{12,28},{16,0},{20,4},{24,8},{28,12},{1,17},{... | collective-permute-start | bytes 196616 | tf_op jit(solution)/shard_map/ppermute | solution.py:265
  16.8 1.4 %collective-permute-start.3 = (bf16[8,4096]{1,0:T(8,128)(2,1)S(1)}, bf16[8,4096]{1,0:T(8,128)(2,1)S(1)}, u32[]{:S(2)}, u32[]{:S(2)}) collective-permute-start(bf16[8,4096]{1,0:T(8,128)(2,1)S(1)} %copy-done.1), channel_id=1, source_target_pairs={{0,24},{4,28},{8,0},{12,4},{16,8},{20,12},{24,16},{28,20},{1,25},{... | collective-permute-start | bytes 196616 | tf_op jit(solution)/shard_map/ppermute | solution.py:265
  18.2 6.9 %all-to-all-done.taps_ref = bf16[32,40,128]{2,1,0:T(8,128)(2,1)S(1)} async-done(((bf16[32,40,128]{2,1,0:T(8,128)(2,1)}), bf16[32,40,128]{2,1,0:T(8,128)(2,1)S(1)}, u32[]{:S(2)}, u32[]{:S(2)}) %all-to-all-start) | async-done | bytes 327712 | tf_op jit(solution)/shard_map/all_to_all | solution.py:242
  25.1 2.8 %conv.1._ = bf16[64,2048]{1,0:T(8,128)(2,1)} custom-call(s32[1]{0:T(128)S(6)} %copy.10.len_ref, bf16[32,40,128]{2,1,0:T(8,128)(2,1)S(1)} %all-to-all-done.taps_ref, bf16[256,2048]{1,0:T(8,128)(2,1)S(1)} %source.1.source_ref), custom_call_target="tpu_custom_call" | custom-call | tf_op jit(solution)/shard_map/conv/pallas_call | solution.py:266
  27.9 0.0 collective-permute-done.1.refs_1_
  27.9 0.0 collective-permute-done.2.refs_2_
  27.9 0.0 collective-permute-done.3.refs_3_
  27.9 3.4 %all-to-all-start.1 = ((bf16[8,8,2048]{2,1,0:T(8,128)(2,1)}), bf16[8,8,2048]{2,1,0:T(8,128)(2,1)S(1)}, u32[]{:S(2)}, u32[]{:S(2)}) async-start(bf16[8,8,2048]{2,1,0:T(8,128)(2,1)} %bitcast.4), calls=%async_computation.1 | async-start | bytes 524288 | tf_op jit(solution)/shard_map/all_to_all | solution.py:277
  31.4 0.5 %collective-permute-start.4 = (bf16[4,8,4096]{2,1,0:T(8,128)(2,1)S(1)}, bf16[4,8,4096]{2,1,0:T(8,128)(2,1)S(1)}, u32[]{:S(2)}, u32[]{:S(2)}) collective-permute-start(bf16[4,8,4096]{2,1,0:T(8,128)(2,1)S(1)} %get-tuple-element.25.own_stack_ref), channel_id=1, source_target_pairs={{0,4},{4,0},{8,12},{12,8},{16,20},{20,16},{24,28},{28,24},{1,5},{5... | collective-permute-start | bytes 786440 | tf_op jit(solution)/shard_map/ppermute | solution.py:291
  31.9 0.1 collective-permute-start.5
  32.0 1.1 %collective-permute-done.5.peer_head_ref = bf16[2,40,128]{2,1,0:T(8,128)(2,1)S(1)} collective-permute-done((bf16[2,40,128]{2,1,0:T(8,128)(2,1)S(1)}, bf16[2,40,128]{2,1,0:T(8,128)(2,1)S(1)}, u32[]{:S(2)}, u32[]{:S(2)}) %collective-permute-start.5) | collective-permute-done | bytes 20512 | tf_op jit(solution)/shard_map/ppermute | solution.py:292
  33.1 0.0 collective-permute-done.4.peer_stack_ref
  33.1 0.0 copy-start.3
  33.1 0.7 %copy-done.3 = s32[1,8,1]{1,2,0:T(1,128)S(1)} copy-done((s32[1,8,1]{1,2,0:T(1,128)S(1)}, s32[1,8,1]{1,2,0:T(1,128)}, u32[]{:S(2)}) %copy-start.3) | copy-done | bytes 56
  33.7 0.0 copy-start.2
  33.7 1.3 %span.1 = (f32[8,4096]{1,0:T(8,128)S(1)}, bf16[2,8,4096]{2,1,0:T(8,128)(2,1)}) custom-call(s32[8]{0:T(128)S(1)} %bitcast.12, bf16[4,8,4096]{2,1,0:T(8,128)(2,1)S(1)} %get-tuple-element.25.own_stack_ref, bf16[4,8,4096]{2,1,0:T(8,128)(2,1)S(1)} %collective-permute-done.4.peer_stack_ref, bf16[2,40,128]{2,1,0:T(8,128)(2,1)S(1)} %get-tuple-element.26.own_head_ref, ...), custom_call_target="tpu_custom_call" | custom-call | tf_op jit(solution)/shard_map/span/pallas_call | solution.py:294
  35.0 6.0 %all-to-all-done.1.parts_ref = bf16[8,8,2048]{2,1,0:T(8,128)(2,1)S(1)} async-done(((bf16[8,8,2048]{2,1,0:T(8,128)(2,1)}), bf16[8,8,2048]{2,1,0:T(8,128)(2,1)S(1)}, u32[]{:S(2)}, u32[]{:S(2)}) %all-to-all-start.1) | async-done | bytes 262176 | tf_op jit(solution)/shard_map/all_to_all | solution.py:277
  41.0 0.0 copy-done.2
  41.0 0.7 %finish.1 = bf16[8,4096]{1,0:T(8,128)(2,1)} custom-call(bf16[8,8,2048]{2,1,0:T(8,128)(2,1)S(1)} %all-to-all-done.1.parts_ref, bf16[8,4096]{1,0:T(8,128)(2,1)S(1)} %bitcast.11, f32[8,4096]{1,0:T(8,128)S(1)} %get-tuple-element.28.extra_ref), custom_call_target="tpu_custom_call" | custom-call | tf_op jit(solution)/shard_map/finish/pallas_call | solution.py:310
  (1 shorter events, 0.0 us)
Async XLA Ops:
  0.6 9.9 %collective-permute-start = (bf16[128,4096]{1,0:T(8,128)(2,1)}, bf16[128,4096]{1,0:T(8,128)(2,1)S(1)}, u32[]{:S(2)}, u32[]{:S(2)}) collective-permute-start(bf16[128,4096]{1,0:T(8,128)(2,1)} %bitcast.9), channel_id=1, source_target_pairs={{0,4},{4,0},{8,12},{12,8},{16,20},{20,16},{24,28},{28,24},{1,5},{5... | collective-permute-start | bytes 3145736 | tf_op jit(solution)/shard_map/ppermute | solution.py:243
  2.9 22.2 %all-to-all-start = ((bf16[32,40,128]{2,1,0:T(8,128)(2,1)}), bf16[32,40,128]{2,1,0:T(8,128)(2,1)S(1)}, u32[]{:S(2)}, u32[]{:S(2)}) async-start(bf16[32,40,128]{2,1,0:T(8,128)(2,1)} %get-tuple-element.16), calls=%async_computation | async-start | bytes 655360 | tf_op jit(solution)/shard_map/all_to_all | solution.py:242
  10.5 1.2 %copy-start = (bf16[1,128,4096]{2,1,0:T(8,128)(2,1)S(1)}, bf16[1,128,4096]{2,1,0:T(8,128)(2,1)}, u32[]{:S(2)}) copy-start(bf16[1,128,4096]{2,1,0:T(8,128)(2,1)} %param.8) | copy-start | bytes 3145732
  11.7 0.8 %copy-start.1 = (bf16[8,4096]{1,0:T(8,128)(2,1)S(1)}, bf16[8,4096]{1,0:T(8,128)(2,1)}, u32[]{:S(2)}) copy-start(bf16[8,4096]{1,0:T(8,128)(2,1)} %get-tuple-element.21.refs_0_.input_ref) | copy-start | bytes 196612
  12.6 15.4 %collective-permute-start.1 = (bf16[8,4096]{1,0:T(8,128)(2,1)S(1)}, bf16[8,4096]{1,0:T(8,128)(2,1)S(1)}, u32[]{:S(2)}, u32[]{:S(2)}) collective-permute-start(bf16[8,4096]{1,0:T(8,128)(2,1)S(1)} %copy-done.1), channel_id=1, source_target_pairs={{0,8},{4,12},{8,16},{12,20},{16,24},{20,28},{24,0},{28,4},{1,9},{5... | collective-permute-start | bytes 196616 | tf_op jit(solution)/shard_map/ppermute | solution.py:265
  14.3 13.6 %collective-permute-start.2 = (bf16[8,4096]{1,0:T(8,128)(2,1)S(1)}, bf16[8,4096]{1,0:T(8,128)(2,1)S(1)}, u32[]{:S(2)}, u32[]{:S(2)}) collective-permute-start(bf16[8,4096]{1,0:T(8,128)(2,1)S(1)} %copy-done.1), channel_id=1, source_target_pairs={{0,16},{4,20},{8,24},{12,28},{16,0},{20,4},{24,8},{28,12},{1,17},{... | collective-permute-start | bytes 196616 | tf_op jit(solution)/shard_map/ppermute | solution.py:265
  16.8 11.2 %collective-permute-start.3 = (bf16[8,4096]{1,0:T(8,128)(2,1)S(1)}, bf16[8,4096]{1,0:T(8,128)(2,1)S(1)}, u32[]{:S(2)}, u32[]{:S(2)}) collective-permute-start(bf16[8,4096]{1,0:T(8,128)(2,1)S(1)} %copy-done.1), channel_id=1, source_target_pairs={{0,24},{4,28},{8,0},{12,4},{16,8},{20,12},{24,16},{28,20},{1,25},{... | collective-permute-start | bytes 196616 | tf_op jit(solution)/shard_map/ppermute | solution.py:265
  27.9 13.1 %all-to-all-start.1 = ((bf16[8,8,2048]{2,1,0:T(8,128)(2,1)}), bf16[8,8,2048]{2,1,0:T(8,128)(2,1)S(1)}, u32[]{:S(2)}, u32[]{:S(2)}) async-start(bf16[8,8,2048]{2,1,0:T(8,128)(2,1)} %bitcast.4), calls=%async_computation.1 | async-start | bytes 524288 | tf_op jit(solution)/shard_map/all_to_all | solution.py:277
  31.4 1.7 %collective-permute-start.4 = (bf16[4,8,4096]{2,1,0:T(8,128)(2,1)S(1)}, bf16[4,8,4096]{2,1,0:T(8,128)(2,1)S(1)}, u32[]{:S(2)}, u32[]{:S(2)}) collective-permute-start(bf16[4,8,4096]{2,1,0:T(8,128)(2,1)S(1)} %get-tuple-element.25.own_stack_ref), channel_id=1, source_target_pairs={{0,4},{4,0},{8,12},{12,8},{16,20},{20,16},{24,28},{28,24},{1,5},{5... | collective-permute-start | bytes 786440 | tf_op jit(solution)/shard_map/ppermute | solution.py:291
  31.9 1.2 %collective-permute-start.5 = (bf16[2,40,128]{2,1,0:T(8,128)(2,1)S(1)}, bf16[2,40,128]{2,1,0:T(8,128)(2,1)S(1)}, u32[]{:S(2)}, u32[]{:S(2)}) collective-permute-start(bf16[2,40,128]{2,1,0:T(8,128)(2,1)S(1)} %get-tuple-element.26.own_head_ref), channel_id=1, source_target_pairs={{0,4},{4,0},{8,12},{12,8},{16,20},{20,16},{24,28},{28,24},{1,5},{5... | collective-permute-start | bytes 61448 | tf_op jit(solution)/shard_map/ppermute | solution.py:292
  33.1 0.7 %copy-start.3 = (s32[1,8,1]{1,2,0:T(1,128)S(1)}, s32[1,8,1]{1,2,0:T(1,128)}, u32[]{:S(2)}) copy-start(s32[1,8,1]{1,2,0:T(1,128)} %param.15) | copy-start | bytes 100
  33.7 7.3 %copy-start.2 = (bf16[1,8,4096]{2,1,0:T(8,128)(2,1)S(1)}, bf16[1,8,4096]{2,1,0:T(8,128)(2,1)}, u32[]{:S(2)}) copy-start(bf16[1,8,4096]{2,1,0:T(8,128)(2,1)} %param.9) | copy-start | bytes 196612

commit v5 on v2

--- a/solution.py
+++ b/solution.py
@@ -19,21 +19,38 @@
     return -(-value // step) * step
 
 
-def pack_kernel(n_ten, taps_ref, bias_ref, key_ref, value_ref, send_ref, input_ref):
-    n_dev, padded, lanes = send_ref.shape
+def pack_kernel(n_ten, taps_hbm, bias_hbm, send_hbm, token_ref, taps_ref, bias_ref, block_ref, sems):
+    n_dev, padded, lanes = send_hbm.shape
     rows = taps_ref.shape[0]
+    fetch = [
+        pltpu.make_async_copy(taps_hbm, taps_ref, sems.at[0]),
+        pltpu.make_async_copy(bias_hbm, bias_ref, sems.at[1]),
+    ]
+    for copy in fetch:
+        copy.start()
+    for copy in fetch:
+        copy.wait()
     bias = bias_ref[...].astype(f32)
     if bias.shape[1] < lanes:
         bias = jnp.concatenate([bias, jnp.zeros((1, lanes - bias.shape[1]), f32)], axis=1)
-    blocks = []
     for half in range(2):
         taps = taps_ref[:, half * lanes : (half + 1) * lanes].astype(f32)
         parts = [taps, bias]
         if padded > rows + 1:
             parts.append(jnp.zeros((padded - rows - 1, lanes), f32))
-        blocks.append(jnp.concatenate(parts, axis=0).astype(bf16))
-    for dest in range(n_dev):
-        send_ref[dest] = blocks[(dest // n_ten) % 2]
+        block_ref[half] = jnp.concatenate(parts, axis=0).astype(bf16)
+    copies = [
+        pltpu.make_async_copy(block_ref.at[(i // n_ten) % 2], send_hbm.at[i], sems.at[2 + i])
+        for i in range(n_dev)
+    ]
+    for copy in copies:
+        copy.start()
+    token_ref[...] = jnp.zeros_like(token_ref)
+    for copy in copies:
+        copy.wait()
+
+
+def input_kernel(_, key_ref, value_ref, input_ref):
     input_ref[...] = (key_ref[...].astype(f32) * value_ref[...].astype(f32)).astype(bf16)
 
 
@@ -110,9 +127,8 @@
 def gather_kernel(fr, bias_width, _, taps_ref, *refs):
     pages, (stack_ref, head_ref, bias_ref) = refs[:-3], refs[-3:]
     chip = lax.div(lax.axis_index("blk"), 2)
-    n_chip = len(pages)
     for step, page in enumerate(pages):
-        stack_ref[lax.rem(chip + n_chip - step, n_chip)] = page[...]
+        stack_ref[lax.bitwise_xor(chip, step)] = page[...]
     head_ref[...] = taps_ref[: head_ref.shape[0]]
     each = LANES // bias_width
     for index in range(taps_ref.shape[0] // each):
@@ -208,25 +224,34 @@
     bias_width = skip_bias.shape[0]
     swap = [(i, i ^ 1) for i in range(n_blk)]
 
-    send, inputs = pl.pallas_call(
+    send, token = pl.pallas_call(
         functools.partial(pack_kernel, n_ten),
         out_shape=(
             jax.ShapeDtypeStruct((n_dev, padded, groups // 2), bf16),
-            jax.ShapeDtypeStruct((span_rows, width), bf16),
+            jax.ShapeDtypeStruct((8, LANES), f32),
         ),
-        in_specs=[whole()] * 4,
-        out_specs=(whole(), whole()),
-        compiler_params=limit(8),
+        in_specs=[whole(pltpu.HBM)] * 2,
+        out_specs=(whole(pltpu.HBM), whole()),
+        scratch_shapes=[
+            pltpu.VMEM((fr, groups), bf16),
+            pltpu.VMEM((1, bias_width), bf16),
+            pltpu.VMEM((2, padded, groups // 2), bf16),
+            pltpu.SemaphoreType.DMA((2 + n_dev,)),
+        ],
+        compiler_params=limit(58),
         name="pack",
-    )(filter_taps, skip_bias.reshape(1, bias_width), span_key[0], span_value[0])
-
+    )(filter_taps, skip_bias.reshape(1, bias_width))
     taps = lax.all_to_all(send, ("blk", "tenant"), split_axis=0, concat_axis=0, tiled=True)
-    history, inputs = lax.optimization_barrier((history, inputs))
+
+    inputs = pl.pallas_call(
+        input_kernel,
+        out_shape=jax.ShapeDtypeStruct((span_rows, width), bf16),
+        in_specs=[whole(pl.ANY)] + [whole()] * 2,
+        out_specs=whole(),
+        compiler_params=limit(8),
+        name="inputs",
+    )(token, span_key[0], span_value[0])
     peer_history = lax.ppermute(history, "blk", swap)
-    pages = [inputs]
-    for step in range(1, n_chip):
-        turn = [(i, (i + 2 * step) % n_blk) for i in range(n_blk)]
-        pages.append(lax.ppermute(inputs, "blk", turn))
 
     def half_block(count):
         return pl.BlockSpec((count, half), lambda i, n: (0, lax.rem(lax.axis_index("blk"), 2)))
@@ -244,6 +269,15 @@
         name="source",
     )(lengths, history, peer_history)
 
+    source, inputs = lax.optimization_barrier((source, inputs))
+    pages = {0: inputs}
+    far = n_chip // 2
+    while far:
+        across = [(i, i ^ (2 * far)) for i in range(n_blk)]
+        pages.update({at ^ far: lax.ppermute(page, "blk", across) for at, page in pages.items()})
+        far //= 2
+    pages = [pages[at] for at in range(n_chip)]
+
     partial = pl.pallas_call(
         functools.partial(conv_kernel, fr, span, gsize),
         out_shape=jax.ShapeDtypeStruct((span, half), bf16),
@@ -254,6 +288,7 @@
         name="conv",
     )(lengths, taps, source)
 
+    partial, *pages = lax.optimization_barrier((partial, *pages))
     parts = lax.all_to_all(
         partial.reshape(n_blk, span_rows, half), "blk", split_axis=0, concat_axis=0, tiled=True
     )

time: 49.6 us -> 42.6 us (0.86)
  waiting for transfers between devices: 19.9 us -> 15.7 us
  local copies, waits for them, and re-layouts: 4.93 us -> 1.9 us
  Pallas kernels: 5.81 us -> 7.45 us
  starting transfers between devices: 17.2 us -> 15.7 us
    all_to_all x1, waiting for transfers between devices: 10.2 us -> 0.23 us  [per_device(): lax.all_to_all(send, ('blk', 'tenant'), split_axis=0, concat_axis=0, tile...]
    all_to_all x1, waiting for transfers between devices: 0.01 us -> 5.99 us  [per_device(): lax.all_to_all(partial.reshape(n_blk, span_rows, half), 'blk', split_axis...]
    unnamed x14 -> x12, local copies, waits for them, and re-layouts: 4.93 us -> 1.9 us
    pallas_call x1, Pallas kernels: 0.77 us -> 2.37 us  [per_device(): pl.pallas_call(functools.partial(pack_kernel, n_ten), out_shape=(jax.Shap...]
    ppermute x3, starting transfers between devices: 5.76 us -> 4.25 us  [per_device(): lax.ppermute(page, 'blk', across)]
  transfers between devices with their start and end apart: 8 -> 8, of which waited for: 4 -> 5; matrix products, arithmetic and copies ran while one was open for 0% -> 0% of each run, Pallas kernels for 3% -> 16%
where the time goes in v5:
time: 42.6 us; the launch traced here: 42.1 us
  starting transfers between devices  15.7 us (37%)
  waiting for transfers between devices  15.7 us (37%)
  Pallas kernels  7.45 us (17%)
  local copies, waits for them, and re-layouts  1.9 us (4%)
  between operations  1.4 us (3%)
    ppermute x3, waiting for transfers between devices, per_device(): lax.ppermute(page, 'blk', across)  8.37 us
    all_to_all x1, starting transfers between devices, per_device(): lax.all_to_all(send, ('blk', 'tenant'), split_axis=0, concat_axis=0, tile...  6.97 us
    all_to_all x1, waiting for transfers between devices, per_device(): lax.all_to_all(partial.reshape(n_blk, span_rows, half), 'blk', split_axis...  5.99 us
    ppermute x3, starting transfers between devices, per_device(): lax.ppermute(page, 'blk', across)  4.25 us
    all_to_all x1, starting transfers between devices, per_device(): lax.all_to_all(partial.reshape(n_blk, span_rows, half), 'blk', split_axis...  3.41 us
    pallas_call x1, Pallas kernels, per_device(): pl.pallas_call(functools.partial(conv_kernel, fr, span, gsize), out_shape...  2.85 us
    pallas_call x1, Pallas kernels, per_device(): pl.pallas_call(functools.partial(pack_kernel, n_ten), out_shape=(jax.Shap...  2.37 us
    unnamed x12, local copies, waits for them, and re-layouts  1.9 us
  transfers between devices with their start and end apart: 8, of which 5 were waited for; matrix products, arithmetic and copies ran while one was open for 0% of the time, Pallas kernels for 16%

profile of v5, /device:TPU:0, one launch (start us, length us, event | category | flops | bytes accessed | tf_op | source)
XLA Modules:
  0.0 42.1 jit_solution(17982625377317233419)
XLA Ops:
  0.6 0.5 %collective-permute-start = (bf16[128,4096]{1,0:T(8,128)(2,1)}, bf16[128,4096]{1,0:T(8,128)(2,1)S(1)}, u32[]{:S(2)}, u32[]{:S(2)}) collective-permute-start(bf16[128,4096]{1,0:T(8,128)(2,1)} %bitcast.9), channel_id=1, source_target_pairs={{0,4},{4,0},{8,12},{12,8},{16,20},{20,16},{24,28},{28,24},{1,5},{5... | collective-permute-start | bytes 3145736 | tf_op jit(solution)/shard_map/ppermute | solution.py:254
  1.1 2.4 %pack.1 = (bf16[32,40,128]{2,1,0:T(8,128)(2,1)}, f32[8,128]{1,0:T(8,128)}) custom-call(bf16[34,256]{1,0:T(8,128)(2,1)} %taps_hbm.1, bf16[1,128]{1,0:T(2,128)(2,1)} %bitcast.16), custom_call_target="tpu_custom_call" | custom-call | tf_op jit(solution)/shard_map/pack/pallas_call | solution.py:227
  3.5 0.0 copy-start.1
  3.5 0.0 copy-start.2
  3.5 7.0 %all-to-all-start = ((bf16[32,40,128]{2,1,0:T(8,128)(2,1)}), bf16[32,40,128]{2,1,0:T(8,128)(2,1)S(1)}, u32[]{:S(2)}, u32[]{:S(2)}) async-start(bf16[32,40,128]{2,1,0:T(8,128)(2,1)} %get-tuple-element.16), calls=%async_computation | async-start | bytes 655360 | tf_op jit(solution)/shard_map/all_to_all | solution.py:244
  10.5 0.0 copy-start.4
  11.2 0.0 copy-done.1
  11.2 0.0 copy-done.2
  11.2 0.0 copy-done.4
  11.3 0.0 collective-permute-done.peer_ref
  11.3 0.0 copy-start
  11.3 1.2 %copy-done = bf16[1,128,4096]{2,1,0:T(8,128)(2,1)S(1)} copy-done((bf16[1,128,4096]{2,1,0:T(8,128)(2,1)S(1)}, bf16[1,128,4096]{2,1,0:T(8,128)(2,1)}, u32[]{:S(2)}) %copy-start) | copy-done | bytes 1048600
  12.5 0.2 source.1.source_ref
  12.7 2.7 %collective-permute-start.2 = (bf16[8,4096]{1,0:T(8,128)(2,1)S(1)}, bf16[8,4096]{1,0:T(8,128)(2,1)S(1)}, u32[]{:S(2)}, u32[]{:S(2)}) collective-permute-start(bf16[8,4096]{1,0:T(8,128)(2,1)S(1)} %inputs.1.refs_0_.input_ref), channel_id=1, source_target_pairs={{0,16},{4,20},{8,24},{12,28},{16,0},{20,4},{24,8},{28,12},{1,17},{... | collective-permute-start | bytes 196616 | tf_op jit(solution)/shard_map/ppermute | solution.py:277
  15.4 1.5 %collective-permute-start.1 = (bf16[8,4096]{1,0:T(8,128)(2,1)S(1)}, bf16[8,4096]{1,0:T(8,128)(2,1)S(1)}, u32[]{:S(2)}, u32[]{:S(2)}) collective-permute-start(bf16[8,4096]{1,0:T(8,128)(2,1)S(1)} %inputs.1.refs_0_.input_ref), channel_id=1, source_target_pairs={{0,8},{4,12},{8,0},{12,4},{16,24},{20,28},{24,16},{28,20},{1,9},{5... | collective-permute-start | bytes 196616 | tf_op jit(solution)/shard_map/ppermute | solution.py:277
  16.9 7.2 %collective-permute-done.2.refs_2_ = bf16[8,4096]{1,0:T(8,128)(2,1)S(1)} collective-permute-done((bf16[8,4096]{1,0:T(8,128)(2,1)S(1)}, bf16[8,4096]{1,0:T(8,128)(2,1)S(1)}, u32[]{:S(2)}, u32[]{:S(2)}) %collective-permute-start.2) | collective-permute-done | bytes 65568 | tf_op jit(solution)/shard_map/ppermute | solution.py:277
  24.1 0.0 collective-permute-start.3
  24.1 0.2 all-to-all-done.taps_ref
  24.4 2.9 %conv.1._ = bf16[64,2048]{1,0:T(8,128)(2,1)} custom-call(s32[1]{0:T(128)S(6)} %copy.10.len_ref, bf16[32,40,128]{2,1,0:T(8,128)(2,1)S(1)} %all-to-all-done.taps_ref, bf16[256,2048]{1,0:T(8,128)(2,1)S(1)} %source.1.source_ref), custom_call_target="tpu_custom_call" | custom-call | tf_op jit(solution)/shard_map/conv/pallas_call | solution.py:281
  27.2 0.0 collective-permute-done.1.refs_1_
  27.2 1.2 %collective-permute-done.3.refs_3_ = bf16[8,4096]{1,0:T(8,128)(2,1)S(1)} collective-permute-done((bf16[8,4096]{1,0:T(8,128)(2,1)S(1)}, bf16[8,4096]{1,0:T(8,128)(2,1)S(1)}, u32[]{:S(2)}, u32[]{:S(2)}) %collective-permute-start.3) | collective-permute-done | bytes 65568 | tf_op jit(solution)/shard_map/ppermute | solution.py:277
  28.4 3.4 %all-to-all-start.1 = ((bf16[8,8,2048]{2,1,0:T(8,128)(2,1)}), bf16[8,8,2048]{2,1,0:T(8,128)(2,1)S(1)}, u32[]{:S(2)}, u32[]{:S(2)}) async-start(bf16[8,8,2048]{2,1,0:T(8,128)(2,1)} %bitcast.4), calls=%async_computation.1 | async-start | bytes 524288 | tf_op jit(solution)/shard_map/all_to_all | solution.py:292
  31.9 0.5 %collective-permute-start.4 = (bf16[4,8,4096]{2,1,0:T(8,128)(2,1)S(1)}, bf16[4,8,4096]{2,1,0:T(8,128)(2,1)S(1)}, u32[]{:S(2)}, u32[]{:S(2)}) collective-permute-start(bf16[4,8,4096]{2,1,0:T(8,128)(2,1)S(1)} %get-tuple-element.25.own_stack_ref), channel_id=1, source_target_pairs={{0,4},{4,0},{8,12},{12,8},{16,20},{20,16},{24,28},{28,24},{1,5},{5... | collective-permute-start | bytes 786440 | tf_op jit(solution)/shard_map/ppermute | solution.py:306
  32.3 0.1 collective-permute-start.5
  32.4 1.1 %collective-permute-done.5.peer_head_ref = bf16[2,40,128]{2,1,0:T(8,128)(2,1)S(1)} collective-permute-done((bf16[2,40,128]{2,1,0:T(8,128)(2,1)S(1)}, bf16[2,40,128]{2,1,0:T(8,128)(2,1)S(1)}, u32[]{:S(2)}, u32[]{:S(2)}) %collective-permute-start.5) | collective-permute-done | bytes 20512 | tf_op jit(solution)/shard_map/ppermute | solution.py:307
  33.5 0.0 collective-permute-done.4.peer_stack_ref
  33.5 0.0 copy-start.5
  33.5 0.7 %copy-done.5 = s32[1,8,1]{1,2,0:T(1,128)S(1)} copy-done((s32[1,8,1]{1,2,0:T(1,128)S(1)}, s32[1,8,1]{1,2,0:T(1,128)}, u32[]{:S(2)}) %copy-start.5) | copy-done | bytes 56
  34.2 1.3 %span.1 = (f32[8,4096]{1,0:T(8,128)S(1)}, bf16[2,8,4096]{2,1,0:T(8,128)(2,1)}) custom-call(s32[8]{0:T(128)S(1)} %bitcast.14, bf16[4,8,4096]{2,1,0:T(8,128)(2,1)S(1)} %get-tuple-element.25.own_stack_ref, bf16[4,8,4096]{2,1,0:T(8,128)(2,1)S(1)} %collective-permute-done.4.peer_stack_ref, bf16[2,40,128]{2,1,0:T(8,128)(2,1)S(1)} %get-tuple-element.26.own_head_ref, ...), custom_call_target="tpu_custom_call" | custom-call | tf_op jit(solution)/shard_map/span/pallas_call | solution.py:309
  35.5 6.0 %all-to-all-done.1.parts_ref = bf16[8,8,2048]{2,1,0:T(8,128)(2,1)S(1)} async-done(((bf16[8,8,2048]{2,1,0:T(8,128)(2,1)}), bf16[8,8,2048]{2,1,0:T(8,128)(2,1)S(1)}, u32[]{:S(2)}, u32[]{:S(2)}) %all-to-all-start.1) | async-done | bytes 262176 | tf_op jit(solution)/shard_map/all_to_all | solution.py:292
  41.5 0.0 copy-done.3
  41.5 0.7 %finish.1 = bf16[8,4096]{1,0:T(8,128)(2,1)} custom-call(bf16[8,8,2048]{2,1,0:T(8,128)(2,1)S(1)} %all-to-all-done.1.parts_ref, bf16[8,4096]{1,0:T(8,128)(2,1)S(1)} %bitcast.13, f32[8,4096]{1,0:T(8,128)S(1)} %get-tuple-element.28.extra_ref), custom_call_target="tpu_custom_call" | custom-call | tf_op jit(solution)/shard_map/finish/pallas_call | solution.py:325
  (3 shorter events, 0.1 us)
Async XLA Ops:
  0.6 10.6 %collective-permute-start = (bf16[128,4096]{1,0:T(8,128)(2,1)}, bf16[128,4096]{1,0:T(8,128)(2,1)S(1)}, u32[]{:S(2)}, u32[]{:S(2)}) collective-permute-start(bf16[128,4096]{1,0:T(8,128)(2,1)} %bitcast.9), channel_id=1, source_target_pairs={{0,4},{4,0},{8,12},{12,8},{16,20},{20,16},{24,28},{28,24},{1,5},{5... | collective-permute-start | bytes 3145736 | tf_op jit(solution)/shard_map/ppermute | solution.py:254
  3.5 7.7 %copy-start.1 = (bf16[1,8,4096]{2,1,0:T(8,128)(2,1)S(1)}, bf16[1,8,4096]{2,1,0:T(8,128)(2,1)}, u32[]{:S(2)}) copy-start(bf16[1,8,4096]{2,1,0:T(8,128)(2,1)} %param.10) | copy-start | bytes 196612
  3.5 7.7 %copy-start.2 = (bf16[1,8,4096]{2,1,0:T(8,128)(2,1)S(1)}, bf16[1,8,4096]{2,1,0:T(8,128)(2,1)}, u32[]{:S(2)}) copy-start(bf16[1,8,4096]{2,1,0:T(8,128)(2,1)} %param.11) | copy-start | bytes 196612
  3.5 20.8 %all-to-all-start = ((bf16[32,40,128]{2,1,0:T(8,128)(2,1)}), bf16[32,40,128]{2,1,0:T(8,128)(2,1)S(1)}, u32[]{:S(2)}, u32[]{:S(2)}) async-start(bf16[32,40,128]{2,1,0:T(8,128)(2,1)} %get-tuple-element.16), calls=%async_computation | async-start | bytes 655360 | tf_op jit(solution)/shard_map/all_to_all | solution.py:244
  10.5 0.7 %copy-start.4 = (f32[8,128]{1,0:T(8,128)S(1)}, f32[8,128]{1,0:T(8,128)}, u32[]{:S(2)}) copy-start(f32[8,128]{1,0:T(8,128)} %get-tuple-element.17._) | copy-start | bytes 12292
  11.3 1.2 %copy-start = (bf16[1,128,4096]{2,1,0:T(8,128)(2,1)S(1)}, bf16[1,128,4096]{2,1,0:T(8,128)(2,1)}, u32[]{:S(2)}) copy-start(bf16[1,128,4096]{2,1,0:T(8,128)(2,1)} %param.8) | copy-start | bytes 3145732
  12.7 11.4 %collective-permute-start.2 = (bf16[8,4096]{1,0:T(8,128)(2,1)S(1)}, bf16[8,4096]{1,0:T(8,128)(2,1)S(1)}, u32[]{:S(2)}, u32[]{:S(2)}) collective-permute-start(bf16[8,4096]{1,0:T(8,128)(2,1)S(1)} %inputs.1.refs_0_.input_ref), channel_id=1, source_target_pairs={{0,16},{4,20},{8,24},{12,28},{16,0},{20,4},{24,8},{28,12},{1,17},{... | collective-permute-start | bytes 196616 | tf_op jit(solution)/shard_map/ppermute | solution.py:277
  15.4 11.8 %collective-permute-start.1 = (bf16[8,4096]{1,0:T(8,128)(2,1)S(1)}, bf16[8,4096]{1,0:T(8,128)(2,1)S(1)}, u32[]{:S(2)}, u32[]{:S(2)}) collective-permute-start(bf16[8,4096]{1,0:T(8,128)(2,1)S(1)} %inputs.1.refs_0_.input_ref), channel_id=1, source_target_pairs={{0,8},{4,12},{8,0},{12,4},{16,24},{20,28},{24,16},{28,20},{1,9},{5... | collective-permute-start | bytes 196616 | tf_op jit(solution)/shard_map/ppermute | solution.py:277
  24.1 4.3 %collective-permute-start.3 = (bf16[8,4096]{1,0:T(8,128)(2,1)S(1)}, bf16[8,4096]{1,0:T(8,128)(2,1)S(1)}, u32[]{:S(2)}, u32[]{:S(2)}) collective-permute-start(bf16[8,4096]{1,0:T(8,128)(2,1)S(1)} %collective-permute-done.2.refs_2_), channel_id=1, source_target_pairs={{0,8},{4,12},{8,0},{12,4},{16,24},{20,28},{24,16},{28,20},{1,9},{5... | collective-permute-start | bytes 196616 | tf_op jit(solution)/shard_map/ppermute | solution.py:277
  28.4 13.1 %all-to-all-start.1 = ((bf16[8,8,2048]{2,1,0:T(8,128)(2,1)}), bf16[8,8,2048]{2,1,0:T(8,128)(2,1)S(1)}, u32[]{:S(2)}, u32[]{:S(2)}) async-start(bf16[8,8,2048]{2,1,0:T(8,128)(2,1)} %bitcast.4), calls=%async_computation.1 | async-start | bytes 524288 | tf_op jit(solution)/shard_map/all_to_all | solution.py:292
  31.9 1.7 %collective-permute-start.4 = (bf16[4,8,4096]{2,1,0:T(8,128)(2,1)S(1)}, bf16[4,8,4096]{2,1,0:T(8,128)(2,1)S(1)}, u32[]{:S(2)}, u32[]{:S(2)}) collective-permute-start(bf16[4,8,4096]{2,1,0:T(8,128)(2,1)S(1)} %get-tuple-element.25.own_stack_ref), channel_id=1, source_target_pairs={{0,4},{4,0},{8,12},{12,8},{16,20},{20,16},{24,28},{28,24},{1,5},{5... | collective-permute-start | bytes 786440 | tf_op jit(solution)/shard_map/ppermute | solution.py:306
  32.3 1.2 %collective-permute-start.5 = (bf16[2,40,128]{2,1,0:T(8,128)(2,1)S(1)}, bf16[2,40,128]{2,1,0:T(8,128)(2,1)S(1)}, u32[]{:S(2)}, u32[]{:S(2)}) collective-permute-start(bf16[2,40,128]{2,1,0:T(8,128)(2,1)S(1)} %get-tuple-element.26.own_head_ref), channel_id=1, source_target_pairs={{0,4},{4,0},{8,12},{12,8},{16,20},{20,16},{24,28},{28,24},{1,5},{5... | collective-permute-start | bytes 61448 | tf_op jit(solution)/shard_map/ppermute | solution.py:307
  33.5 0.7 %copy-start.5 = (s32[1,8,1]{1,2,0:T(1,128)S(1)}, s32[1,8,1]{1,2,0:T(1,128)}, u32[]{:S(2)}) copy-start(s32[1,8,1]{1,2,0:T(1,128)} %param.15) | copy-start | bytes 100
  34.2 7.3 %copy-start.3 = (bf16[1,8,4096]{2,1,0:T(8,128)(2,1)S(1)}, bf16[1,8,4096]{2,1,0:T(8,128)(2,1)}, u32[]{:S(2)}) copy-start(bf16[1,8,4096]{2,1,0:T(8,128)(2,1)} %param.9) | copy-start | bytes 196612

commit v6 on v4

--- a/solution.py
+++ b/solution.py
@@ -19,7 +19,37 @@
     return -(-value // step) * step
 
 
-def pack_kernel(n_ten, taps_hbm, bias_hbm, key_hbm, value_hbm, send_ref, input_ref, *scratch):
+def middle_out(count):
+    low, high = list(range(count // 2))[::-1], list(range(count // 2, count))
+    return [chip for pair in zip(low, high, strict=True) for chip in pair]
+
+
+def part_order(n_blk):
+    return [2 * chip + core for chip in middle_out(n_blk // 2) for core in (1, 0)]
+
+
+def tap_order(n_blk, n_ten):
+    chips = middle_out(n_blk // 2)
+    chips = chips[len(chips) // 2 :] + chips[: len(chips) // 2]
+    return [
+        (2 * chip + core) * n_ten + tenant
+        for core in range(2)
+        for chip in chips
+        for tenant in range(n_ten)
+    ]
+
+
+def tap_place(number, n_blk, n_ten):
+    order = tap_order(n_blk, n_ten)
+    block, tenant = lax.div(number, n_ten), lax.rem(number, n_ten)
+    core, chip = lax.rem(block, 2), lax.div(block, 2)
+    place = jnp.int32(0)
+    for each in range(n_blk // 2):
+        place = jnp.where(chip == each, order.index(2 * each * n_ten), place)
+    return place + core * (len(order) // 2) + tenant
+
+
+def pack_kernel(order, n_ten, taps_hbm, bias_hbm, key_hbm, value_hbm, send_ref, input_ref, *scratch):
     held, sems = scratch[:-1], scratch[-1]
     copies = [
         pltpu.make_async_copy(source, target, sems.at[i])
@@ -44,8 +74,8 @@
         if padded > rows + 1:
             parts.append(jnp.zeros((padded - rows - 1, lanes), f32))
         blocks.append(jnp.concatenate(parts, axis=0).astype(bf16))
-    for dest in range(n_dev):
-        send_ref[dest] = blocks[(dest // n_ten) % 2]
+    for place in range(n_dev):
+        send_ref[place] = blocks[(order[place] // n_ten) % 2]
     input_ref[...] = (key_ref[...].astype(f32) * value_ref[...].astype(f32)).astype(bf16)
 
 
@@ -100,15 +130,18 @@
     return total
 
 
-def conv_kernel(fr, span, gsize, len_ref, taps_ref, source_ref, out_ref, line_ref):
+def conv_kernel(fr, n_ten, gsize, len_ref, taps_ref, source_ref, out_ref, line_ref):
     n_dev, _, groups = taps_ref.shape
+    n_blk, page, _ = out_ref.shape
+    span = n_blk * page
     rows = source_ref.shape[0]
     base = len_ref[0] - lax.div(lax.axis_index("blk"), 2) * rows
     blocks = min(n_dev, -(-(fr - 1 + rows + span - 1) // fr))
     low = jnp.maximum(base - rows + 1, 0)
     first = jnp.clip(lax.div(low, fr), 0, n_dev - blocks)
+    window = [taps_ref[tap_place(first + i, n_blk, n_ten)] for i in range(blocks)]
     line_ref[...] = reversed_taps(
-        taps_ref[pl.ds(first, blocks)], first, fr, base + span - 1, line_ref.shape[1]
+        jnp.stack(window), first, fr, base + span - 1, line_ref.shape[1]
     )
     per = LANES // gsize
     for index in range(groups // per):
@@ -116,20 +149,23 @@
         total = toeplitz_product(
             line_ref, index * per, gsize, span, rows, source_ref[:, columns]
         )
-        out_ref[:, columns] = total.astype(bf16)
-
-
-def gather_kernel(fr, bias_width, _, taps_ref, *refs):
+        for place, block in enumerate(part_order(n_blk)):
+            out_ref[place, :, columns] = total[block * page : (block + 1) * page].astype(bf16)
+
+
+def gather_kernel(order, fr, bias_width, _, taps_ref, *refs):
     pages, (stack_ref, head_ref, bias_ref) = refs[:-3], refs[-3:]
     chip = lax.div(lax.axis_index("blk"), 2)
     n_chip = len(pages)
     for step, page in enumerate(pages):
         stack_ref[lax.rem(chip + n_chip - step, n_chip)] = page[...]
-    head_ref[...] = taps_ref[: head_ref.shape[0]]
+    for index in range(head_ref.shape[0]):
+        head_ref[index] = taps_ref[order.index(index)]
     each = LANES // bias_width
     for index in range(taps_ref.shape[0] // each):
         row = [
-            taps_ref[index * each + i, fr : fr + 1, :bias_width].astype(f32) for i in range(each)
+            taps_ref[order.index(index * each + i), fr : fr + 1, :bias_width].astype(f32)
+            for i in range(each)
         ]
         row = row[0] if each == 1 else jnp.concatenate(row, axis=1)
         bias_ref[:, index * LANES : (index + 1) * LANES] = row
@@ -190,8 +226,9 @@
     for core in range(2):
         columns = slice(core * half, (core + 1) * half)
         total = extra_ref[:, columns]
-        for chip in range(n_blk // 2):
-            total = total + parts_ref[2 * chip + core].astype(f32)
+        for place, block in enumerate(part_order(n_blk)):
+            if block % 2 == core:
+                total = total + parts_ref[place].astype(f32)
         gate = gate_ref[:, columns].astype(f32)
         mixed_ref[:, columns] = (gate * total).astype(bf16)
 
@@ -221,7 +258,7 @@
     swap = [(i, i ^ 1) for i in range(n_blk)]
 
     send, inputs = pl.pallas_call(
-        functools.partial(pack_kernel, n_ten),
+        functools.partial(pack_kernel, tap_order(n_blk, n_ten), n_ten),
         out_shape=(
             jax.ShapeDtypeStruct((n_dev, padded, groups // 2), bf16),
             jax.ShapeDtypeStruct((span_rows, width), bf16),
@@ -239,7 +276,14 @@
         name="pack",
     )(filter_taps, skip_bias.reshape(1, bias_width), span_key[0], span_value[0])
 
-    taps = lax.all_to_all(send, ("blk", "tenant"), split_axis=0, concat_axis=0, tiled=True)
+    taps = lax.all_to_all(
+        send,
+        ("blk", "tenant"),
+        split_axis=0,
+        concat_axis=0,
+        axis_index_groups=[tap_order(n_blk, n_ten)],
+        tiled=True,
+    )
     peer_history = lax.ppermute(history, "blk", swap)
 
     def half_block(count):
@@ -264,8 +308,8 @@
         turn = [(i, (i + 2 * step) % n_blk) for i in range(n_blk)]
         pages.append(lax.ppermute(inputs, "blk", turn))
     partial = pl.pallas_call(
-        functools.partial(conv_kernel, fr, span, gsize),
-        out_shape=jax.ShapeDtypeStruct((span, half), bf16),
+        functools.partial(conv_kernel, fr, n_ten, gsize),
+        out_shape=jax.ShapeDtypeStruct((n_blk, span_rows, half), bf16),
         in_specs=[whole(pltpu.SMEM), whole(), whole()],
         out_specs=whole(),
         scratch_shapes=[pltpu.VMEM((groups // 2, round_up(2 * rows + span - 1, LANES)), f32)],
@@ -275,13 +319,18 @@
 
     partial, *pages = lax.optimization_barrier((partial, *pages))
     parts = lax.all_to_all(
-        partial.reshape(n_blk, span_rows, half), "blk", split_axis=0, concat_axis=0, tiled=True
+        partial,
+        "blk",
+        split_axis=0,
+        concat_axis=0,
+        axis_index_groups=[part_order(n_blk)],
+        tiled=True,
     )
 
     stack = jax.ShapeDtypeStruct((n_chip, span_rows, width), bf16)
     head = jax.ShapeDtypeStruct((min(n_dev, -(-span // fr)), padded, groups // 2), bf16)
     own_stack, own_head, bias = pl.pallas_call(
-        functools.partial(gather_kernel, fr, bias_width),
+        functools.partial(gather_kernel, tap_order(n_blk, n_ten), fr, bias_width),
         out_shape=(stack, head, jax.ShapeDtypeStruct((1, width), f32)),
         in_specs=[whole(pl.ANY)] + [whole()] * (1 + n_chip),
         out_specs=(whole(),) * 3,

time: 42.2 us -> 38.9 us (0.922)
  the two profiles are of different devices: /device:TPU:0 before, /device:TPU:1 now
where the time goes in v6:
time: 38.9 us; the launch traced here: 38.4 us
  starting transfers between devices  15.9 us (41%)
  waiting for transfers between devices  11.9 us (31%)
  Pallas kernels  6.79 us (17%)
  local copies, waits for them, and re-layouts  2.53 us (7%)
  between operations  1.35 us (3%)
    all_to_all x1, starting transfers between devices, per_device(): lax.all_to_all(send, ('blk', 'tenant'), split_axis=0, concat_axis=0, axis...  7.16 us
    all_to_all x1, waiting for transfers between devices, per_device(): lax.all_to_all(send, ('blk', 'tenant'), split_axis=0, concat_axis=0, axis...  7.15 us
    ppermute x3, starting transfers between devices, per_device(): pages.append(lax.ppermute(inputs, 'blk', turn))  4.66 us
    all_to_all x1, waiting for transfers between devices, per_device(): lax.all_to_all(partial, 'blk', split_axis=0, concat_axis=0, axis_index_gr...  3.67 us
    all_to_all x1, starting transfers between devices, per_device(): lax.all_to_all(partial, 'blk', split_axis=0, concat_axis=0, axis_index_gr...  3.37 us
    pallas_call x1, Pallas kernels, per_device(): pl.pallas_call(functools.partial(conv_kernel, fr, n_ten, gsize), out_shap...  2.87 us
    unnamed x8, local copies, waits for them, and re-layouts  2.53 us
    pallas_call x1, Pallas kernels, per_device(): pl.pallas_call(functools.partial(pack_kernel, tap_order(n_blk, n_ten), n_...  1.72 us
  transfers between devices with their start and end apart: 8, of which 3 were waited for; matrix products, arithmetic and copies ran while one was open for 0% of the time, Pallas kernels for 16%

profile of v6, /device:TPU:1, one launch (start us, length us, event | category | flops | bytes accessed | tf_op | source)
XLA Modules:
  0.0 38.4 jit_solution(5947225985426753396)
XLA Ops:
  0.6 0.1 collective-permute-start
  0.8 1.7 %pack.1 = (bf16[32,40,128]{2,1,0:T(8,128)(2,1)}, bf16[8,4096]{1,0:T(8,128)(2,1)}) custom-call(bf16[34,256]{1,0:T(8,128)(2,1)} %taps_hbm.1, bf16[1,128]{1,0:T(2,128)(2,1)} %bitcast.15, bf16[8,4096]{1,0:T(8,128)(2,1)} %bitcast.12, bf16[8,4096]{1,0:T(8,128)(2,1)} %bitcast.13), custom_call_target="tpu_custom_call" | custom-call | tf_op jit(solution)/shard_map/pack/pallas_call | solution.py:260
  2.5 7.2 %all-to-all-start = ((bf16[32,40,128]{2,1,0:T(8,128)(2,1)}), bf16[32,40,128]{2,1,0:T(8,128)(2,1)S(1)}, u32[]{:S(2)}, u32[]{:S(2)}) async-start(bf16[32,40,128]{2,1,0:T(8,128)(2,1)} %get-tuple-element.16), calls=%async_computation | async-start | bytes 655360 | tf_op jit(solution)/shard_map/all_to_all | solution.py:279
  10.3 0.0 collective-permute-done.peer_ref
  10.3 0.0 copy-start
  10.3 1.2 %copy-done = bf16[1,128,4096]{2,1,0:T(8,128)(2,1)S(1)} copy-done((bf16[1,128,4096]{2,1,0:T(8,128)(2,1)S(1)}, bf16[1,128,4096]{2,1,0:T(8,128)(2,1)}, u32[]{:S(2)}) %copy-start) | copy-done | bytes 1048600
  11.5 0.0 copy-start.1
  11.5 0.2 source.1.source_ref
  11.7 0.7 %copy-done.1 = bf16[8,4096]{1,0:T(8,128)(2,1)S(1)} copy-done((bf16[8,4096]{1,0:T(8,128)(2,1)S(1)}, bf16[8,4096]{1,0:T(8,128)(2,1)}, u32[]{:S(2)}) %copy-start.1) | copy-done | bytes 65560
  12.4 1.4 %collective-permute-start.1 = (bf16[8,4096]{1,0:T(8,128)(2,1)S(1)}, bf16[8,4096]{1,0:T(8,128)(2,1)S(1)}, u32[]{:S(2)}, u32[]{:S(2)}) collective-permute-start(bf16[8,4096]{1,0:T(8,128)(2,1)S(1)} %copy-done.1), channel_id=1, source_target_pairs={{0,8},{4,12},{8,16},{12,20},{16,24},{20,28},{24,0},{28,4},{1,9},{5... | collective-permute-start | bytes 196616 | tf_op jit(solution)/shard_map/ppermute | solution.py:309
  13.8 2.1 %collective-permute-start.2 = (bf16[8,4096]{1,0:T(8,128)(2,1)S(1)}, bf16[8,4096]{1,0:T(8,128)(2,1)S(1)}, u32[]{:S(2)}, u32[]{:S(2)}) collective-permute-start(bf16[8,4096]{1,0:T(8,128)(2,1)S(1)} %copy-done.1), channel_id=1, source_target_pairs={{0,16},{4,20},{8,24},{12,28},{16,0},{20,4},{24,8},{28,12},{1,17},{... | collective-permute-start | bytes 196616 | tf_op jit(solution)/shard_map/ppermute | solution.py:309
  15.9 1.1 %collective-permute-start.3 = (bf16[8,4096]{1,0:T(8,128)(2,1)S(1)}, bf16[8,4096]{1,0:T(8,128)(2,1)S(1)}, u32[]{:S(2)}, u32[]{:S(2)}) collective-permute-start(bf16[8,4096]{1,0:T(8,128)(2,1)S(1)} %copy-done.1), channel_id=1, source_target_pairs={{0,24},{4,28},{8,0},{12,4},{16,8},{20,12},{24,16},{28,20},{1,25},{... | collective-permute-start | bytes 196616 | tf_op jit(solution)/shard_map/ppermute | solution.py:309
  17.0 7.2 %all-to-all-done.taps_ref = bf16[32,40,128]{2,1,0:T(8,128)(2,1)S(1)} async-done(((bf16[32,40,128]{2,1,0:T(8,128)(2,1)}), bf16[32,40,128]{2,1,0:T(8,128)(2,1)S(1)}, u32[]{:S(2)}, u32[]{:S(2)}) %all-to-all-start) | async-done | bytes 327712 | tf_op jit(solution)/shard_map/all_to_all | solution.py:279
  24.2 2.9 %conv.1._ = bf16[8,8,2048]{2,1,0:T(8,128)(2,1)} custom-call(s32[1]{0:T(128)S(6)} %copy.10.len_ref, bf16[32,40,128]{2,1,0:T(8,128)(2,1)S(1)} %all-to-all-done.taps_ref, bf16[256,2048]{1,0:T(8,128)(2,1)S(1)} %source.1.source_ref), custom_call_target="tpu_custom_call" | custom-call | tf_op jit(solution)/shard_map/conv/pallas_call | solution.py:310
  27.0 0.0 collective-permute-done.1.refs_1_
  27.1 0.0 collective-permute-done.2.refs_2_
  27.1 0.0 collective-permute-done.3.refs_3_
  27.1 3.4 %all-to-all-start.1 = ((bf16[8,8,2048]{2,1,0:T(8,128)(2,1)}), bf16[8,8,2048]{2,1,0:T(8,128)(2,1)S(1)}, u32[]{:S(2)}, u32[]{:S(2)}) async-start(bf16[8,8,2048]{2,1,0:T(8,128)(2,1)} %conv.1._), calls=%async_computation.1 | async-start | bytes 524288 | tf_op jit(solution)/shard_map/all_to_all | solution.py:321
  30.5 0.1 collective-permute-start.4
  30.6 0.5 %collective-permute-start.5 = (bf16[2,40,128]{2,1,0:T(8,128)(2,1)S(1)}, bf16[2,40,128]{2,1,0:T(8,128)(2,1)S(1)}, u32[]{:S(2)}, u32[]{:S(2)}) collective-permute-start(bf16[2,40,128]{2,1,0:T(8,128)(2,1)S(1)} %get-tuple-element.26.own_head_ref), channel_id=1, source_target_pairs={{0,4},{4,0},{8,12},{12,8},{16,20},{20,16},{24,28},{28,24},{1,5},{5... | collective-permute-start | bytes 61448 | tf_op jit(solution)/shard_map/ppermute | solution.py:341
  31.1 1.1 %collective-permute-done.5.peer_head_ref = bf16[2,40,128]{2,1,0:T(8,128)(2,1)S(1)} collective-permute-done((bf16[2,40,128]{2,1,0:T(8,128)(2,1)S(1)}, bf16[2,40,128]{2,1,0:T(8,128)(2,1)S(1)}, u32[]{:S(2)}, u32[]{:S(2)}) %collective-permute-start.5) | collective-permute-done | bytes 20512 | tf_op jit(solution)/shard_map/ppermute | solution.py:341
  32.1 0.0 collective-permute-done.4.peer_stack_ref
  32.1 0.0 copy-start.3
  32.1 0.7 %copy-done.3 = s32[1,8,1]{1,2,0:T(1,128)S(1)} copy-done((s32[1,8,1]{1,2,0:T(1,128)S(1)}, s32[1,8,1]{1,2,0:T(1,128)}, u32[]{:S(2)}) %copy-start.3) | copy-done | bytes 56
  32.8 0.0 copy-start.2
  32.8 1.3 %span.1 = (f32[8,4096]{1,0:T(8,128)S(1)}, bf16[2,8,4096]{2,1,0:T(8,128)(2,1)}) custom-call(s32[8]{0:T(128)S(1)} %bitcast.11, bf16[4,8,4096]{2,1,0:T(8,128)(2,1)S(1)} %get-tuple-element.25.own_stack_ref, bf16[4,8,4096]{2,1,0:T(8,128)(2,1)S(1)} %collective-permute-done.4.peer_stack_ref, bf16[2,40,128]{2,1,0:T(8,128)(2,1)S(1)} %get-tuple-element.26.own_head_ref, ...), custom_call_target="tpu_custom_call" | custom-call | tf_op jit(solution)/shard_map/span/pallas_call | solution.py:343
  34.1 3.7 %all-to-all-done.1.parts_ref = bf16[8,8,2048]{2,1,0:T(8,128)(2,1)S(1)} async-done(((bf16[8,8,2048]{2,1,0:T(8,128)(2,1)}), bf16[8,8,2048]{2,1,0:T(8,128)(2,1)S(1)}, u32[]{:S(2)}, u32[]{:S(2)}) %all-to-all-start.1) | async-done | bytes 262176 | tf_op jit(solution)/shard_map/all_to_all | solution.py:321
  37.8 0.0 copy-done.2
  37.8 0.7 %finish.1 = bf16[8,4096]{1,0:T(8,128)(2,1)} custom-call(bf16[8,8,2048]{2,1,0:T(8,128)(2,1)S(1)} %all-to-all-done.1.parts_ref, bf16[8,4096]{1,0:T(8,128)(2,1)S(1)} %bitcast.10, f32[8,4096]{1,0:T(8,128)S(1)} %get-tuple-element.28.extra_ref), custom_call_target="tpu_custom_call" | custom-call | tf_op jit(solution)/shard_map/finish/pallas_call | solution.py:359
  (1 shorter events, 0.0 us)
Async XLA Ops:
  0.6 9.7 %collective-permute-start = (bf16[128,4096]{1,0:T(8,128)(2,1)}, bf16[128,4096]{1,0:T(8,128)(2,1)S(1)}, u32[]{:S(2)}, u32[]{:S(2)}) collective-permute-start(bf16[128,4096]{1,0:T(8,128)(2,1)} %bitcast.8), channel_id=1, source_target_pairs={{0,4},{4,0},{8,12},{12,8},{16,20},{20,16},{24,28},{28,24},{1,5},{5... | collective-permute-start | bytes 3145736 | tf_op jit(solution)/shard_map/ppermute | solution.py:287
  2.5 21.7 %all-to-all-start = ((bf16[32,40,128]{2,1,0:T(8,128)(2,1)}), bf16[32,40,128]{2,1,0:T(8,128)(2,1)S(1)}, u32[]{:S(2)}, u32[]{:S(2)}) async-start(bf16[32,40,128]{2,1,0:T(8,128)(2,1)} %get-tuple-element.16), calls=%async_computation | async-start | bytes 655360 | tf_op jit(solution)/shard_map/all_to_all | solution.py:279
  10.3 1.2 %copy-start = (bf16[1,128,4096]{2,1,0:T(8,128)(2,1)S(1)}, bf16[1,128,4096]{2,1,0:T(8,128)(2,1)}, u32[]{:S(2)}) copy-start(bf16[1,128,4096]{2,1,0:T(8,128)(2,1)} %param.8) | copy-start | bytes 3145732
  11.5 0.8 %copy-start.1 = (bf16[8,4096]{1,0:T(8,128)(2,1)S(1)}, bf16[8,4096]{1,0:T(8,128)(2,1)}, u32[]{:S(2)}) copy-start(bf16[8,4096]{1,0:T(8,128)(2,1)} %get-tuple-element.21.refs_0_.input_ref) | copy-start | bytes 196612
  12.4 14.7 %collective-permute-start.1 = (bf16[8,4096]{1,0:T(8,128)(2,1)S(1)}, bf16[8,4096]{1,0:T(8,128)(2,1)S(1)}, u32[]{:S(2)}, u32[]{:S(2)}) collective-permute-start(bf16[8,4096]{1,0:T(8,128)(2,1)S(1)} %copy-done.1), channel_id=1, source_target_pairs={{0,8},{4,12},{8,16},{12,20},{16,24},{20,28},{24,0},{28,4},{1,9},{5... | collective-permute-start | bytes 196616 | tf_op jit(solution)/shard_map/ppermute | solution.py:309
  13.8 13.3 %collective-permute-start.2 = (bf16[8,4096]{1,0:T(8,128)(2,1)S(1)}, bf16[8,4096]{1,0:T(8,128)(2,1)S(1)}, u32[]{:S(2)}, u32[]{:S(2)}) collective-permute-start(bf16[8,4096]{1,0:T(8,128)(2,1)S(1)} %copy-done.1), channel_id=1, source_target_pairs={{0,16},{4,20},{8,24},{12,28},{16,0},{20,4},{24,8},{28,12},{1,17},{... | collective-permute-start | bytes 196616 | tf_op jit(solution)/shard_map/ppermute | solution.py:309
  15.9 11.2 %collective-permute-start.3 = (bf16[8,4096]{1,0:T(8,128)(2,1)S(1)}, bf16[8,4096]{1,0:T(8,128)(2,1)S(1)}, u32[]{:S(2)}, u32[]{:S(2)}) collective-permute-start(bf16[8,4096]{1,0:T(8,128)(2,1)S(1)} %copy-done.1), channel_id=1, source_target_pairs={{0,24},{4,28},{8,0},{12,4},{16,8},{20,12},{24,16},{28,20},{1,25},{... | collective-permute-start | bytes 196616 | tf_op jit(solution)/shard_map/ppermute | solution.py:309
  27.1 10.7 %all-to-all-start.1 = ((bf16[8,8,2048]{2,1,0:T(8,128)(2,1)}), bf16[8,8,2048]{2,1,0:T(8,128)(2,1)S(1)}, u32[]{:S(2)}, u32[]{:S(2)}) async-start(bf16[8,8,2048]{2,1,0:T(8,128)(2,1)} %conv.1._), calls=%async_computation.1 | async-start | bytes 524288 | tf_op jit(solution)/shard_map/all_to_all | solution.py:321
  30.5 1.6 %collective-permute-start.4 = (bf16[4,8,4096]{2,1,0:T(8,128)(2,1)S(1)}, bf16[4,8,4096]{2,1,0:T(8,128)(2,1)S(1)}, u32[]{:S(2)}, u32[]{:S(2)}) collective-permute-start(bf16[4,8,4096]{2,1,0:T(8,128)(2,1)S(1)} %get-tuple-element.25.own_stack_ref), channel_id=1, source_target_pairs={{0,4},{4,0},{8,12},{12,8},{16,20},{20,16},{24,28},{28,24},{1,5},{5... | collective-permute-start | bytes 786440 | tf_op jit(solution)/shard_map/ppermute | solution.py:340
  30.6 1.6 %collective-permute-start.5 = (bf16[2,40,128]{2,1,0:T(8,128)(2,1)S(1)}, bf16[2,40,128]{2,1,0:T(8,128)(2,1)S(1)}, u32[]{:S(2)}, u32[]{:S(2)}) collective-permute-start(bf16[2,40,128]{2,1,0:T(8,128)(2,1)S(1)} %get-tuple-element.26.own_head_ref), channel_id=1, source_target_pairs={{0,4},{4,0},{8,12},{12,8},{16,20},{20,16},{24,28},{28,24},{1,5},{5... | collective-permute-start | bytes 61448 | tf_op jit(solution)/shard_map/ppermute | solution.py:341
  32.1 0.7 %copy-start.3 = (s32[1,8,1]{1,2,0:T(1,128)S(1)}, s32[1,8,1]{1,2,0:T(1,128)}, u32[]{:S(2)}) copy-start(s32[1,8,1]{1,2,0:T(1,128)} %param.15) | copy-start | bytes 100
  32.8 5.0 %copy-start.2 = (bf16[1,8,4096]{2,1,0:T(8,128)(2,1)S(1)}, bf16[1,8,4096]{2,1,0:T(8,128)(2,1)}, u32[]{:S(2)}) copy-start(bf16[1,8,4096]{2,1,0:T(8,128)(2,1)} %param.9) | copy-start | bytes 196612

commit v7 on v6

--- a/solution.py
+++ b/solution.py
@@ -156,9 +156,8 @@
 def gather_kernel(order, fr, bias_width, _, taps_ref, *refs):
     pages, (stack_ref, head_ref, bias_ref) = refs[:-3], refs[-3:]
     chip = lax.div(lax.axis_index("blk"), 2)
-    n_chip = len(pages)
     for step, page in enumerate(pages):
-        stack_ref[lax.rem(chip + n_chip - step, n_chip)] = page[...]
+        stack_ref[lax.bitwise_xor(chip, step)] = page[...]
     for index in range(head_ref.shape[0]):
         head_ref[index] = taps_ref[order.index(index)]
     each = LANES // bias_width
@@ -302,11 +301,14 @@
         name="source",
     )(lengths, history, peer_history)
 
-    source, inputs = lax.optimization_barrier((source, inputs))
-    pages = [inputs]
-    for step in range(1, n_chip):
-        turn = [(i, (i + 2 * step) % n_blk) for i in range(n_blk)]
-        pages.append(lax.ppermute(inputs, "blk", turn))
+    pages = {0: inputs}
+    far = n_chip // 2
+    while far:
+        across = [(i, i ^ (2 * far)) for i in range(n_blk)]
+        pages.update({at ^ far: lax.ppermute(page, "blk", across) for at, page in pages.items()})
+        far //= 2
+    pages = [pages[at] for at in range(n_chip)]
+
     partial = pl.pallas_call(
         functools.partial(conv_kernel, fr, n_ten, gsize),
         out_shape=jax.ShapeDtypeStruct((n_blk, span_rows, half), bf16),

time: 38.9 us -> 41.5 us (1.067)
  waiting for transfers between devices: 11.9 us -> 14.8 us
  local copies, waits for them, and re-layouts: 2.53 us -> 1.89 us
    ppermute x3, waiting for transfers between devices: 0.01 us -> 9.39 us  [per_device(): lax.ppermute(page, 'blk', across)]
    all_to_all x1, waiting for transfers between devices: 7.15 us -> 0.01 us  [per_device(): lax.all_to_all(send, ('blk', 'tenant'), split_axis=0, concat_axis=0, axis...]
    all_to_all x1, starting transfers between devices: 3.37 us -> 4.8 us  [per_device(): lax.all_to_all(partial, 'blk', split_axis=0, concat_axis=0, axis_index_gr...]
    ppermute x3, starting transfers between devices: 4.66 us -> 3.59 us  [per_device(): lax.ppermute(page, 'blk', across)]
    unnamed x8, local copies, waits for them, and re-layouts: 2.53 us -> 1.89 us
    all_to_all x1, waiting for transfers between devices: 3.67 us -> 4.24 us  [per_device(): lax.all_to_all(partial, 'blk', split_axis=0, concat_axis=0, axis_index_gr...]
    ppermute x1, starting transfers between devices: 0.07 us -> 0.49 us  [per_device(): peer_stack = lax.ppermute(own_stack, 'blk', swap)]
    ppermute x1, starting transfers between devices: 0.5 us -> 0.08 us  [per_device(): peer_head = lax.ppermute(own_head, 'blk', swap)]
  transfers between devices with their start and end apart: 8 -> 8, of which waited for: 3 -> 3; matrix products, arithmetic and copies ran while one was open for 0% -> 0% of each run, Pallas kernels for 16% -> 15%
where the time goes in v7:
time: 41.5 us; the launch traced here: 41.1 us
  starting transfers between devices  16.2 us (39%)
  waiting for transfers between devices  14.8 us (36%)
  Pallas kernels  6.82 us (16%)
  local copies, waits for them, and re-layouts  1.89 us (5%)
  between operations  1.36 us (3%)
    ppermute x3, waiting for transfers between devices, per_device(): lax.ppermute(page, 'blk', across)  9.39 us
    all_to_all x1, starting transfers between devices, per_device(): lax.all_to_all(send, ('blk', 'tenant'), split_axis=0, concat_axis=0, axis...  7.16 us
    all_to_all x1, starting transfers between devices, per_device(): lax.all_to_all(partial, 'blk', split_axis=0, concat_axis=0, axis_index_gr...  4.8 us
    all_to_all x1, waiting for transfers between devices, per_device(): lax.all_to_all(partial, 'blk', split_axis=0, concat_axis=0, axis_index_gr...  4.24 us
    ppermute x3, starting transfers between devices, per_device(): lax.ppermute(page, 'blk', across)  3.59 us
    pallas_call x1, Pallas kernels, per_device(): pl.pallas_call(functools.partial(conv_kernel, fr, n_ten, gsize), out_shap...  2.89 us
    unnamed x8, local copies, waits for them, and re-layouts  1.89 us
    pallas_call x1, Pallas kernels, per_device(): pl.pallas_call(functools.partial(pack_kernel, tap_order(n_blk, n_ten), n_...  1.72 us
  transfers between devices with their start and end apart: 8, of which 3 were waited for; matrix products, arithmetic and copies ran while one was open for 0% of the time, Pallas kernels for 15%

profile of v7, /device:TPU:1, one launch (start us, length us, event | category | flops | bytes accessed | tf_op | source)
XLA Modules:
  0.0 41.1 jit_solution(3828066577886188584)
XLA Ops:
  0.6 0.1 collective-permute-start
  0.8 1.7 %pack.1 = (bf16[32,40,128]{2,1,0:T(8,128)(2,1)}, bf16[8,4096]{1,0:T(8,128)(2,1)}) custom-call(bf16[34,256]{1,0:T(8,128)(2,1)} %taps_hbm.1, bf16[1,128]{1,0:T(2,128)(2,1)} %bitcast.15, bf16[8,4096]{1,0:T(8,128)(2,1)} %bitcast.12, bf16[8,4096]{1,0:T(8,128)(2,1)} %bitcast.13), custom_call_target="tpu_custom_call" | custom-call | tf_op jit(solution)/shard_map/pack/pallas_call | solution.py:259
  2.5 0.0 copy-start.1
  2.5 7.2 %all-to-all-start = ((bf16[32,40,128]{2,1,0:T(8,128)(2,1)}), bf16[32,40,128]{2,1,0:T(8,128)(2,1)S(1)}, u32[]{:S(2)}, u32[]{:S(2)}) async-start(bf16[32,40,128]{2,1,0:T(8,128)(2,1)} %get-tuple-element.14), calls=%async_computation | async-start | bytes 655360 | tf_op jit(solution)/shard_map/all_to_all | solution.py:278
  9.7 0.0 copy-done.1
  9.7 2.4 %collective-permute-start.2 = (bf16[8,4096]{1,0:T(8,128)(2,1)S(1)}, bf16[8,4096]{1,0:T(8,128)(2,1)S(1)}, u32[]{:S(2)}, u32[]{:S(2)}) collective-permute-start(bf16[8,4096]{1,0:T(8,128)(2,1)S(1)} %copy-done.1), channel_id=1, source_target_pairs={{0,16},{4,20},{8,24},{12,28},{16,0},{20,4},{24,8},{28,12},{1,17},{... | collective-permute-start | bytes 196616 | tf_op jit(solution)/shard_map/ppermute | solution.py:308
  12.0 1.2 %collective-permute-start.1 = (bf16[8,4096]{1,0:T(8,128)(2,1)S(1)}, bf16[8,4096]{1,0:T(8,128)(2,1)S(1)}, u32[]{:S(2)}, u32[]{:S(2)}) collective-permute-start(bf16[8,4096]{1,0:T(8,128)(2,1)S(1)} %copy-done.1), channel_id=1, source_target_pairs={{0,8},{4,12},{8,0},{12,4},{16,24},{20,28},{24,16},{28,20},{1,9},{5... | collective-permute-start | bytes 196616 | tf_op jit(solution)/shard_map/ppermute | solution.py:308
  13.3 9.4 %collective-permute-done.2.refs_2_ = bf16[8,4096]{1,0:T(8,128)(2,1)S(1)} collective-permute-done((bf16[8,4096]{1,0:T(8,128)(2,1)S(1)}, bf16[8,4096]{1,0:T(8,128)(2,1)S(1)}, u32[]{:S(2)}, u32[]{:S(2)}) %collective-permute-start.2) | collective-permute-done | bytes 65568 | tf_op jit(solution)/shard_map/ppermute | solution.py:308
  22.6 0.0 collective-permute-start.3
  23.3 0.0 collective-permute-done.peer_ref
  23.3 0.0 copy-start
  23.3 1.2 %copy-done = bf16[1,128,4096]{2,1,0:T(8,128)(2,1)S(1)} copy-done((bf16[1,128,4096]{2,1,0:T(8,128)(2,1)S(1)}, bf16[1,128,4096]{2,1,0:T(8,128)(2,1)}, u32[]{:S(2)}) %copy-start) | copy-done | bytes 1048600
  24.5 0.2 source.1.source_ref
  24.7 0.0 all-to-all-done.taps_ref
  24.7 2.9 %conv.1._ = bf16[8,8,2048]{2,1,0:T(8,128)(2,1)} custom-call(s32[1]{0:T(128)S(6)} %copy.10.len_ref, bf16[32,40,128]{2,1,0:T(8,128)(2,1)S(1)} %all-to-all-done.taps_ref, bf16[256,2048]{1,0:T(8,128)(2,1)S(1)} %source.1.source_ref), custom_call_target="tpu_custom_call" | custom-call | tf_op jit(solution)/shard_map/conv/pallas_call | solution.py:312
  27.6 0.0 collective-permute-done.1.refs_1_
  27.6 0.0 collective-permute-done.3.refs_3_
  27.6 4.8 %all-to-all-start.1 = ((bf16[8,8,2048]{2,1,0:T(8,128)(2,1)}), bf16[8,8,2048]{2,1,0:T(8,128)(2,1)S(1)}, u32[]{:S(2)}, u32[]{:S(2)}) async-start(bf16[8,8,2048]{2,1,0:T(8,128)(2,1)} %conv.1._), calls=%async_computation.1 | async-start | bytes 524288 | tf_op jit(solution)/shard_map/all_to_all | solution.py:323
  32.5 0.5 %collective-permute-start.4 = (bf16[4,8,4096]{2,1,0:T(8,128)(2,1)S(1)}, bf16[4,8,4096]{2,1,0:T(8,128)(2,1)S(1)}, u32[]{:S(2)}, u32[]{:S(2)}) collective-permute-start(bf16[4,8,4096]{2,1,0:T(8,128)(2,1)S(1)} %get-tuple-element.21.own_stack_ref), channel_id=1, source_target_pairs={{0,4},{4,0},{8,12},{12,8},{16,20},{20,16},{24,28},{28,24},{1,5},{5... | collective-permute-start | bytes 786440 | tf_op jit(solution)/shard_map/ppermute | solution.py:342
  33.0 0.1 collective-permute-start.5
  33.1 1.1 %collective-permute-done.5.peer_head_ref = bf16[2,40,128]{2,1,0:T(8,128)(2,1)S(1)} collective-permute-done((bf16[2,40,128]{2,1,0:T(8,128)(2,1)S(1)}, bf16[2,40,128]{2,1,0:T(8,128)(2,1)S(1)}, u32[]{:S(2)}, u32[]{:S(2)}) %collective-permute-start.5) | collective-permute-done | bytes 20512 | tf_op jit(solution)/shard_map/ppermute | solution.py:343
  34.2 0.0 collective-permute-done.4.peer_stack_ref
  34.2 0.0 copy-start.3
  34.2 0.7 %copy-done.3 = s32[1,8,1]{1,2,0:T(1,128)S(1)} copy-done((s32[1,8,1]{1,2,0:T(1,128)S(1)}, s32[1,8,1]{1,2,0:T(1,128)}, u32[]{:S(2)}) %copy-start.3) | copy-done | bytes 56
  34.8 0.0 copy-start.2
  34.8 1.3 %span.1 = (f32[8,4096]{1,0:T(8,128)S(1)}, bf16[2,8,4096]{2,1,0:T(8,128)(2,1)}) custom-call(s32[8]{0:T(128)S(1)} %bitcast.11, bf16[4,8,4096]{2,1,0:T(8,128)(2,1)S(1)} %get-tuple-element.21.own_stack_ref, bf16[4,8,4096]{2,1,0:T(8,128)(2,1)S(1)} %collective-permute-done.4.peer_stack_ref, bf16[2,40,128]{2,1,0:T(8,128)(2,1)S(1)} %get-tuple-element.22.own_head_ref, ...), custom_call_target="tpu_custom_call" | custom-call | tf_op jit(solution)/shard_map/span/pallas_call | solution.py:345
  36.1 4.2 %all-to-all-done.1.parts_ref = bf16[8,8,2048]{2,1,0:T(8,128)(2,1)S(1)} async-done(((bf16[8,8,2048]{2,1,0:T(8,128)(2,1)}), bf16[8,8,2048]{2,1,0:T(8,128)(2,1)S(1)}, u32[]{:S(2)}, u32[]{:S(2)}) %all-to-all-start.1) | async-done | bytes 262176 | tf_op jit(solution)/shard_map/all_to_all | solution.py:323
  40.4 0.0 copy-done.2
  40.4 0.7 %finish.1 = bf16[8,4096]{1,0:T(8,128)(2,1)} custom-call(bf16[8,8,2048]{2,1,0:T(8,128)(2,1)S(1)} %all-to-all-done.1.parts_ref, bf16[8,4096]{1,0:T(8,128)(2,1)S(1)} %bitcast.10, f32[8,4096]{1,0:T(8,128)S(1)} %get-tuple-element.24.extra_ref), custom_call_target="tpu_custom_call" | custom-call | tf_op jit(solution)/shard_map/finish/pallas_call | solution.py:361
  (1 shorter events, 0.0 us)
Async XLA Ops:
  0.6 22.7 %collective-permute-start = (bf16[128,4096]{1,0:T(8,128)(2,1)}, bf16[128,4096]{1,0:T(8,128)(2,1)S(1)}, u32[]{:S(2)}, u32[]{:S(2)}) collective-permute-start(bf16[128,4096]{1,0:T(8,128)(2,1)} %bitcast.8), channel_id=1, source_target_pairs={{0,4},{4,0},{8,12},{12,8},{16,20},{20,16},{24,28},{28,24},{1,5},{5... | collective-permute-start | bytes 3145736 | tf_op jit(solution)/shard_map/ppermute | solution.py:286
  2.5 7.2 %copy-start.1 = (bf16[8,4096]{1,0:T(8,128)(2,1)S(1)}, bf16[8,4096]{1,0:T(8,128)(2,1)}, u32[]{:S(2)}) copy-start(bf16[8,4096]{1,0:T(8,128)(2,1)} %get-tuple-element.17.refs_0_.input_ref) | copy-start | bytes 196612
  2.5 22.2 %all-to-all-start = ((bf16[32,40,128]{2,1,0:T(8,128)(2,1)}), bf16[32,40,128]{2,1,0:T(8,128)(2,1)S(1)}, u32[]{:S(2)}, u32[]{:S(2)}) async-start(bf16[32,40,128]{2,1,0:T(8,128)(2,1)} %get-tuple-element.14), calls=%async_computation | async-start | bytes 655360 | tf_op jit(solution)/shard_map/all_to_all | solution.py:278
  9.7 13.0 %collective-permute-start.2 = (bf16[8,4096]{1,0:T(8,128)(2,1)S(1)}, bf16[8,4096]{1,0:T(8,128)(2,1)S(1)}, u32[]{:S(2)}, u32[]{:S(2)}) collective-permute-start(bf16[8,4096]{1,0:T(8,128)(2,1)S(1)} %copy-done.1), channel_id=1, source_target_pairs={{0,16},{4,20},{8,24},{12,28},{16,0},{20,4},{24,8},{28,12},{1,17},{... | collective-permute-start | bytes 196616 | tf_op jit(solution)/shard_map/ppermute | solution.py:308
  12.0 15.6 %collective-permute-start.1 = (bf16[8,4096]{1,0:T(8,128)(2,1)S(1)}, bf16[8,4096]{1,0:T(8,128)(2,1)S(1)}, u32[]{:S(2)}, u32[]{:S(2)}) collective-permute-start(bf16[8,4096]{1,0:T(8,128)(2,1)S(1)} %copy-done.1), channel_id=1, source_target_pairs={{0,8},{4,12},{8,0},{12,4},{16,24},{20,28},{24,16},{28,20},{1,9},{5... | collective-permute-start | bytes 196616 | tf_op jit(solution)/shard_map/ppermute | solution.py:308
  22.6 5.0 %collective-permute-start.3 = (bf16[8,4096]{1,0:T(8,128)(2,1)S(1)}, bf16[8,4096]{1,0:T(8,128)(2,1)S(1)}, u32[]{:S(2)}, u32[]{:S(2)}) collective-permute-start(bf16[8,4096]{1,0:T(8,128)(2,1)S(1)} %collective-permute-done.2.refs_2_), channel_id=1, source_target_pairs={{0,8},{4,12},{8,0},{12,4},{16,24},{20,28},{24,16},{28,20},{1,9},{5... | collective-permute-start | bytes 196616 | tf_op jit(solution)/shard_map/ppermute | solution.py:308
  23.3 1.2 %copy-start = (bf16[1,128,4096]{2,1,0:T(8,128)(2,1)S(1)}, bf16[1,128,4096]{2,1,0:T(8,128)(2,1)}, u32[]{:S(2)}) copy-start(bf16[1,128,4096]{2,1,0:T(8,128)(2,1)} %param.8) | copy-start | bytes 3145732
  27.6 12.7 %all-to-all-start.1 = ((bf16[8,8,2048]{2,1,0:T(8,128)(2,1)}), bf16[8,8,2048]{2,1,0:T(8,128)(2,1)S(1)}, u32[]{:S(2)}, u32[]{:S(2)}) async-start(bf16[8,8,2048]{2,1,0:T(8,128)(2,1)} %conv.1._), calls=%async_computation.1 | async-start | bytes 524288 | tf_op jit(solution)/shard_map/all_to_all | solution.py:323
  32.5 1.7 %collective-permute-start.4 = (bf16[4,8,4096]{2,1,0:T(8,128)(2,1)S(1)}, bf16[4,8,4096]{2,1,0:T(8,128)(2,1)S(1)}, u32[]{:S(2)}, u32[]{:S(2)}) collective-permute-start(bf16[4,8,4096]{2,1,0:T(8,128)(2,1)S(1)} %get-tuple-element.21.own_stack_ref), channel_id=1, source_target_pairs={{0,4},{4,0},{8,12},{12,8},{16,20},{20,16},{24,28},{28,24},{1,5},{5... | collective-permute-start | bytes 786440 | tf_op jit(solution)/shard_map/ppermute | solution.py:342
  33.0 1.2 %collective-permute-start.5 = (bf16[2,40,128]{2,1,0:T(8,128)(2,1)S(1)}, bf16[2,40,128]{2,1,0:T(8,128)(2,1)S(1)}, u32[]{:S(2)}, u32[]{:S(2)}) collective-permute-start(bf16[2,40,128]{2,1,0:T(8,128)(2,1)S(1)} %get-tuple-element.22.own_head_ref), channel_id=1, source_target_pairs={{0,4},{4,0},{8,12},{12,8},{16,20},{20,16},{24,28},{28,24},{1,5},{5... | collective-permute-start | bytes 61448 | tf_op jit(solution)/shard_map/ppermute | solution.py:343
  34.2 0.7 %copy-start.3 = (s32[1,8,1]{1,2,0:T(1,128)S(1)}, s32[1,8,1]{1,2,0:T(1,128)}, u32[]{:S(2)}) copy-start(s32[1,8,1]{1,2,0:T(1,128)} %param.15) | copy-start | bytes 100
  34.8 5.6 %copy-start.2 = (bf16[1,8,4096]{2,1,0:T(8,128)(2,1)S(1)}, bf16[1,8,4096]{2,1,0:T(8,128)(2,1)}, u32[]{:S(2)}) copy-start(bf16[1,8,4096]{2,1,0:T(8,128)(2,1)} %param.9) | copy-start | bytes 196612

commit v8 on v6

--- a/solution.py
+++ b/solution.py
@@ -49,20 +49,20 @@
     return place + core * (len(order) // 2) + tenant
 
 
-def pack_kernel(order, n_ten, taps_hbm, bias_hbm, key_hbm, value_hbm, send_ref, input_ref, *scratch):
+def pack_kernel(order, n_ten, taps_hbm, bias_hbm, send_ref, token_ref, *scratch):
     held, sems = scratch[:-1], scratch[-1]
     copies = [
         pltpu.make_async_copy(source, target, sems.at[i])
-        for i, (source, target) in enumerate(
-            zip((taps_hbm, bias_hbm, key_hbm, value_hbm), held, strict=True)
-        )
+        for i, (source, target) in enumerate(zip((taps_hbm, bias_hbm), held, strict=True))
     ]
     for copy in copies:
         copy.start()
+    token_ref[...] = jnp.zeros_like(token_ref)
     for copy in copies:
         copy.wait()
-    taps_ref, bias_ref, key_ref, value_ref = held
-    n_dev, padded, lanes = send_ref.shape
+    taps_ref, bias_ref = held
+    n_dev, pairs, _, lanes = send_ref.shape
+    padded = 2 * pairs
     rows = taps_ref.shape[0]
     bias = bias_ref[...].astype(f32)
     if bias.shape[1] < lanes:
@@ -73,9 +73,12 @@
         parts = [taps, bias]
         if padded > rows + 1:
             parts.append(jnp.zeros((padded - rows - 1, lanes), f32))
-        blocks.append(jnp.concatenate(parts, axis=0).astype(bf16))
+        blocks.append(jnp.concatenate(parts, axis=0).astype(bf16).reshape(pairs, 2, lanes))
     for place in range(n_dev):
         send_ref[place] = blocks[(order[place] // n_ten) % 2]
+
+
+def input_kernel(_, key_ref, value_ref, input_ref):
     input_ref[...] = (key_ref[...].astype(f32) * value_ref[...].astype(f32)).astype(bf16)
 
 
@@ -98,13 +101,13 @@
 
 def reversed_taps(window, first, fr, top_lag, lanes):
     blocks, padded, groups = window.shape
-    shape = (blocks, padded, lanes)
-    block = lax.broadcasted_iota(jnp.int32, shape, 0)
-    row = lax.broadcasted_iota(jnp.int32, shape, 1)
-    lane = lax.broadcasted_iota(jnp.int32, shape, 2)
+    shape = (blocks * padded, lanes)
+    index = lax.broadcasted_iota(jnp.int32, shape, 0)
+    lane = lax.broadcasted_iota(jnp.int32, shape, 1)
+    block = lax.div(index * ((1 << 16) // padded + 1), 1 << 16)
+    row = index - block * padded
     lag = (first + block) * fr + row
-    pick = jnp.where((row < fr) & (lag + lane == top_lag), 1.0, 0.0)
-    pick = pick.reshape(blocks * padded, lanes).astype(bf16)
+    pick = jnp.where((row < fr) & (lag + lane == top_lag), 1.0, 0.0).astype(bf16)
     return lax.dot_general(
         window.reshape(blocks * padded, groups),
         pick,
@@ -131,7 +134,7 @@
 
 
 def conv_kernel(fr, n_ten, gsize, len_ref, taps_ref, source_ref, out_ref, line_ref):
-    n_dev, _, groups = taps_ref.shape
+    n_dev, pairs, _, groups = taps_ref.shape
     n_blk, page, _ = out_ref.shape
     span = n_blk * page
     rows = source_ref.shape[0]
@@ -139,7 +142,10 @@
     blocks = min(n_dev, -(-(fr - 1 + rows + span - 1) // fr))
     low = jnp.maximum(base - rows + 1, 0)
     first = jnp.clip(lax.div(low, fr), 0, n_dev - blocks)
-    window = [taps_ref[tap_place(first + i, n_blk, n_ten)] for i in range(blocks)]
+    window = [
+        taps_ref[tap_place(first + i, n_blk, n_ten)].reshape(2 * pairs, groups)
+        for i in range(blocks)
+    ]
     line_ref[...] = reversed_taps(
         jnp.stack(window), first, fr, base + span - 1, line_ref.shape[1]
     )
@@ -160,11 +166,11 @@
     for step, page in enumerate(pages):
         stack_ref[lax.rem(chip + n_chip - step, n_chip)] = page[...]
     for index in range(head_ref.shape[0]):
-        head_ref[index] = taps_ref[order.index(index)]
+        head_ref[index] = taps_ref[order.index(index)].reshape(head_ref.shape[1:])
     each = LANES // bias_width
     for index in range(taps_ref.shape[0] // each):
         row = [
-            taps_ref[order.index(index * each + i), fr : fr + 1, :bias_width].astype(f32)
+            taps_ref[order.index(index * each + i), fr // 2, fr % 2 : fr % 2 + 1, :bias_width].astype(f32)
             for i in range(each)
         ]
         row = row[0] if each == 1 else jnp.concatenate(row, axis=1)
@@ -253,29 +259,26 @@
     span = span_rows * n_blk
     fr, groups = filter_taps.shape
     gsize = width // groups
-    padded = round_up(fr + 1, 8)
+    pairs = round_up(fr + 1, 2) // 2
     bias_width = skip_bias.shape[0]
     swap = [(i, i ^ 1) for i in range(n_blk)]
 
-    send, inputs = pl.pallas_call(
+    send, token = pl.pallas_call(
         functools.partial(pack_kernel, tap_order(n_blk, n_ten), n_ten),
         out_shape=(
-            jax.ShapeDtypeStruct((n_dev, padded, groups // 2), bf16),
-            jax.ShapeDtypeStruct((span_rows, width), bf16),
+            jax.ShapeDtypeStruct((n_dev, pairs, 2, groups // 2), bf16),
+            jax.ShapeDtypeStruct((8, LANES), f32),
         ),
-        in_specs=[whole(pltpu.HBM)] * 4,
+        in_specs=[whole(pltpu.HBM)] * 2,
         out_specs=(whole(), whole()),
         scratch_shapes=[
             pltpu.VMEM((fr, groups), bf16),
             pltpu.VMEM((1, bias_width), bf16),
-            pltpu.VMEM((span_rows, width), bf16),
-            pltpu.VMEM((span_rows, width), bf16),
-            pltpu.SemaphoreType.DMA((4,)),
+            pltpu.SemaphoreType.DMA((2,)),
         ],
         compiler_params=limit(58),
         name="pack",
-    )(filter_taps, skip_bias.reshape(1, bias_width), span_key[0], span_value[0])
-
+    )(filter_taps, skip_bias.reshape(1, bias_width))
     taps = lax.all_to_all(
         send,
         ("blk", "tenant"),
@@ -302,7 +305,16 @@
         name="source",
     )(lengths, history, peer_history)
 
-    source, inputs = lax.optimization_barrier((source, inputs))
+    inputs = pl.pallas_call(
+        input_kernel,
+        out_shape=jax.ShapeDtypeStruct((span_rows, width), bf16),
+        in_specs=[whole(pl.ANY)] + [whole()] * 2,
+        out_specs=whole(),
+        compiler_params=limit(8),
+        cost_estimate=pl.CostEstimate(flops=32768, bytes_accessed=3 * span_rows * width * 2, transcendentals=0),
+        name="inputs",
+    )(source, span_key[0], span_value[0])
+
     pages = [inputs]
     for step in range(1, n_chip):
         turn = [(i, (i + 2 * step) % n_blk) for i in range(n_blk)]
@@ -328,7 +340,7 @@
     )
 
     stack = jax.ShapeDtypeStruct((n_chip, span_rows, width), bf16)
-    head = jax.ShapeDtypeStruct((min(n_dev, -(-span // fr)), padded, groups // 2), bf16)
+    head = jax.ShapeDtypeStruct((min(n_dev, -(-span // fr)), 2 * pairs, groups // 2), bf16)
     own_stack, own_head, bias = pl.pallas_call(
         functools.partial(gather_kernel, tap_order(n_blk, n_ten), fr, bias_width),
         out_shape=(stack, head, jax.ShapeDtypeStruct((1, width), f32)),

time: 38.9 us -> 38.2 us (0.982)
  waiting for transfers between devices: 11.9 us -> 11.1 us
    all_to_all x1, waiting for transfers between devices: 7.15 us -> 6.35 us  [per_device(): lax.all_to_all(send, ('blk', 'tenant'), split_axis=0, concat_axis=0, axis...]
    unnamed x8 -> x10, local copies, waits for them, and re-layouts: 2.53 us -> 2.56 us
where the time goes in v8:
time: 38.2 us; the launch traced here: 37.8 us
  starting transfers between devices  15.9 us (42%)
  waiting for transfers between devices  11.1 us (29%)
  Pallas kernels  6.86 us (18%)
  local copies, waits for them, and re-layouts  2.56 us (7%)
  between operations  1.35 us (4%)
    all_to_all x1, starting transfers between devices, per_device(): lax.all_to_all(send, ('blk', 'tenant'), split_axis=0, concat_axis=0, axis...  7.16 us
    all_to_all x1, waiting for transfers between devices, per_device(): lax.all_to_all(send, ('blk', 'tenant'), split_axis=0, concat_axis=0, axis...  6.35 us
    ppermute x3, starting transfers between devices, per_device(): pages.append(lax.ppermute(inputs, 'blk', turn))  4.71 us
    all_to_all x1, waiting for transfers between devices, per_device(): lax.all_to_all(partial, 'blk', split_axis=0, concat_axis=0, axis_index_gr...  3.66 us
    all_to_all x1, starting transfers between devices, per_device(): lax.all_to_all(partial, 'blk', split_axis=0, concat_axis=0, axis_index_gr...  3.37 us
    pallas_call x1, Pallas kernels, per_device(): pl.pallas_call(functools.partial(conv_kernel, fr, n_ten, gsize), out_shap...  2.99 us
    unnamed x10, local copies, waits for them, and re-layouts  2.56 us
    pallas_call x1, Pallas kernels, per_device(): pl.pallas_call(functools.partial(pack_kernel, tap_order(n_blk, n_ten), n_...  1.63 us
  transfers between devices with their start and end apart: 8, of which 3 were waited for; matrix products, arithmetic and copies ran while one was open for 0% of the time, Pallas kernels for 16%

profile of v8, /device:TPU:1, one launch (start us, length us, event | category | flops | bytes accessed | tf_op | source)
XLA Modules:
  0.0 37.8 jit_solution(658167683365221369)
XLA Ops:
  0.6 0.1 collective-permute-start
  0.8 1.6 %pack.1 = (bf16[32,18,2,128]{3,2,1,0:T(2,128)(2,1)}, f32[8,128]{1,0:T(8,128)}) custom-call(bf16[34,256]{1,0:T(8,128)(2,1)} %taps_hbm.1, bf16[1,128]{1,0:T(2,128)(2,1)} %bitcast.15), custom_call_target="tpu_custom_call" | custom-call | tf_op jit(solution)/shard_map/pack/pallas_call | solution.py:266
  2.4 7.2 %all-to-all-start = ((bf16[32,18,2,128]{3,2,1,0:T(2,128)(2,1)}), bf16[32,18,2,128]{3,2,1,0:T(2,128)(2,1)S(1)}, u32[]{:S(2)}, u32[]{:S(2)}) async-start(bf16[32,18,2,128]{3,2,1,0:T(2,128)(2,1)} %get-tuple-element.13), calls=%async_computation | async-start | bytes 589824 | tf_op jit(solution)/shard_map/all_to_all | solution.py:282
  10.2 0.0 collective-permute-done.peer_ref
  10.2 0.0 copy-start
  10.2 1.2 %copy-done = bf16[1,128,4096]{2,1,0:T(8,128)(2,1)S(1)} copy-done((bf16[1,128,4096]{2,1,0:T(8,128)(2,1)S(1)}, bf16[1,128,4096]{2,1,0:T(8,128)(2,1)}, u32[]{:S(2)}) %copy-start) | copy-done | bytes 1048600
  11.4 0.0 copy-start.1
  11.4 0.0 copy-start.2
  11.4 0.2 source.1.source_ref._
  11.6 0.6 %copy-done.1 = bf16[1,8,4096]{2,1,0:T(8,128)(2,1)S(1)} copy-done((bf16[1,8,4096]{2,1,0:T(8,128)(2,1)S(1)}, bf16[1,8,4096]{2,1,0:T(8,128)(2,1)}, u32[]{:S(2)}) %copy-start.1) | copy-done | bytes 65560
  12.3 0.0 copy-done.2
  12.3 1.4 %collective-permute-start.1 = (bf16[8,4096]{1,0:T(8,128)(2,1)S(1)}, bf16[8,4096]{1,0:T(8,128)(2,1)S(1)}, u32[]{:S(2)}, u32[]{:S(2)}) collective-permute-start(bf16[8,4096]{1,0:T(8,128)(2,1)S(1)} %inputs.1.refs_0_.input_ref), channel_id=1, source_target_pairs={{0,8},{4,12},{8,16},{12,20},{16,24},{20,28},{24,0},{28,4},{1,9},{5... | collective-permute-start | bytes 196616 | tf_op jit(solution)/shard_map/ppermute | solution.py:321
  13.8 2.1 %collective-permute-start.2 = (bf16[8,4096]{1,0:T(8,128)(2,1)S(1)}, bf16[8,4096]{1,0:T(8,128)(2,1)S(1)}, u32[]{:S(2)}, u32[]{:S(2)}) collective-permute-start(bf16[8,4096]{1,0:T(8,128)(2,1)S(1)} %inputs.1.refs_0_.input_ref), channel_id=1, source_target_pairs={{0,16},{4,20},{8,24},{12,28},{16,0},{20,4},{24,8},{28,12},{1,17},{... | collective-permute-start | bytes 196616 | tf_op jit(solution)/shard_map/ppermute | solution.py:321
  15.9 1.1 %collective-permute-start.3 = (bf16[8,4096]{1,0:T(8,128)(2,1)S(1)}, bf16[8,4096]{1,0:T(8,128)(2,1)S(1)}, u32[]{:S(2)}, u32[]{:S(2)}) collective-permute-start(bf16[8,4096]{1,0:T(8,128)(2,1)S(1)} %inputs.1.refs_0_.input_ref), channel_id=1, source_target_pairs={{0,24},{4,28},{8,0},{12,4},{16,8},{20,12},{24,16},{28,20},{1,25},{... | collective-permute-start | bytes 196616 | tf_op jit(solution)/shard_map/ppermute | solution.py:321
  17.0 6.3 %all-to-all-done.taps_ref = bf16[32,18,2,128]{3,2,1,0:T(2,128)(2,1)S(1)} async-done(((bf16[32,18,2,128]{3,2,1,0:T(2,128)(2,1)}), bf16[32,18,2,128]{3,2,1,0:T(2,128)(2,1)S(1)}, u32[]{:S(2)}, u32[]{:S(2)}) %all-to-all-start) | async-done | bytes 294944 | tf_op jit(solution)/shard_map/all_to_all | solution.py:282
  23.4 3.0 %conv.1._ = bf16[8,8,2048]{2,1,0:T(8,128)(2,1)} custom-call(s32[1]{0:T(128)S(6)} %copy.10.len_ref, bf16[32,18,2,128]{3,2,1,0:T(2,128)(2,1)S(1)} %all-to-all-done.taps_ref, bf16[256,2048]{1,0:T(8,128)(2,1)S(1)} %source.1.source_ref._), custom_call_target="tpu_custom_call" | custom-call | tf_op jit(solution)/shard_map/conv/pallas_call | solution.py:322
  26.4 0.0 collective-permute-done.1.refs_1_
  26.4 0.0 collective-permute-done.2.refs_2_
  26.4 0.0 collective-permute-done.3.refs_3_
  26.4 3.4 %all-to-all-start.1 = ((bf16[8,8,2048]{2,1,0:T(8,128)(2,1)}), bf16[8,8,2048]{2,1,0:T(8,128)(2,1)S(1)}, u32[]{:S(2)}, u32[]{:S(2)}) async-start(bf16[8,8,2048]{2,1,0:T(8,128)(2,1)} %conv.1._), calls=%async_computation.1 | async-start | bytes 524288 | tf_op jit(solution)/shard_map/all_to_all | solution.py:333
  29.8 0.1 collective-permute-start.4
  29.9 0.5 %collective-permute-start.5 = (bf16[2,36,128]{2,1,0:T(8,128)(2,1)S(1)}, bf16[2,36,128]{2,1,0:T(8,128)(2,1)S(1)}, u32[]{:S(2)}, u32[]{:S(2)}) collective-permute-start(bf16[2,36,128]{2,1,0:T(8,128)(2,1)S(1)} %get-tuple-element.20.own_head_ref), channel_id=1, source_target_pairs={{0,4},{4,0},{8,12},{12,8},{16,20},{20,16},{24,28},{28,24},{1,5},{5... | collective-permute-start | bytes 55304 | tf_op jit(solution)/shard_map/ppermute | solution.py:353
  30.4 1.1 %collective-permute-done.5.peer_head_ref = bf16[2,36,128]{2,1,0:T(8,128)(2,1)S(1)} collective-permute-done((bf16[2,36,128]{2,1,0:T(8,128)(2,1)S(1)}, bf16[2,36,128]{2,1,0:T(8,128)(2,1)S(1)}, u32[]{:S(2)}, u32[]{:S(2)}) %collective-permute-start.5) | collective-permute-done | bytes 18464 | tf_op jit(solution)/shard_map/ppermute | solution.py:353
  31.5 0.0 collective-permute-done.4.peer_stack_ref
  31.5 0.0 copy-start.4
  31.5 0.7 %copy-done.4 = s32[1,8,1]{1,2,0:T(1,128)S(1)} copy-done((s32[1,8,1]{1,2,0:T(1,128)S(1)}, s32[1,8,1]{1,2,0:T(1,128)}, u32[]{:S(2)}) %copy-start.4) | copy-done | bytes 56
  32.1 0.0 copy-start.3
  32.1 1.3 %span.1 = (f32[8,4096]{1,0:T(8,128)S(1)}, bf16[2,8,4096]{2,1,0:T(8,128)(2,1)}) custom-call(s32[8]{0:T(128)S(1)} %bitcast.13, bf16[4,8,4096]{2,1,0:T(8,128)(2,1)S(1)} %get-tuple-element.19.own_stack_ref, bf16[4,8,4096]{2,1,0:T(8,128)(2,1)S(1)} %collective-permute-done.4.peer_stack_ref, bf16[2,36,128]{2,1,0:T(8,128)(2,1)S(1)} %get-tuple-element.20.own_head_ref, ...), custom_call_target="tpu_custom_call" | custom-call | tf_op jit(solution)/shard_map/span/pallas_call | solution.py:355
  33.4 3.7 %all-to-all-done.1.parts_ref = bf16[8,8,2048]{2,1,0:T(8,128)(2,1)S(1)} async-done(((bf16[8,8,2048]{2,1,0:T(8,128)(2,1)}), bf16[8,8,2048]{2,1,0:T(8,128)(2,1)S(1)}, u32[]{:S(2)}, u32[]{:S(2)}) %all-to-all-start.1) | async-done | bytes 262176 | tf_op jit(solution)/shard_map/all_to_all | solution.py:333
  37.1 0.0 copy-done.3
  37.1 0.7 %finish.1 = bf16[8,4096]{1,0:T(8,128)(2,1)} custom-call(bf16[8,8,2048]{2,1,0:T(8,128)(2,1)S(1)} %all-to-all-done.1.parts_ref, bf16[8,4096]{1,0:T(8,128)(2,1)S(1)} %bitcast.12, f32[8,4096]{1,0:T(8,128)S(1)} %get-tuple-element.22.extra_ref), custom_call_target="tpu_custom_call" | custom-call | tf_op jit(solution)/shard_map/finish/pallas_call | solution.py:371
  (2 shorter events, 0.1 us)
Async XLA Ops:
  0.6 9.6 %collective-permute-start = (bf16[128,4096]{1,0:T(8,128)(2,1)}, bf16[128,4096]{1,0:T(8,128)(2,1)S(1)}, u32[]{:S(2)}, u32[]{:S(2)}) collective-permute-start(bf16[128,4096]{1,0:T(8,128)(2,1)} %bitcast.8), channel_id=1, source_target_pairs={{0,4},{4,0},{8,12},{12,8},{16,20},{20,16},{24,28},{28,24},{1,5},{5... | collective-permute-start | bytes 3145736 | tf_op jit(solution)/shard_map/ppermute | solution.py:290
  2.4 21.0 %all-to-all-start = ((bf16[32,18,2,128]{3,2,1,0:T(2,128)(2,1)}), bf16[32,18,2,128]{3,2,1,0:T(2,128)(2,1)S(1)}, u32[]{:S(2)}, u32[]{:S(2)}) async-start(bf16[32,18,2,128]{3,2,1,0:T(2,128)(2,1)} %get-tuple-element.13), calls=%async_computation | async-start | bytes 589824 | tf_op jit(solution)/shard_map/all_to_all | solution.py:282
  10.2 1.2 %copy-start = (bf16[1,128,4096]{2,1,0:T(8,128)(2,1)S(1)}, bf16[1,128,4096]{2,1,0:T(8,128)(2,1)}, u32[]{:S(2)}) copy-start(bf16[1,128,4096]{2,1,0:T(8,128)(2,1)} %param.8) | copy-start | bytes 3145732
  11.4 0.8 %copy-start.1 = (bf16[1,8,4096]{2,1,0:T(8,128)(2,1)S(1)}, bf16[1,8,4096]{2,1,0:T(8,128)(2,1)}, u32[]{:S(2)}) copy-start(bf16[1,8,4096]{2,1,0:T(8,128)(2,1)} %param.10) | copy-start | bytes 196612
  11.4 0.9 %copy-start.2 = (bf16[1,8,4096]{2,1,0:T(8,128)(2,1)S(1)}, bf16[1,8,4096]{2,1,0:T(8,128)(2,1)}, u32[]{:S(2)}) copy-start(bf16[1,8,4096]{2,1,0:T(8,128)(2,1)} %param.11) | copy-start | bytes 196612
  12.3 14.1 %collective-permute-start.1 = (bf16[8,4096]{1,0:T(8,128)(2,1)S(1)}, bf16[8,4096]{1,0:T(8,128)(2,1)S(1)}, u32[]{:S(2)}, u32[]{:S(2)}) collective-permute-start(bf16[8,4096]{1,0:T(8,128)(2,1)S(1)} %inputs.1.refs_0_.input_ref), channel_id=1, source_target_pairs={{0,8},{4,12},{8,16},{12,20},{16,24},{20,28},{24,0},{28,4},{1,9},{5... | collective-permute-start | bytes 196616 | tf_op jit(solution)/shard_map/ppermute | solution.py:321
  13.8 12.6 %collective-permute-start.2 = (bf16[8,4096]{1,0:T(8,128)(2,1)S(1)}, bf16[8,4096]{1,0:T(8,128)(2,1)S(1)}, u32[]{:S(2)}, u32[]{:S(2)}) collective-permute-start(bf16[8,4096]{1,0:T(8,128)(2,1)S(1)} %inputs.1.refs_0_.input_ref), channel_id=1, source_target_pairs={{0,16},{4,20},{8,24},{12,28},{16,0},{20,4},{24,8},{28,12},{1,17},{... | collective-permute-start | bytes 196616 | tf_op jit(solution)/shard_map/ppermute | solution.py:321
  15.9 10.5 %collective-permute-start.3 = (bf16[8,4096]{1,0:T(8,128)(2,1)S(1)}, bf16[8,4096]{1,0:T(8,128)(2,1)S(1)}, u32[]{:S(2)}, u32[]{:S(2)}) collective-permute-start(bf16[8,4096]{1,0:T(8,128)(2,1)S(1)} %inputs.1.refs_0_.input_ref), channel_id=1, source_target_pairs={{0,24},{4,28},{8,0},{12,4},{16,8},{20,12},{24,16},{28,20},{1,25},{... | collective-permute-start | bytes 196616 | tf_op jit(solution)/shard_map/ppermute | solution.py:321
  26.4 10.7 %all-to-all-start.1 = ((bf16[8,8,2048]{2,1,0:T(8,128)(2,1)}), bf16[8,8,2048]{2,1,0:T(8,128)(2,1)S(1)}, u32[]{:S(2)}, u32[]{:S(2)}) async-start(bf16[8,8,2048]{2,1,0:T(8,128)(2,1)} %conv.1._), calls=%async_computation.1 | async-start | bytes 524288 | tf_op jit(solution)/shard_map/all_to_all | solution.py:333
  29.8 1.6 %collective-permute-start.4 = (bf16[4,8,4096]{2,1,0:T(8,128)(2,1)S(1)}, bf16[4,8,4096]{2,1,0:T(8,128)(2,1)S(1)}, u32[]{:S(2)}, u32[]{:S(2)}) collective-permute-start(bf16[4,8,4096]{2,1,0:T(8,128)(2,1)S(1)} %get-tuple-element.19.own_stack_ref), channel_id=1, source_target_pairs={{0,4},{4,0},{8,12},{12,8},{16,20},{20,16},{24,28},{28,24},{1,5},{5... | collective-permute-start | bytes 786440 | tf_op jit(solution)/shard_map/ppermute | solution.py:352
  29.9 1.6 %collective-permute-start.5 = (bf16[2,36,128]{2,1,0:T(8,128)(2,1)S(1)}, bf16[2,36,128]{2,1,0:T(8,128)(2,1)S(1)}, u32[]{:S(2)}, u32[]{:S(2)}) collective-permute-start(bf16[2,36,128]{2,1,0:T(8,128)(2,1)S(1)} %get-tuple-element.20.own_head_ref), channel_id=1, source_target_pairs={{0,4},{4,0},{8,12},{12,8},{16,20},{20,16},{24,28},{28,24},{1,5},{5... | collective-permute-start | bytes 55304 | tf_op jit(solution)/shard_map/ppermute | solution.py:353
  31.5 0.7 %copy-start.4 = (s32[1,8,1]{1,2,0:T(1,128)S(1)}, s32[1,8,1]{1,2,0:T(1,128)}, u32[]{:S(2)}) copy-start(s32[1,8,1]{1,2,0:T(1,128)} %param.15) | copy-start | bytes 100
  32.1 5.0 %copy-start.3 = (bf16[1,8,4096]{2,1,0:T(8,128)(2,1)S(1)}, bf16[1,8,4096]{2,1,0:T(8,128)(2,1)}, u32[]{:S(2)}) copy-start(bf16[1,8,4096]{2,1,0:T(8,128)(2,1)} %param.9) | copy-start | bytes 196612

commit v9 on v8

--- a/solution.py
+++ b/solution.py
@@ -82,7 +82,8 @@
     input_ref[...] = (key_ref[...].astype(f32) * value_ref[...].astype(f32)).astype(bf16)
 
 
-def source_kernel(len_ref, own_ref, peer_ref, out_ref):
+def source_kernel(len_ref, own_ref, *refs):
+    peer_refs, out_ref = refs[:-1], refs[-1]
     blk = lax.axis_index("blk")
     core = lax.rem(blk, 2)
     rows, width = own_ref.shape
@@ -90,13 +91,15 @@
     length = len_ref[0]
 
     def masked(value, first):
-        index = first + lax.broadcasted_iota(jnp.int32, (rows, width), 0)
+        index = first + lax.broadcasted_iota(jnp.int32, value.shape, 0)
         return jnp.where(index < length, value.astype(f32), 0.0).astype(bf16)
 
     own_at = pl.multiple_of(core * rows, rows)
-    peer_at = pl.multiple_of((1 - core) * rows, rows)
     out_ref[pl.ds(own_at, rows), :] = masked(own_ref[...], start + core * rows)
-    out_ref[pl.ds(peer_at, rows), :] = masked(peer_ref[...], start + (1 - core) * rows)
+    piece = rows // len(peer_refs)
+    for i, peer_ref in enumerate(peer_refs):
+        peer_at = pl.multiple_of((1 - core) * rows + i * piece, piece)
+        out_ref[pl.ds(peer_at, piece), :] = masked(peer_ref[...], start + peer_at)
 
 
 def reversed_taps(window, first, fr, top_lag, lanes):
@@ -287,7 +290,11 @@
         axis_index_groups=[tap_order(n_blk, n_ten)],
         tiled=True,
     )
-    peer_history = lax.ppermute(history, "blk", swap)
+    pieces = 4
+    piece = rows // pieces
+    peer_history = [
+        lax.ppermute(history[i * piece : (i + 1) * piece], "blk", swap) for i in range(pieces)
+    ]
 
     def half_block(count):
         return pl.BlockSpec((count, half), lambda i, n: (0, lax.rem(lax.axis_index("blk"), 2)))
@@ -297,13 +304,13 @@
         grid_spec=pltpu.PrefetchScalarGridSpec(
             num_scalar_prefetch=1,
             grid=(1,),
-            in_specs=[half_block(rows), half_block(rows)],
+            in_specs=[half_block(rows)] + [half_block(piece)] * pieces,
             out_specs=pl.BlockSpec((2 * rows, half), lambda i, n: (0, 0)),
         ),
         out_shape=jax.ShapeDtypeStruct((2 * rows, half), bf16),
         compiler_params=limit(8),
         name="source",
-    )(lengths, history, peer_history)
+    )(lengths, history, *peer_history)
 
     inputs = pl.pallas_call(
         input_kernel,

time: 38.2 us -> 37.3 us (0.976)
  waiting for transfers between devices: 11.1 us -> 9.08 us
  starting transfers between devices: 15.9 us -> 16.8 us
    all_to_all x1, waiting for transfers between devices: 6.35 us -> 3.16 us  [per_device(): lax.all_to_all(send, ('blk', 'tenant'), split_axis=0, concat_axis=0, axis...]
    slice x0 -> x1, local copies, waits for them, and re-layouts: none -> 1.36 us  [per_device(): history[i * piece:(i + 1) * piece]]
    unnamed x10, local copies, waits for them, and re-layouts: 2.56 us -> 1.34 us
    ppermute x1 -> x4, waiting for transfers between devices: 0.01 us -> 0.98 us  [per_device(): lax.ppermute(history[i * piece:(i + 1) * piece], 'blk', swap)]
    ppermute x1 -> x4, starting transfers between devices: 0.12 us -> 1.09 us  [per_device(): lax.ppermute(history[i * piece:(i + 1) * piece], 'blk', swap)]
  transfers between devices with their start and end apart: 8 -> 11, of which waited for: 3 -> 6; matrix products, arithmetic and copies ran while one was open for 0% -> 4% of each run, Pallas kernels for 16% -> 12%
where the time goes in v9:
time: 37.3 us; the launch traced here: 36.9 us
  starting transfers between devices  16.8 us (45%)
  waiting for transfers between devices  9.08 us (24%)
  Pallas kernels  6.88 us (18%)
  local copies, waits for them, and re-layouts  2.7 us (7%)
  between operations  1.37 us (4%)
    all_to_all x1, starting transfers between devices, per_device(): lax.all_to_all(send, ('blk', 'tenant'), split_axis=0, concat_axis=0, axis...  7.1 us
    ppermute x3, starting transfers between devices, per_device(): pages.append(lax.ppermute(inputs, 'blk', turn))  4.71 us
    all_to_all x1, waiting for transfers between devices, per_device(): lax.all_to_all(partial, 'blk', split_axis=0, concat_axis=0, axis_index_gr...  3.87 us
    all_to_all x1, starting transfers between devices, per_device(): lax.all_to_all(partial, 'blk', split_axis=0, concat_axis=0, axis_index_gr...  3.37 us
    all_to_all x1, waiting for transfers between devices, per_device(): lax.all_to_all(send, ('blk', 'tenant'), split_axis=0, concat_axis=0, axis...  3.16 us
    pallas_call x1, Pallas kernels, per_device(): pl.pallas_call(functools.partial(conv_kernel, fr, n_ten, gsize), out_shap...  3 us
    pallas_call x1, Pallas kernels, per_device(): pl.pallas_call(functools.partial(pack_kernel, tap_order(n_blk, n_ten), n_...  1.64 us
    slice x1, local copies, waits for them, and re-layouts, per_device(): history[i * piece:(i + 1) * piece]  1.36 us
  transfers between devices with their start and end apart: 11, of which 6 were waited for; matrix products, arithmetic and copies ran while one was open for 4% of the time, Pallas kernels for 12%

profile of v9, /device:TPU:1, one launch (start us, length us, event | category | flops | bytes accessed | tf_op | source)
XLA Modules:
  0.0 36.9 jit_solution(2225235722038715141)
XLA Ops:
  0.6 1.6 %pack.1 = (bf16[32,18,2,128]{3,2,1,0:T(2,128)(2,1)}, f32[8,128]{1,0:T(8,128)}) custom-call(bf16[34,256]{1,0:T(8,128)(2,1)} %taps_hbm.1, bf16[1,128]{1,0:T(2,128)(2,1)} %bitcast.22), custom_call_target="tpu_custom_call" | custom-call | tf_op jit(solution)/shard_map/pack/pallas_call | solution.py:269
  2.3 7.1 %all-to-all-start = ((bf16[32,18,2,128]{3,2,1,0:T(2,128)(2,1)}), bf16[32,18,2,128]{3,2,1,0:T(2,128)(2,1)S(1)}, u32[]{:S(2)}, u32[]{:S(2)}) async-start(bf16[32,18,2,128]{3,2,1,0:T(2,128)(2,1)} %get-tuple-element.13), calls=%async_computation | async-start | bytes 589824 | tf_op jit(solution)/shard_map/all_to_all | solution.py:285
  9.4 0.0 copy-start
  9.4 1.4 %slice_bitcast_fusion = (bf16[32,4096]{1,0:T(8,128)(2,1)S(1)}, bf16[32,4096]{1,0:T(8,128)(2,1)S(1)}, bf16[32,4096]{1,0:T(8,128)(2,1)S(1)}, bf16[32,4096]{1,0:T(8,128)(2,1)S(1)}) fusion(bf16[1,128,4096]{2,1,0:T(8,128)(2,1)} %param.8), kind=kLoop, calls=%fused_computation | loop fusion | bytes 2097152 | tf_op jit(solution)/shard_map/slice | solution.py:296
  10.8 0.3 collective-permute-start
  11.1 0.3 collective-permute-start.1
  11.3 0.3 collective-permute-start.2
  11.6 0.3 collective-permute-start.3
  12.5 0.0 collective-permute-done.refs_0_
  12.5 0.2 collective-permute-done.1.refs_1_
  12.7 0.4 %collective-permute-done.2.refs_2_ = bf16[32,4096]{1,0:T(8,128)(2,1)S(1)} collective-permute-done((bf16[32,4096]{1,0:T(8,128)(2,1)S(1)}, bf16[32,4096]{1,0:T(8,128)(2,1)S(1)}, u32[]{:S(2)}, u32[]{:S(2)}) %collective-permute-start.2) | collective-permute-done | bytes 262176 | tf_op jit(solution)/shard_map/ppermute | solution.py:296
  13.1 0.4 %collective-permute-done.3.refs_3_ = bf16[32,4096]{1,0:T(8,128)(2,1)S(1)} collective-permute-done((bf16[32,4096]{1,0:T(8,128)(2,1)S(1)}, bf16[32,4096]{1,0:T(8,128)(2,1)S(1)}, u32[]{:S(2)}, u32[]{:S(2)}) %collective-permute-start.3) | collective-permute-done | bytes 262176 | tf_op jit(solution)/shard_map/ppermute | solution.py:296
  13.5 0.2 source.1.source_ref._
  13.7 0.6 %copy-done.1 = bf16[1,8,4096]{2,1,0:T(8,128)(2,1)S(1)} copy-done((bf16[1,8,4096]{2,1,0:T(8,128)(2,1)S(1)}, bf16[1,8,4096]{2,1,0:T(8,128)(2,1)}, u32[]{:S(2)}) %copy-start.1) | copy-done | bytes 65560
  14.3 0.0 copy-done.2
  14.4 1.4 %collective-permute-start.4 = (bf16[8,4096]{1,0:T(8,128)(2,1)S(1)}, bf16[8,4096]{1,0:T(8,128)(2,1)S(1)}, u32[]{:S(2)}, u32[]{:S(2)}) collective-permute-start(bf16[8,4096]{1,0:T(8,128)(2,1)S(1)} %inputs.1.refs_0_.input_ref), channel_id=1, source_target_pairs={{0,8},{4,12},{8,16},{12,20},{16,24},{20,28},{24,0},{28,4},{1,9},{5... | collective-permute-start | bytes 196616 | tf_op jit(solution)/shard_map/ppermute | solution.py:328
  15.8 2.1 %collective-permute-start.5 = (bf16[8,4096]{1,0:T(8,128)(2,1)S(1)}, bf16[8,4096]{1,0:T(8,128)(2,1)S(1)}, u32[]{:S(2)}, u32[]{:S(2)}) collective-permute-start(bf16[8,4096]{1,0:T(8,128)(2,1)S(1)} %inputs.1.refs_0_.input_ref), channel_id=1, source_target_pairs={{0,16},{4,20},{8,24},{12,28},{16,0},{20,4},{24,8},{28,12},{1,17},{... | collective-permute-start | bytes 196616 | tf_op jit(solution)/shard_map/ppermute | solution.py:328
  18.0 1.1 %collective-permute-start.6 = (bf16[8,4096]{1,0:T(8,128)(2,1)S(1)}, bf16[8,4096]{1,0:T(8,128)(2,1)S(1)}, u32[]{:S(2)}, u32[]{:S(2)}) collective-permute-start(bf16[8,4096]{1,0:T(8,128)(2,1)S(1)} %inputs.1.refs_0_.input_ref), channel_id=1, source_target_pairs={{0,24},{4,28},{8,0},{12,4},{16,8},{20,12},{24,16},{28,20},{1,25},{... | collective-permute-start | bytes 196616 | tf_op jit(solution)/shard_map/ppermute | solution.py:328
  19.1 3.2 %all-to-all-done.taps_ref = bf16[32,18,2,128]{3,2,1,0:T(2,128)(2,1)S(1)} async-done(((bf16[32,18,2,128]{3,2,1,0:T(2,128)(2,1)}), bf16[32,18,2,128]{3,2,1,0:T(2,128)(2,1)S(1)}, u32[]{:S(2)}, u32[]{:S(2)}) %all-to-all-start) | async-done | bytes 294944 | tf_op jit(solution)/shard_map/all_to_all | solution.py:285
  22.3 3.0 %conv.1._ = bf16[8,8,2048]{2,1,0:T(8,128)(2,1)} custom-call(s32[1]{0:T(128)S(6)} %copy.10.len_ref, bf16[32,18,2,128]{3,2,1,0:T(2,128)(2,1)S(1)} %all-to-all-done.taps_ref, bf16[256,2048]{1,0:T(8,128)(2,1)S(1)} %source.1.source_ref._), custom_call_target="tpu_custom_call" | custom-call | tf_op jit(solution)/shard_map/conv/pallas_call | solution.py:329
  25.3 0.0 collective-permute-done.4.refs_1_
  25.3 0.0 collective-permute-done.5.refs_2_
  25.3 0.0 collective-permute-done.6.refs_3_
  25.3 3.4 %all-to-all-start.1 = ((bf16[8,8,2048]{2,1,0:T(8,128)(2,1)}), bf16[8,8,2048]{2,1,0:T(8,128)(2,1)S(1)}, u32[]{:S(2)}, u32[]{:S(2)}) async-start(bf16[8,8,2048]{2,1,0:T(8,128)(2,1)} %conv.1._), calls=%async_computation.1 | async-start | bytes 524288 | tf_op jit(solution)/shard_map/all_to_all | solution.py:340
  28.7 0.1 collective-permute-start.7
  28.8 0.5 %collective-permute-start.8 = (bf16[2,36,128]{2,1,0:T(8,128)(2,1)S(1)}, bf16[2,36,128]{2,1,0:T(8,128)(2,1)S(1)}, u32[]{:S(2)}, u32[]{:S(2)}) collective-permute-start(bf16[2,36,128]{2,1,0:T(8,128)(2,1)S(1)} %get-tuple-element.20.own_head_ref), channel_id=1, source_target_pairs={{0,4},{4,0},{8,12},{12,8},{16,20},{20,16},{24,28},{28,24},{1,5},{5... | collective-permute-start | bytes 55304 | tf_op jit(solution)/shard_map/ppermute | solution.py:360
  29.3 1.1 %collective-permute-done.8.peer_head_ref = bf16[2,36,128]{2,1,0:T(8,128)(2,1)S(1)} collective-permute-done((bf16[2,36,128]{2,1,0:T(8,128)(2,1)S(1)}, bf16[2,36,128]{2,1,0:T(8,128)(2,1)S(1)}, u32[]{:S(2)}, u32[]{:S(2)}) %collective-permute-start.8) | collective-permute-done | bytes 18464 | tf_op jit(solution)/shard_map/ppermute | solution.py:360
  30.3 0.0 collective-permute-done.7.peer_stack_ref
  30.3 0.7 %copy-done.4 = s32[1,8,1]{1,2,0:T(1,128)S(1)} copy-done((s32[1,8,1]{1,2,0:T(1,128)S(1)}, s32[1,8,1]{1,2,0:T(1,128)}, u32[]{:S(2)}) %copy-start.4) | copy-done | bytes 56
  31.0 1.3 %span.1 = (f32[8,4096]{1,0:T(8,128)S(1)}, bf16[2,8,4096]{2,1,0:T(8,128)(2,1)}) custom-call(s32[8]{0:T(128)S(1)} %bitcast.20, bf16[4,8,4096]{2,1,0:T(8,128)(2,1)S(1)} %get-tuple-element.19.own_stack_ref, bf16[4,8,4096]{2,1,0:T(8,128)(2,1)S(1)} %collective-permute-done.7.peer_stack_ref, bf16[2,36,128]{2,1,0:T(8,128)(2,1)S(1)} %get-tuple-element.20.own_head_ref, ...), custom_call_target="tpu_custom_call" | custom-call | tf_op jit(solution)/shard_map/span/pallas_call | solution.py:362
  32.3 3.9 %all-to-all-done.1.parts_ref = bf16[8,8,2048]{2,1,0:T(8,128)(2,1)S(1)} async-done(((bf16[8,8,2048]{2,1,0:T(8,128)(2,1)}), bf16[8,8,2048]{2,1,0:T(8,128)(2,1)S(1)}, u32[]{:S(2)}, u32[]{:S(2)}) %all-to-all-start.1) | async-done | bytes 262176 | tf_op jit(solution)/shard_map/all_to_all | solution.py:340
  36.2 0.7 %finish.1 = bf16[8,4096]{1,0:T(8,128)(2,1)} custom-call(bf16[8,8,2048]{2,1,0:T(8,128)(2,1)S(1)} %all-to-all-done.1.parts_ref, bf16[8,4096]{1,0:T(8,128)(2,1)S(1)} %bitcast.19, f32[8,4096]{1,0:T(8,128)S(1)} %get-tuple-element.22.extra_ref), custom_call_target="tpu_custom_call" | custom-call | tf_op jit(solution)/shard_map/finish/pallas_call | solution.py:378
  (8 shorter events, 0.1 us)
Async XLA Ops:
  2.3 20.0 %all-to-all-start = ((bf16[32,18,2,128]{3,2,1,0:T(2,128)(2,1)}), bf16[32,18,2,128]{3,2,1,0:T(2,128)(2,1)S(1)}, u32[]{:S(2)}, u32[]{:S(2)}) async-start(bf16[32,18,2,128]{3,2,1,0:T(2,128)(2,1)} %get-tuple-element.13), calls=%async_computation | async-start | bytes 589824 | tf_op jit(solution)/shard_map/all_to_all | solution.py:285
  9.4 4.1 %copy-start = (bf16[1,128,4096]{2,1,0:T(8,128)(2,1)S(1)}, bf16[1,128,4096]{2,1,0:T(8,128)(2,1)}, u32[]{:S(2)}) copy-start(bf16[1,128,4096]{2,1,0:T(8,128)(2,1)} %param.8) | copy-start | bytes 3145732
  10.8 1.7 %collective-permute-start = (bf16[32,4096]{1,0:T(8,128)(2,1)S(1)}, bf16[32,4096]{1,0:T(8,128)(2,1)S(1)}, u32[]{:S(2)}, u32[]{:S(2)}) collective-permute-start(bf16[32,4096]{1,0:T(8,128)(2,1)S(1)} %get-tuple-element.26), channel_id=1, source_target_pairs={{0,4},{4,0},{8,12},{12,8},{16,20},{20,16},{24,28},{28,24},{1,5},{5... | collective-permute-start | bytes 786440 | tf_op jit(solution)/shard_map/ppermute | solution.py:296
  11.1 1.7 %collective-permute-start.1 = (bf16[32,4096]{1,0:T(8,128)(2,1)S(1)}, bf16[32,4096]{1,0:T(8,128)(2,1)S(1)}, u32[]{:S(2)}, u32[]{:S(2)}) collective-permute-start(bf16[32,4096]{1,0:T(8,128)(2,1)S(1)} %get-tuple-element.25), channel_id=1, source_target_pairs={{0,4},{4,0},{8,12},{12,8},{16,20},{20,16},{24,28},{28,24},{1,5},{5... | collective-permute-start | bytes 786440 | tf_op jit(solution)/shard_map/ppermute | solution.py:296
  11.3 1.8 %collective-permute-start.2 = (bf16[32,4096]{1,0:T(8,128)(2,1)S(1)}, bf16[32,4096]{1,0:T(8,128)(2,1)S(1)}, u32[]{:S(2)}, u32[]{:S(2)}) collective-permute-start(bf16[32,4096]{1,0:T(8,128)(2,1)S(1)} %get-tuple-element.27), channel_id=1, source_target_pairs={{0,4},{4,0},{8,12},{12,8},{16,20},{20,16},{24,28},{28,24},{1,5},{5... | collective-permute-start | bytes 786440 | tf_op jit(solution)/shard_map/ppermute | solution.py:296
  11.6 1.9 %collective-permute-start.3 = (bf16[32,4096]{1,0:T(8,128)(2,1)S(1)}, bf16[32,4096]{1,0:T(8,128)(2,1)S(1)}, u32[]{:S(2)}, u32[]{:S(2)}) collective-permute-start(bf16[32,4096]{1,0:T(8,128)(2,1)S(1)} %get-tuple-element.24), channel_id=1, source_target_pairs={{0,4},{4,0},{8,12},{12,8},{16,20},{20,16},{24,28},{28,24},{1,5},{5... | collective-permute-start | bytes 786440 | tf_op jit(solution)/shard_map/ppermute | solution.py:296
  13.5 0.8 %copy-start.1 = (bf16[1,8,4096]{2,1,0:T(8,128)(2,1)S(1)}, bf16[1,8,4096]{2,1,0:T(8,128)(2,1)}, u32[]{:S(2)}) copy-start(bf16[1,8,4096]{2,1,0:T(8,128)(2,1)} %param.10) | copy-start | bytes 196612
  13.5 0.9 %copy-start.2 = (bf16[1,8,4096]{2,1,0:T(8,128)(2,1)S(1)}, bf16[1,8,4096]{2,1,0:T(8,128)(2,1)}, u32[]{:S(2)}) copy-start(bf16[1,8,4096]{2,1,0:T(8,128)(2,1)} %param.11) | copy-start | bytes 196612
  14.4 10.9 %collective-permute-start.4 = (bf16[8,4096]{1,0:T(8,128)(2,1)S(1)}, bf16[8,4096]{1,0:T(8,128)(2,1)S(1)}, u32[]{:S(2)}, u32[]{:S(2)}) collective-permute-start(bf16[8,4096]{1,0:T(8,128)(2,1)S(1)} %inputs.1.refs_0_.input_ref), channel_id=1, source_target_pairs={{0,8},{4,12},{8,16},{12,20},{16,24},{20,28},{24,0},{28,4},{1,9},{5... | collective-permute-start | bytes 196616 | tf_op jit(solution)/shard_map/ppermute | solution.py:328
  15.8 9.4 %collective-permute-start.5 = (bf16[8,4096]{1,0:T(8,128)(2,1)S(1)}, bf16[8,4096]{1,0:T(8,128)(2,1)S(1)}, u32[]{:S(2)}, u32[]{:S(2)}) collective-permute-start(bf16[8,4096]{1,0:T(8,128)(2,1)S(1)} %inputs.1.refs_0_.input_ref), channel_id=1, source_target_pairs={{0,16},{4,20},{8,24},{12,28},{16,0},{20,4},{24,8},{28,12},{1,17},{... | collective-permute-start | bytes 196616 | tf_op jit(solution)/shard_map/ppermute | solution.py:328
  18.0 7.3 %collective-permute-start.6 = (bf16[8,4096]{1,0:T(8,128)(2,1)S(1)}, bf16[8,4096]{1,0:T(8,128)(2,1)S(1)}, u32[]{:S(2)}, u32[]{:S(2)}) collective-permute-start(bf16[8,4096]{1,0:T(8,128)(2,1)S(1)} %inputs.1.refs_0_.input_ref), channel_id=1, source_target_pairs={{0,24},{4,28},{8,0},{12,4},{16,8},{20,12},{24,16},{28,20},{1,25},{... | collective-permute-start | bytes 196616 | tf_op jit(solution)/shard_map/ppermute | solution.py:328
  25.3 10.9 %all-to-all-start.1 = ((bf16[8,8,2048]{2,1,0:T(8,128)(2,1)}), bf16[8,8,2048]{2,1,0:T(8,128)(2,1)S(1)}, u32[]{:S(2)}, u32[]{:S(2)}) async-start(bf16[8,8,2048]{2,1,0:T(8,128)(2,1)} %conv.1._), calls=%async_computation.1 | async-start | bytes 524288 | tf_op jit(solution)/shard_map/all_to_all | solution.py:340
  28.7 1.6 %collective-permute-start.7 = (bf16[4,8,4096]{2,1,0:T(8,128)(2,1)S(1)}, bf16[4,8,4096]{2,1,0:T(8,128)(2,1)S(1)}, u32[]{:S(2)}, u32[]{:S(2)}) collective-permute-start(bf16[4,8,4096]{2,1,0:T(8,128)(2,1)S(1)} %get-tuple-element.19.own_stack_ref), channel_id=1, source_target_pairs={{0,4},{4,0},{8,12},{12,8},{16,20},{20,16},{24,28},{28,24},{1,5},{5... | collective-permute-start | bytes 786440 | tf_op jit(solution)/shard_map/ppermute | solution.py:359
  28.8 1.6 %collective-permute-start.8 = (bf16[2,36,128]{2,1,0:T(8,128)(2,1)S(1)}, bf16[2,36,128]{2,1,0:T(8,128)(2,1)S(1)}, u32[]{:S(2)}, u32[]{:S(2)}) collective-permute-start(bf16[2,36,128]{2,1,0:T(8,128)(2,1)S(1)} %get-tuple-element.20.own_head_ref), channel_id=1, source_target_pairs={{0,4},{4,0},{8,12},{12,8},{16,20},{20,16},{24,28},{28,24},{1,5},{5... | collective-permute-start | bytes 55304 | tf_op jit(solution)/shard_map/ppermute | solution.py:360
  30.3 0.7 %copy-start.4 = (s32[1,8,1]{1,2,0:T(1,128)S(1)}, s32[1,8,1]{1,2,0:T(1,128)}, u32[]{:S(2)}) copy-start(s32[1,8,1]{1,2,0:T(1,128)} %param.15) | copy-start | bytes 100
  31.0 5.2 %copy-start.3 = (bf16[1,8,4096]{2,1,0:T(8,128)(2,1)S(1)}, bf16[1,8,4096]{2,1,0:T(8,128)(2,1)}, u32[]{:S(2)}) copy-start(bf16[1,8,4096]{2,1,0:T(8,128)(2,1)} %param.9) | copy-start | bytes 196612

commit v10 on v9

--- a/solution.py
+++ b/solution.py
@@ -25,7 +25,7 @@
 
 
 def part_order(n_blk):
-    return [2 * chip + core for chip in middle_out(n_blk // 2) for core in (1, 0)]
+    return [2 * chip + core for core in (1, 0) for chip in middle_out(n_blk // 2)[::-1]]
 
 
 def tap_order(n_blk, n_ten):
@@ -33,7 +33,7 @@
     chips = chips[len(chips) // 2 :] + chips[: len(chips) // 2]
     return [
         (2 * chip + core) * n_ten + tenant
-        for core in range(2)
+        for core in (1, 0)
         for chip in chips
         for tenant in range(n_ten)
     ]
@@ -45,8 +45,8 @@
     core, chip = lax.rem(block, 2), lax.div(block, 2)
     place = jnp.int32(0)
     for each in range(n_blk // 2):
-        place = jnp.where(chip == each, order.index(2 * each * n_ten), place)
-    return place + core * (len(order) // 2) + tenant
+        place = jnp.where(chip == each, order.index((2 * each + 1) * n_ten), place)
+    return place + (1 - core) * (len(order) // 2) + tenant
 
 
 def pack_kernel(order, n_ten, taps_hbm, bias_hbm, send_ref, token_ref, *scratch):
@@ -165,9 +165,8 @@
 def gather_kernel(order, fr, bias_width, _, taps_ref, *refs):
     pages, (stack_ref, head_ref, bias_ref) = refs[:-3], refs[-3:]
     chip = lax.div(lax.axis_index("blk"), 2)
-    n_chip = len(pages)
     for step, page in enumerate(pages):
-        stack_ref[lax.rem(chip + n_chip - step, n_chip)] = page[...]
+        stack_ref[lax.bitwise_xor(chip, step)] = page[...]
     for index in range(head_ref.shape[0]):
         head_ref[index] = taps_ref[order.index(index)].reshape(head_ref.shape[1:])
     each = LANES // bias_width
@@ -324,7 +323,7 @@
 
     pages = [inputs]
     for step in range(1, n_chip):
-        turn = [(i, (i + 2 * step) % n_blk) for i in range(n_blk)]
+        turn = [(i, i ^ (2 * step)) for i in range(n_blk)]
         pages.append(lax.ppermute(inputs, "blk", turn))
     partial = pl.pallas_call(
         functools.partial(conv_kernel, fr, n_ten, gsize),

time: 37.3 us -> 36.7 us (0.984)
  the two profiles are of different devices: /device:TPU:1 before, /device:TPU:0 now
where the time goes in v10:
time: 36.7 us; the launch traced here: 36.2 us
  starting transfers between devices  18.3 us (50%)
  waiting for transfers between devices  7.05 us (19%)
  Pallas kernels  6.86 us (19%)
  local copies, waits for them, and re-layouts  2.7 us (7%)
  between operations  1.35 us (4%)
    all_to_all x1, starting transfers between devices, per_device(): lax.all_to_all(send, ('blk', 'tenant'), split_axis=0, concat_axis=0, axis...  7.3 us
    all_to_all x1, starting transfers between devices, per_device(): lax.all_to_all(partial, 'blk', split_axis=0, concat_axis=0, axis_index_gr...  4.85 us
    ppermute x3, starting transfers between devices, per_device(): pages.append(lax.ppermute(inputs, 'blk', turn))  4.45 us
    pallas_call x1, Pallas kernels, per_device(): pl.pallas_call(functools.partial(conv_kernel, fr, n_ten, gsize), out_shap...  2.97 us
    all_to_all x1, waiting for transfers between devices, per_device(): lax.all_to_all(partial, 'blk', split_axis=0, concat_axis=0, axis_index_gr...  2.03 us
    ppermute x3, waiting for transfers between devices, per_device(): pages.append(lax.ppermute(inputs, 'blk', turn))  1.82 us
    pallas_call x1, Pallas kernels, per_device(): pl.pallas_call(functools.partial(pack_kernel, tap_order(n_blk, n_ten), n_...  1.64 us
    slice x1, local copies, waits for them, and re-layouts, per_device(): history[i * piece:(i + 1) * piece]  1.36 us
  transfers between devices with their start and end apart: 11, of which 8 were waited for; matrix products, arithmetic and copies ran while one was open for 4% of the time, Pallas kernels for 13%

profile of v10, /device:TPU:0, one launch (start us, length us, event | category | flops | bytes accessed | tf_op | source)
XLA Modules:
  0.0 36.2 jit_solution(6026675196641311931)
XLA Ops:
  0.6 1.6 %pack.1 = (bf16[32,18,2,128]{3,2,1,0:T(2,128)(2,1)}, f32[8,128]{1,0:T(8,128)}) custom-call(bf16[34,256]{1,0:T(8,128)(2,1)} %taps_hbm.1, bf16[1,128]{1,0:T(2,128)(2,1)} %bitcast.22), custom_call_target="tpu_custom_call" | custom-call | tf_op jit(solution)/shard_map/pack/pallas_call | solution.py:268
  2.3 7.3 %all-to-all-start = ((bf16[32,18,2,128]{3,2,1,0:T(2,128)(2,1)}), bf16[32,18,2,128]{3,2,1,0:T(2,128)(2,1)S(1)}, u32[]{:S(2)}, u32[]{:S(2)}) async-start(bf16[32,18,2,128]{3,2,1,0:T(2,128)(2,1)} %get-tuple-element.13), calls=%async_computation | async-start | bytes 589824 | tf_op jit(solution)/shard_map/all_to_all | solution.py:284
  9.6 0.0 copy-start
  9.6 1.4 %slice_bitcast_fusion = (bf16[32,4096]{1,0:T(8,128)(2,1)S(1)}, bf16[32,4096]{1,0:T(8,128)(2,1)S(1)}, bf16[32,4096]{1,0:T(8,128)(2,1)S(1)}, bf16[32,4096]{1,0:T(8,128)(2,1)S(1)}) fusion(bf16[1,128,4096]{2,1,0:T(8,128)(2,1)} %param.8), kind=kLoop, calls=%fused_computation | loop fusion | bytes 2097152 | tf_op jit(solution)/shard_map/slice | solution.py:295
  11.0 0.3 collective-permute-start
  11.3 0.3 collective-permute-start.1
  11.5 0.3 collective-permute-start.2
  11.8 0.3 collective-permute-start.3
  12.7 0.0 collective-permute-done.refs_0_
  12.7 0.2 collective-permute-done.1.refs_1_
  12.9 0.4 %collective-permute-done.2.refs_2_ = bf16[32,4096]{1,0:T(8,128)(2,1)S(1)} collective-permute-done((bf16[32,4096]{1,0:T(8,128)(2,1)S(1)}, bf16[32,4096]{1,0:T(8,128)(2,1)S(1)}, u32[]{:S(2)}, u32[]{:S(2)}) %collective-permute-start.2) | collective-permute-done | bytes 262176 | tf_op jit(solution)/shard_map/ppermute | solution.py:295
  13.3 0.4 %collective-permute-done.3.refs_3_ = bf16[32,4096]{1,0:T(8,128)(2,1)S(1)} collective-permute-done((bf16[32,4096]{1,0:T(8,128)(2,1)S(1)}, bf16[32,4096]{1,0:T(8,128)(2,1)S(1)}, u32[]{:S(2)}, u32[]{:S(2)}) %collective-permute-start.3) | collective-permute-done | bytes 262176 | tf_op jit(solution)/shard_map/ppermute | solution.py:295
  13.7 0.2 source.1.source_ref._
  13.9 0.6 %copy-done.1 = bf16[1,8,4096]{2,1,0:T(8,128)(2,1)S(1)} copy-done((bf16[1,8,4096]{2,1,0:T(8,128)(2,1)S(1)}, bf16[1,8,4096]{2,1,0:T(8,128)(2,1)}, u32[]{:S(2)}) %copy-start.1) | copy-done | bytes 65560
  14.5 0.0 copy-done.2
  14.6 1.8 %collective-permute-start.4 = (bf16[8,4096]{1,0:T(8,128)(2,1)S(1)}, bf16[8,4096]{1,0:T(8,128)(2,1)S(1)}, u32[]{:S(2)}, u32[]{:S(2)}) collective-permute-start(bf16[8,4096]{1,0:T(8,128)(2,1)S(1)} %inputs.1.refs_0_.input_ref), channel_id=1, source_target_pairs={{0,8},{4,12},{8,0},{12,4},{16,24},{20,28},{24,16},{28,20},{1,9},{5... | collective-permute-start | bytes 196616 | tf_op jit(solution)/shard_map/ppermute | solution.py:327
  16.4 2.4 %collective-permute-start.5 = (bf16[8,4096]{1,0:T(8,128)(2,1)S(1)}, bf16[8,4096]{1,0:T(8,128)(2,1)S(1)}, u32[]{:S(2)}, u32[]{:S(2)}) collective-permute-start(bf16[8,4096]{1,0:T(8,128)(2,1)S(1)} %inputs.1.refs_0_.input_ref), channel_id=1, source_target_pairs={{0,16},{4,20},{8,24},{12,28},{16,0},{20,4},{24,8},{28,12},{1,17},{... | collective-permute-start | bytes 196616 | tf_op jit(solution)/shard_map/ppermute | solution.py:327
  18.8 0.2 collective-permute-start.6
  19.0 1.2 %all-to-all-done.taps_ref = bf16[32,18,2,128]{3,2,1,0:T(2,128)(2,1)S(1)} async-done(((bf16[32,18,2,128]{3,2,1,0:T(2,128)(2,1)}), bf16[32,18,2,128]{3,2,1,0:T(2,128)(2,1)S(1)}, u32[]{:S(2)}, u32[]{:S(2)}) %all-to-all-start) | async-done | bytes 294944 | tf_op jit(solution)/shard_map/all_to_all | solution.py:284
  20.2 3.0 %conv.1._ = bf16[8,8,2048]{2,1,0:T(8,128)(2,1)} custom-call(s32[1]{0:T(128)S(6)} %copy.10.len_ref, bf16[32,18,2,128]{3,2,1,0:T(2,128)(2,1)S(1)} %all-to-all-done.taps_ref, bf16[256,2048]{1,0:T(8,128)(2,1)S(1)} %source.1.source_ref._), custom_call_target="tpu_custom_call" | custom-call | tf_op jit(solution)/shard_map/conv/pallas_call | solution.py:328
  23.2 0.0 collective-permute-done.4.refs_1_
  23.2 0.8 %collective-permute-done.5.refs_2_ = bf16[8,4096]{1,0:T(8,128)(2,1)S(1)} collective-permute-done((bf16[8,4096]{1,0:T(8,128)(2,1)S(1)}, bf16[8,4096]{1,0:T(8,128)(2,1)S(1)}, u32[]{:S(2)}, u32[]{:S(2)}) %collective-permute-start.5) | collective-permute-done | bytes 65568 | tf_op jit(solution)/shard_map/ppermute | solution.py:327
  24.0 1.0 %collective-permute-done.6.refs_3_ = bf16[8,4096]{1,0:T(8,128)(2,1)S(1)} collective-permute-done((bf16[8,4096]{1,0:T(8,128)(2,1)S(1)}, bf16[8,4096]{1,0:T(8,128)(2,1)S(1)}, u32[]{:S(2)}, u32[]{:S(2)}) %collective-permute-start.6) | collective-permute-done | bytes 65568 | tf_op jit(solution)/shard_map/ppermute | solution.py:327
  25.0 4.8 %all-to-all-start.1 = ((bf16[8,8,2048]{2,1,0:T(8,128)(2,1)}), bf16[8,8,2048]{2,1,0:T(8,128)(2,1)S(1)}, u32[]{:S(2)}, u32[]{:S(2)}) async-start(bf16[8,8,2048]{2,1,0:T(8,128)(2,1)} %conv.1._), calls=%async_computation.1 | async-start | bytes 524288 | tf_op jit(solution)/shard_map/all_to_all | solution.py:339
  29.9 0.1 collective-permute-start.7
  30.1 0.4 %collective-permute-start.8 = (bf16[2,36,128]{2,1,0:T(8,128)(2,1)S(1)}, bf16[2,36,128]{2,1,0:T(8,128)(2,1)S(1)}, u32[]{:S(2)}, u32[]{:S(2)}) collective-permute-start(bf16[2,36,128]{2,1,0:T(8,128)(2,1)S(1)} %get-tuple-element.20.own_head_ref), channel_id=1, source_target_pairs={{0,4},{4,0},{8,12},{12,8},{16,20},{20,16},{24,28},{28,24},{1,5},{5... | collective-permute-start | bytes 55304 | tf_op jit(solution)/shard_map/ppermute | solution.py:359
  30.5 1.1 %collective-permute-done.8.peer_head_ref = bf16[2,36,128]{2,1,0:T(8,128)(2,1)S(1)} collective-permute-done((bf16[2,36,128]{2,1,0:T(8,128)(2,1)S(1)}, bf16[2,36,128]{2,1,0:T(8,128)(2,1)S(1)}, u32[]{:S(2)}, u32[]{:S(2)}) %collective-permute-start.8) | collective-permute-done | bytes 18464 | tf_op jit(solution)/shard_map/ppermute | solution.py:359
  31.5 0.0 collective-permute-done.7.peer_stack_ref
  31.5 0.7 %copy-done.4 = s32[1,8,1]{1,2,0:T(1,128)S(1)} copy-done((s32[1,8,1]{1,2,0:T(1,128)S(1)}, s32[1,8,1]{1,2,0:T(1,128)}, u32[]{:S(2)}) %copy-start.4) | copy-done | bytes 56
  32.2 1.3 %span.1 = (f32[8,4096]{1,0:T(8,128)S(1)}, bf16[2,8,4096]{2,1,0:T(8,128)(2,1)}) custom-call(s32[8]{0:T(128)S(1)} %bitcast.20, bf16[4,8,4096]{2,1,0:T(8,128)(2,1)S(1)} %get-tuple-element.19.own_stack_ref, bf16[4,8,4096]{2,1,0:T(8,128)(2,1)S(1)} %collective-permute-done.7.peer_stack_ref, bf16[2,36,128]{2,1,0:T(8,128)(2,1)S(1)} %get-tuple-element.20.own_head_ref, ...), custom_call_target="tpu_custom_call" | custom-call | tf_op jit(solution)/shard_map/span/pallas_call | solution.py:361
  33.5 2.0 %all-to-all-done.1.parts_ref = bf16[8,8,2048]{2,1,0:T(8,128)(2,1)S(1)} async-done(((bf16[8,8,2048]{2,1,0:T(8,128)(2,1)}), bf16[8,8,2048]{2,1,0:T(8,128)(2,1)S(1)}, u32[]{:S(2)}, u32[]{:S(2)}) %all-to-all-start.1) | async-done | bytes 262176 | tf_op jit(solution)/shard_map/all_to_all | solution.py:339
  35.5 0.7 %finish.1 = bf16[8,4096]{1,0:T(8,128)(2,1)} custom-call(bf16[8,8,2048]{2,1,0:T(8,128)(2,1)S(1)} %all-to-all-done.1.parts_ref, bf16[8,4096]{1,0:T(8,128)(2,1)S(1)} %bitcast.19, f32[8,4096]{1,0:T(8,128)S(1)} %get-tuple-element.22.extra_ref), custom_call_target="tpu_custom_call" | custom-call | tf_op jit(solution)/shard_map/finish/pallas_call | solution.py:377
  (8 shorter events, 0.1 us)
Async XLA Ops:
  2.3 17.9 %all-to-all-start = ((bf16[32,18,2,128]{3,2,1,0:T(2,128)(2,1)}), bf16[32,18,2,128]{3,2,1,0:T(2,128)(2,1)S(1)}, u32[]{:S(2)}, u32[]{:S(2)}) async-start(bf16[32,18,2,128]{3,2,1,0:T(2,128)(2,1)} %get-tuple-element.13), calls=%async_computation | async-start | bytes 589824 | tf_op jit(solution)/shard_map/all_to_all | solution.py:284
  9.6 4.1 %copy-start = (bf16[1,128,4096]{2,1,0:T(8,128)(2,1)S(1)}, bf16[1,128,4096]{2,1,0:T(8,128)(2,1)}, u32[]{:S(2)}) copy-start(bf16[1,128,4096]{2,1,0:T(8,128)(2,1)} %param.8) | copy-start | bytes 3145732
  11.0 1.7 %collective-permute-start = (bf16[32,4096]{1,0:T(8,128)(2,1)S(1)}, bf16[32,4096]{1,0:T(8,128)(2,1)S(1)}, u32[]{:S(2)}, u32[]{:S(2)}) collective-permute-start(bf16[32,4096]{1,0:T(8,128)(2,1)S(1)} %get-tuple-element.26), channel_id=1, source_target_pairs={{0,4},{4,0},{8,12},{12,8},{16,20},{20,16},{24,28},{28,24},{1,5},{5... | collective-permute-start | bytes 786440 | tf_op jit(solution)/shard_map/ppermute | solution.py:295
  11.3 1.7 %collective-permute-start.1 = (bf16[32,4096]{1,0:T(8,128)(2,1)S(1)}, bf16[32,4096]{1,0:T(8,128)(2,1)S(1)}, u32[]{:S(2)}, u32[]{:S(2)}) collective-permute-start(bf16[32,4096]{1,0:T(8,128)(2,1)S(1)} %get-tuple-element.25), channel_id=1, source_target_pairs={{0,4},{4,0},{8,12},{12,8},{16,20},{20,16},{24,28},{28,24},{1,5},{5... | collective-permute-start | bytes 786440 | tf_op jit(solution)/shard_map/ppermute | solution.py:295
  11.5 1.8 %collective-permute-start.2 = (bf16[32,4096]{1,0:T(8,128)(2,1)S(1)}, bf16[32,4096]{1,0:T(8,128)(2,1)S(1)}, u32[]{:S(2)}, u32[]{:S(2)}) collective-permute-start(bf16[32,4096]{1,0:T(8,128)(2,1)S(1)} %get-tuple-element.27), channel_id=1, source_target_pairs={{0,4},{4,0},{8,12},{12,8},{16,20},{20,16},{24,28},{28,24},{1,5},{5... | collective-permute-start | bytes 786440 | tf_op jit(solution)/shard_map/ppermute | solution.py:295
  11.8 1.9 %collective-permute-start.3 = (bf16[32,4096]{1,0:T(8,128)(2,1)S(1)}, bf16[32,4096]{1,0:T(8,128)(2,1)S(1)}, u32[]{:S(2)}, u32[]{:S(2)}) collective-permute-start(bf16[32,4096]{1,0:T(8,128)(2,1)S(1)} %get-tuple-element.24), channel_id=1, source_target_pairs={{0,4},{4,0},{8,12},{12,8},{16,20},{20,16},{24,28},{28,24},{1,5},{5... | collective-permute-start | bytes 786440 | tf_op jit(solution)/shard_map/ppermute | solution.py:295
  13.7 0.8 %copy-start.1 = (bf16[1,8,4096]{2,1,0:T(8,128)(2,1)S(1)}, bf16[1,8,4096]{2,1,0:T(8,128)(2,1)}, u32[]{:S(2)}) copy-start(bf16[1,8,4096]{2,1,0:T(8,128)(2,1)} %param.10) | copy-start | bytes 196612
  13.7 0.9 %copy-start.2 = (bf16[1,8,4096]{2,1,0:T(8,128)(2,1)S(1)}, bf16[1,8,4096]{2,1,0:T(8,128)(2,1)}, u32[]{:S(2)}) copy-start(bf16[1,8,4096]{2,1,0:T(8,128)(2,1)} %param.11) | copy-start | bytes 196612
  14.6 8.6 %collective-permute-start.4 = (bf16[8,4096]{1,0:T(8,128)(2,1)S(1)}, bf16[8,4096]{1,0:T(8,128)(2,1)S(1)}, u32[]{:S(2)}, u32[]{:S(2)}) collective-permute-start(bf16[8,4096]{1,0:T(8,128)(2,1)S(1)} %inputs.1.refs_0_.input_ref), channel_id=1, source_target_pairs={{0,8},{4,12},{8,0},{12,4},{16,24},{20,28},{24,16},{28,20},{1,9},{5... | collective-permute-start | bytes 196616 | tf_op jit(solution)/shard_map/ppermute | solution.py:327
  16.4 7.5 %collective-permute-start.5 = (bf16[8,4096]{1,0:T(8,128)(2,1)S(1)}, bf16[8,4096]{1,0:T(8,128)(2,1)S(1)}, u32[]{:S(2)}, u32[]{:S(2)}) collective-permute-start(bf16[8,4096]{1,0:T(8,128)(2,1)S(1)} %inputs.1.refs_0_.input_ref), channel_id=1, source_target_pairs={{0,16},{4,20},{8,24},{12,28},{16,0},{20,4},{24,8},{28,12},{1,17},{... | collective-permute-start | bytes 196616 | tf_op jit(solution)/shard_map/ppermute | solution.py:327
  18.8 6.2 %collective-permute-start.6 = (bf16[8,4096]{1,0:T(8,128)(2,1)S(1)}, bf16[8,4096]{1,0:T(8,128)(2,1)S(1)}, u32[]{:S(2)}, u32[]{:S(2)}) collective-permute-start(bf16[8,4096]{1,0:T(8,128)(2,1)S(1)} %inputs.1.refs_0_.input_ref), channel_id=1, source_target_pairs={{0,24},{4,28},{8,16},{12,20},{16,8},{20,12},{24,0},{28,4},{1,25},{... | collective-permute-start | bytes 196616 | tf_op jit(solution)/shard_map/ppermute | solution.py:327
  25.0 10.5 %all-to-all-start.1 = ((bf16[8,8,2048]{2,1,0:T(8,128)(2,1)}), bf16[8,8,2048]{2,1,0:T(8,128)(2,1)S(1)}, u32[]{:S(2)}, u32[]{:S(2)}) async-start(bf16[8,8,2048]{2,1,0:T(8,128)(2,1)} %conv.1._), calls=%async_computation.1 | async-start | bytes 524288 | tf_op jit(solution)/shard_map/all_to_all | solution.py:339
  29.9 1.6 %collective-permute-start.7 = (bf16[4,8,4096]{2,1,0:T(8,128)(2,1)S(1)}, bf16[4,8,4096]{2,1,0:T(8,128)(2,1)S(1)}, u32[]{:S(2)}, u32[]{:S(2)}) collective-permute-start(bf16[4,8,4096]{2,1,0:T(8,128)(2,1)S(1)} %get-tuple-element.19.own_stack_ref), channel_id=1, source_target_pairs={{0,4},{4,0},{8,12},{12,8},{16,20},{20,16},{24,28},{28,24},{1,5},{5... | collective-permute-start | bytes 786440 | tf_op jit(solution)/shard_map/ppermute | solution.py:358
  30.1 1.5 %collective-permute-start.8 = (bf16[2,36,128]{2,1,0:T(8,128)(2,1)S(1)}, bf16[2,36,128]{2,1,0:T(8,128)(2,1)S(1)}, u32[]{:S(2)}, u32[]{:S(2)}) collective-permute-start(bf16[2,36,128]{2,1,0:T(8,128)(2,1)S(1)} %get-tuple-element.20.own_head_ref), channel_id=1, source_target_pairs={{0,4},{4,0},{8,12},{12,8},{16,20},{20,16},{24,28},{28,24},{1,5},{5... | collective-permute-start | bytes 55304 | tf_op jit(solution)/shard_map/ppermute | solution.py:359
  31.5 0.7 %copy-start.4 = (s32[1,8,1]{1,2,0:T(1,128)S(1)}, s32[1,8,1]{1,2,0:T(1,128)}, u32[]{:S(2)}) copy-start(s32[1,8,1]{1,2,0:T(1,128)} %param.15) | copy-start | bytes 100
  32.2 3.4 %copy-start.3 = (bf16[1,8,4096]{2,1,0:T(8,128)(2,1)S(1)}, bf16[1,8,4096]{2,1,0:T(8,128)(2,1)}, u32[]{:S(2)}) copy-start(bf16[1,8,4096]{2,1,0:T(8,128)(2,1)} %param.9) | copy-start | bytes 196612

commit v11 on v10

--- a/solution.py
+++ b/solution.py
@@ -10,6 +10,7 @@
 PAGE = 8
 MOST = 2
 LANES = 128
+OUT_COPIES = 4
 
 bf16 = jnp.bfloat16
 f32 = jnp.float32
@@ -136,7 +137,7 @@
     return total
 
 
-def conv_kernel(fr, n_ten, gsize, len_ref, taps_ref, source_ref, out_ref, line_ref):
+def conv_kernel(fr, n_ten, gsize, len_ref, taps_ref, source_ref, out_hbm, line_ref, out_ref, sems):
     n_dev, pairs, _, groups = taps_ref.shape
     n_blk, page, _ = out_ref.shape
     span = n_blk * page
@@ -153,6 +154,7 @@
         jnp.stack(window), first, fr, base + span - 1, line_ref.shape[1]
     )
     per = LANES // gsize
+    every, copies = groups // per // OUT_COPIES, []
     for index in range(groups // per):
         columns = slice(index * LANES, (index + 1) * LANES)
         total = toeplitz_product(
@@ -160,6 +162,16 @@
         )
         for place, block in enumerate(part_order(n_blk)):
             out_ref[place, :, columns] = total[block * page : (block + 1) * page].astype(bf16)
+        if (index + 1) % every == 0:
+            done = slice((index + 1 - every) * LANES, (index + 1) * LANES)
+            copies.append(
+                pltpu.make_async_copy(
+                    out_ref.at[:, :, done], out_hbm.at[:, :, done], sems.at[len(copies)]
+                )
+            )
+            copies[-1].start()
+    for copy in copies:
+        copy.wait()
 
 
 def gather_kernel(order, fr, bias_width, _, taps_ref, *refs):
@@ -329,8 +341,12 @@
         functools.partial(conv_kernel, fr, n_ten, gsize),
         out_shape=jax.ShapeDtypeStruct((n_blk, span_rows, half), bf16),
         in_specs=[whole(pltpu.SMEM), whole(), whole()],
-        out_specs=whole(),
-        scratch_shapes=[pltpu.VMEM((groups // 2, round_up(2 * rows + span - 1, LANES)), f32)],
+        out_specs=whole(pltpu.HBM),
+        scratch_shapes=[
+            pltpu.VMEM((groups // 2, round_up(2 * rows + span - 1, LANES)), f32),
+            pltpu.VMEM((n_blk, span_rows, half), bf16),
+            pltpu.SemaphoreType.DMA((OUT_COPIES,)),
+        ],
         compiler_params=limit(16),
         name="conv",
     )(lengths, taps, source)

time: 36.7 us -> 36.7 us (level)
  transfers between devices with their start and end apart: 11 -> 11, of which waited for: 8 -> 8; matrix products, arithmetic and copies ran while one was open for 4% -> 4% of each run, Pallas kernels for 13% -> 12%
where the time goes in v11:
time: 36.7 us; the launch traced here: 36.2 us
  starting transfers between devices  18.3 us (50%)
  waiting for transfers between devices  7.08 us (19%)
  Pallas kernels  6.82 us (19%)
  local copies, waits for them, and re-layouts  2.7 us (7%)
  between operations  1.37 us (4%)
    all_to_all x1, starting transfers between devices, per_device(): lax.all_to_all(send, ('blk', 'tenant'), split_axis=0, concat_axis=0, axis...  7.3 us
    all_to_all x1, starting transfers between devices, per_device(): lax.all_to_all(partial, 'blk', split_axis=0, concat_axis=0, axis_index_gr...  4.85 us
    ppermute x3, starting transfers between devices, per_device(): pages.append(lax.ppermute(inputs, 'blk', turn))  4.45 us
    pallas_call x1, Pallas kernels, per_device(): pl.pallas_call(functools.partial(conv_kernel, fr, n_ten, gsize), out_shap...  2.94 us
    all_to_all x1, waiting for transfers between devices, per_device(): lax.all_to_all(partial, 'blk', split_axis=0, concat_axis=0, axis_index_gr...  2.04 us
    ppermute x3, waiting for transfers between devices, per_device(): pages.append(lax.ppermute(inputs, 'blk', turn))  1.84 us
    pallas_call x1, Pallas kernels, per_device(): pl.pallas_call(functools.partial(pack_kernel, tap_order(n_blk, n_ten), n_...  1.64 us
    slice x1, local copies, waits for them, and re-layouts, per_device(): history[i * piece:(i + 1) * piece]  1.36 us
  transfers between devices with their start and end apart: 11, of which 8 were waited for; matrix products, arithmetic and copies ran while one was open for 4% of the time, Pallas kernels for 12%

profile of v11, /device:TPU:0, one launch (start us, length us, event | category | flops | bytes accessed | tf_op | source)
XLA Modules:
  0.0 36.2 jit_solution(749267882777928563)
XLA Ops:
  0.6 1.6 %pack.1 = (bf16[32,18,2,128]{3,2,1,0:T(2,128)(2,1)}, f32[8,128]{1,0:T(8,128)}) custom-call(bf16[34,256]{1,0:T(8,128)(2,1)} %taps_hbm.1, bf16[1,128]{1,0:T(2,128)(2,1)} %bitcast.22), custom_call_target="tpu_custom_call" | custom-call | tf_op jit(solution)/shard_map/pack/pallas_call | solution.py:280
  2.3 7.3 %all-to-all-start = ((bf16[32,18,2,128]{3,2,1,0:T(2,128)(2,1)}), bf16[32,18,2,128]{3,2,1,0:T(2,128)(2,1)S(1)}, u32[]{:S(2)}, u32[]{:S(2)}) async-start(bf16[32,18,2,128]{3,2,1,0:T(2,128)(2,1)} %get-tuple-element.13), calls=%async_computation | async-start | bytes 589824 | tf_op jit(solution)/shard_map/all_to_all | solution.py:296
  9.6 0.0 copy-start
  9.6 1.4 %slice_bitcast_fusion = (bf16[32,4096]{1,0:T(8,128)(2,1)S(1)}, bf16[32,4096]{1,0:T(8,128)(2,1)S(1)}, bf16[32,4096]{1,0:T(8,128)(2,1)S(1)}, bf16[32,4096]{1,0:T(8,128)(2,1)S(1)}) fusion(bf16[1,128,4096]{2,1,0:T(8,128)(2,1)} %param.8), kind=kLoop, calls=%fused_computation | loop fusion | bytes 2097152 | tf_op jit(solution)/shard_map/slice | solution.py:307
  11.0 0.3 collective-permute-start
  11.3 0.3 collective-permute-start.1
  11.5 0.3 collective-permute-start.2
  11.8 0.3 collective-permute-start.3
  12.7 0.0 collective-permute-done.refs_0_
  12.7 0.2 collective-permute-done.1.refs_1_
  12.9 0.4 %collective-permute-done.2.refs_2_ = bf16[32,4096]{1,0:T(8,128)(2,1)S(1)} collective-permute-done((bf16[32,4096]{1,0:T(8,128)(2,1)S(1)}, bf16[32,4096]{1,0:T(8,128)(2,1)S(1)}, u32[]{:S(2)}, u32[]{:S(2)}) %collective-permute-start.2) | collective-permute-done | bytes 262176 | tf_op jit(solution)/shard_map/ppermute | solution.py:307
  13.3 0.4 %collective-permute-done.3.refs_3_ = bf16[32,4096]{1,0:T(8,128)(2,1)S(1)} collective-permute-done((bf16[32,4096]{1,0:T(8,128)(2,1)S(1)}, bf16[32,4096]{1,0:T(8,128)(2,1)S(1)}, u32[]{:S(2)}, u32[]{:S(2)}) %collective-permute-start.3) | collective-permute-done | bytes 262176 | tf_op jit(solution)/shard_map/ppermute | solution.py:307
  13.7 0.2 source.1.source_ref._
  13.9 0.6 %copy-done.1 = bf16[1,8,4096]{2,1,0:T(8,128)(2,1)S(1)} copy-done((bf16[1,8,4096]{2,1,0:T(8,128)(2,1)S(1)}, bf16[1,8,4096]{2,1,0:T(8,128)(2,1)}, u32[]{:S(2)}) %copy-start.1) | copy-done | bytes 65560
  14.5 0.0 copy-done.2
  14.6 1.8 %collective-permute-start.4 = (bf16[8,4096]{1,0:T(8,128)(2,1)S(1)}, bf16[8,4096]{1,0:T(8,128)(2,1)S(1)}, u32[]{:S(2)}, u32[]{:S(2)}) collective-permute-start(bf16[8,4096]{1,0:T(8,128)(2,1)S(1)} %inputs.1.refs_0_.input_ref), channel_id=1, source_target_pairs={{0,8},{4,12},{8,0},{12,4},{16,24},{20,28},{24,16},{28,20},{1,9},{5... | collective-permute-start | bytes 196616 | tf_op jit(solution)/shard_map/ppermute | solution.py:339
  16.4 2.4 %collective-permute-start.5 = (bf16[8,4096]{1,0:T(8,128)(2,1)S(1)}, bf16[8,4096]{1,0:T(8,128)(2,1)S(1)}, u32[]{:S(2)}, u32[]{:S(2)}) collective-permute-start(bf16[8,4096]{1,0:T(8,128)(2,1)S(1)} %inputs.1.refs_0_.input_ref), channel_id=1, source_target_pairs={{0,16},{4,20},{8,24},{12,28},{16,0},{20,4},{24,8},{28,12},{1,17},{... | collective-permute-start | bytes 196616 | tf_op jit(solution)/shard_map/ppermute | solution.py:339
  18.8 0.2 collective-permute-start.6
  19.0 1.2 %all-to-all-done.taps_ref = bf16[32,18,2,128]{3,2,1,0:T(2,128)(2,1)S(1)} async-done(((bf16[32,18,2,128]{3,2,1,0:T(2,128)(2,1)}), bf16[32,18,2,128]{3,2,1,0:T(2,128)(2,1)S(1)}, u32[]{:S(2)}, u32[]{:S(2)}) %all-to-all-start) | async-done | bytes 294944 | tf_op jit(solution)/shard_map/all_to_all | solution.py:296
  20.2 2.9 %conv.1._ = bf16[8,8,2048]{2,1,0:T(8,128)(2,1)} custom-call(s32[1]{0:T(128)S(6)} %copy.10.len_ref, bf16[32,18,2,128]{3,2,1,0:T(2,128)(2,1)S(1)} %all-to-all-done.taps_ref, bf16[256,2048]{1,0:T(8,128)(2,1)S(1)} %source.1.source_ref._), custom_call_target="tpu_custom_call" | custom-call | tf_op jit(solution)/shard_map/conv/pallas_call | solution.py:340
  23.2 0.0 collective-permute-done.4.refs_1_
  23.2 0.8 %collective-permute-done.5.refs_2_ = bf16[8,4096]{1,0:T(8,128)(2,1)S(1)} collective-permute-done((bf16[8,4096]{1,0:T(8,128)(2,1)S(1)}, bf16[8,4096]{1,0:T(8,128)(2,1)S(1)}, u32[]{:S(2)}, u32[]{:S(2)}) %collective-permute-start.5) | collective-permute-done | bytes 65568 | tf_op jit(solution)/shard_map/ppermute | solution.py:339
  24.0 1.0 %collective-permute-done.6.refs_3_ = bf16[8,4096]{1,0:T(8,128)(2,1)S(1)} collective-permute-done((bf16[8,4096]{1,0:T(8,128)(2,1)S(1)}, bf16[8,4096]{1,0:T(8,128)(2,1)S(1)}, u32[]{:S(2)}, u32[]{:S(2)}) %collective-permute-start.6) | collective-permute-done | bytes 65568 | tf_op jit(solution)/shard_map/ppermute | solution.py:339
  25.0 4.8 %all-to-all-start.1 = ((bf16[8,8,2048]{2,1,0:T(8,128)(2,1)}), bf16[8,8,2048]{2,1,0:T(8,128)(2,1)S(1)}, u32[]{:S(2)}, u32[]{:S(2)}) async-start(bf16[8,8,2048]{2,1,0:T(8,128)(2,1)} %conv.1._), calls=%async_computation.1 | async-start | bytes 524288 | tf_op jit(solution)/shard_map/all_to_all | solution.py:355
  29.9 0.1 collective-permute-start.7
  30.1 0.4 %collective-permute-start.8 = (bf16[2,36,128]{2,1,0:T(8,128)(2,1)S(1)}, bf16[2,36,128]{2,1,0:T(8,128)(2,1)S(1)}, u32[]{:S(2)}, u32[]{:S(2)}) collective-permute-start(bf16[2,36,128]{2,1,0:T(8,128)(2,1)S(1)} %get-tuple-element.20.own_head_ref), channel_id=1, source_target_pairs={{0,4},{4,0},{8,12},{12,8},{16,20},{20,16},{24,28},{28,24},{1,5},{5... | collective-permute-start | bytes 55304 | tf_op jit(solution)/shard_map/ppermute | solution.py:375
  30.5 1.1 %collective-permute-done.8.peer_head_ref = bf16[2,36,128]{2,1,0:T(8,128)(2,1)S(1)} collective-permute-done((bf16[2,36,128]{2,1,0:T(8,128)(2,1)S(1)}, bf16[2,36,128]{2,1,0:T(8,128)(2,1)S(1)}, u32[]{:S(2)}, u32[]{:S(2)}) %collective-permute-start.8) | collective-permute-done | bytes 18464 | tf_op jit(solution)/shard_map/ppermute | solution.py:375
  31.5 0.0 collective-permute-done.7.peer_stack_ref
  31.5 0.7 %copy-done.4 = s32[1,8,1]{1,2,0:T(1,128)S(1)} copy-done((s32[1,8,1]{1,2,0:T(1,128)S(1)}, s32[1,8,1]{1,2,0:T(1,128)}, u32[]{:S(2)}) %copy-start.4) | copy-done | bytes 56
  32.2 1.3 %span.1 = (f32[8,4096]{1,0:T(8,128)S(1)}, bf16[2,8,4096]{2,1,0:T(8,128)(2,1)}) custom-call(s32[8]{0:T(128)S(1)} %bitcast.20, bf16[4,8,4096]{2,1,0:T(8,128)(2,1)S(1)} %get-tuple-element.19.own_stack_ref, bf16[4,8,4096]{2,1,0:T(8,128)(2,1)S(1)} %collective-permute-done.7.peer_stack_ref, bf16[2,36,128]{2,1,0:T(8,128)(2,1)S(1)} %get-tuple-element.20.own_head_ref, ...), custom_call_target="tpu_custom_call" | custom-call | tf_op jit(solution)/shard_map/span/pallas_call | solution.py:377
  33.5 2.0 %all-to-all-done.1.parts_ref = bf16[8,8,2048]{2,1,0:T(8,128)(2,1)S(1)} async-done(((bf16[8,8,2048]{2,1,0:T(8,128)(2,1)}), bf16[8,8,2048]{2,1,0:T(8,128)(2,1)S(1)}, u32[]{:S(2)}, u32[]{:S(2)}) %all-to-all-start.1) | async-done | bytes 262176 | tf_op jit(solution)/shard_map/all_to_all | solution.py:355
  35.5 0.7 %finish.1 = bf16[8,4096]{1,0:T(8,128)(2,1)} custom-call(bf16[8,8,2048]{2,1,0:T(8,128)(2,1)S(1)} %all-to-all-done.1.parts_ref, bf16[8,4096]{1,0:T(8,128)(2,1)S(1)} %bitcast.19, f32[8,4096]{1,0:T(8,128)S(1)} %get-tuple-element.22.extra_ref), custom_call_target="tpu_custom_call" | custom-call | tf_op jit(solution)/shard_map/finish/pallas_call | solution.py:393
  (8 shorter events, 0.1 us)
Async XLA Ops:
  2.3 17.9 %all-to-all-start = ((bf16[32,18,2,128]{3,2,1,0:T(2,128)(2,1)}), bf16[32,18,2,128]{3,2,1,0:T(2,128)(2,1)S(1)}, u32[]{:S(2)}, u32[]{:S(2)}) async-start(bf16[32,18,2,128]{3,2,1,0:T(2,128)(2,1)} %get-tuple-element.13), calls=%async_computation | async-start | bytes 589824 | tf_op jit(solution)/shard_map/all_to_all | solution.py:296
  9.6 4.1 %copy-start = (bf16[1,128,4096]{2,1,0:T(8,128)(2,1)S(1)}, bf16[1,128,4096]{2,1,0:T(8,128)(2,1)}, u32[]{:S(2)}) copy-start(bf16[1,128,4096]{2,1,0:T(8,128)(2,1)} %param.8) | copy-start | bytes 3145732
  11.0 1.7 %collective-permute-start = (bf16[32,4096]{1,0:T(8,128)(2,1)S(1)}, bf16[32,4096]{1,0:T(8,128)(2,1)S(1)}, u32[]{:S(2)}, u32[]{:S(2)}) collective-permute-start(bf16[32,4096]{1,0:T(8,128)(2,1)S(1)} %get-tuple-element.26), channel_id=1, source_target_pairs={{0,4},{4,0},{8,12},{12,8},{16,20},{20,16},{24,28},{28,24},{1,5},{5... | collective-permute-start | bytes 786440 | tf_op jit(solution)/shard_map/ppermute | solution.py:307
  11.3 1.7 %collective-permute-start.1 = (bf16[32,4096]{1,0:T(8,128)(2,1)S(1)}, bf16[32,4096]{1,0:T(8,128)(2,1)S(1)}, u32[]{:S(2)}, u32[]{:S(2)}) collective-permute-start(bf16[32,4096]{1,0:T(8,128)(2,1)S(1)} %get-tuple-element.25), channel_id=1, source_target_pairs={{0,4},{4,0},{8,12},{12,8},{16,20},{20,16},{24,28},{28,24},{1,5},{5... | collective-permute-start | bytes 786440 | tf_op jit(solution)/shard_map/ppermute | solution.py:307
  11.5 1.8 %collective-permute-start.2 = (bf16[32,4096]{1,0:T(8,128)(2,1)S(1)}, bf16[32,4096]{1,0:T(8,128)(2,1)S(1)}, u32[]{:S(2)}, u32[]{:S(2)}) collective-permute-start(bf16[32,4096]{1,0:T(8,128)(2,1)S(1)} %get-tuple-element.27), channel_id=1, source_target_pairs={{0,4},{4,0},{8,12},{12,8},{16,20},{20,16},{24,28},{28,24},{1,5},{5... | collective-permute-start | bytes 786440 | tf_op jit(solution)/shard_map/ppermute | solution.py:307
  11.8 1.9 %collective-permute-start.3 = (bf16[32,4096]{1,0:T(8,128)(2,1)S(1)}, bf16[32,4096]{1,0:T(8,128)(2,1)S(1)}, u32[]{:S(2)}, u32[]{:S(2)}) collective-permute-start(bf16[32,4096]{1,0:T(8,128)(2,1)S(1)} %get-tuple-element.24), channel_id=1, source_target_pairs={{0,4},{4,0},{8,12},{12,8},{16,20},{20,16},{24,28},{28,24},{1,5},{5... | collective-permute-start | bytes 786440 | tf_op jit(solution)/shard_map/ppermute | solution.py:307
  13.7 0.8 %copy-start.1 = (bf16[1,8,4096]{2,1,0:T(8,128)(2,1)S(1)}, bf16[1,8,4096]{2,1,0:T(8,128)(2,1)}, u32[]{:S(2)}) copy-start(bf16[1,8,4096]{2,1,0:T(8,128)(2,1)} %param.10) | copy-start | bytes 196612
  13.7 0.9 %copy-start.2 = (bf16[1,8,4096]{2,1,0:T(8,128)(2,1)S(1)}, bf16[1,8,4096]{2,1,0:T(8,128)(2,1)}, u32[]{:S(2)}) copy-start(bf16[1,8,4096]{2,1,0:T(8,128)(2,1)} %param.11) | copy-start | bytes 196612
  14.6 8.6 %collective-permute-start.4 = (bf16[8,4096]{1,0:T(8,128)(2,1)S(1)}, bf16[8,4096]{1,0:T(8,128)(2,1)S(1)}, u32[]{:S(2)}, u32[]{:S(2)}) collective-permute-start(bf16[8,4096]{1,0:T(8,128)(2,1)S(1)} %inputs.1.refs_0_.input_ref), channel_id=1, source_target_pairs={{0,8},{4,12},{8,0},{12,4},{16,24},{20,28},{24,16},{28,20},{1,9},{5... | collective-permute-start | bytes 196616 | tf_op jit(solution)/shard_map/ppermute | solution.py:339
  16.4 7.5 %collective-permute-start.5 = (bf16[8,4096]{1,0:T(8,128)(2,1)S(1)}, bf16[8,4096]{1,0:T(8,128)(2,1)S(1)}, u32[]{:S(2)}, u32[]{:S(2)}) collective-permute-start(bf16[8,4096]{1,0:T(8,128)(2,1)S(1)} %inputs.1.refs_0_.input_ref), channel_id=1, source_target_pairs={{0,16},{4,20},{8,24},{12,28},{16,0},{20,4},{24,8},{28,12},{1,17},{... | collective-permute-start | bytes 196616 | tf_op jit(solution)/shard_map/ppermute | solution.py:339
  18.8 6.2 %collective-permute-start.6 = (bf16[8,4096]{1,0:T(8,128)(2,1)S(1)}, bf16[8,4096]{1,0:T(8,128)(2,1)S(1)}, u32[]{:S(2)}, u32[]{:S(2)}) collective-permute-start(bf16[8,4096]{1,0:T(8,128)(2,1)S(1)} %inputs.1.refs_0_.input_ref), channel_id=1, source_target_pairs={{0,24},{4,28},{8,16},{12,20},{16,8},{20,12},{24,0},{28,4},{1,25},{... | collective-permute-start | bytes 196616 | tf_op jit(solution)/shard_map/ppermute | solution.py:339
  25.0 10.5 %all-to-all-start.1 = ((bf16[8,8,2048]{2,1,0:T(8,128)(2,1)}), bf16[8,8,2048]{2,1,0:T(8,128)(2,1)S(1)}, u32[]{:S(2)}, u32[]{:S(2)}) async-start(bf16[8,8,2048]{2,1,0:T(8,128)(2,1)} %conv.1._), calls=%async_computation.1 | async-start | bytes 524288 | tf_op jit(solution)/shard_map/all_to_all | solution.py:355
  29.9 1.6 %collective-permute-start.7 = (bf16[4,8,4096]{2,1,0:T(8,128)(2,1)S(1)}, bf16[4,8,4096]{2,1,0:T(8,128)(2,1)S(1)}, u32[]{:S(2)}, u32[]{:S(2)}) collective-permute-start(bf16[4,8,4096]{2,1,0:T(8,128)(2,1)S(1)} %get-tuple-element.19.own_stack_ref), channel_id=1, source_target_pairs={{0,4},{4,0},{8,12},{12,8},{16,20},{20,16},{24,28},{28,24},{1,5},{5... | collective-permute-start | bytes 786440 | tf_op jit(solution)/shard_map/ppermute | solution.py:374
  30.1 1.5 %collective-permute-start.8 = (bf16[2,36,128]{2,1,0:T(8,128)(2,1)S(1)}, bf16[2,36,128]{2,1,0:T(8,128)(2,1)S(1)}, u32[]{:S(2)}, u32[]{:S(2)}) collective-permute-start(bf16[2,36,128]{2,1,0:T(8,128)(2,1)S(1)} %get-tuple-element.20.own_head_ref), channel_id=1, source_target_pairs={{0,4},{4,0},{8,12},{12,8},{16,20},{20,16},{24,28},{28,24},{1,5},{5... | collective-permute-start | bytes 55304 | tf_op jit(solution)/shard_map/ppermute | solution.py:375
  31.5 0.7 %copy-start.4 = (s32[1,8,1]{1,2,0:T(1,128)S(1)}, s32[1,8,1]{1,2,0:T(1,128)}, u32[]{:S(2)}) copy-start(s32[1,8,1]{1,2,0:T(1,128)} %param.15) | copy-start | bytes 100
  32.2 3.4 %copy-start.3 = (bf16[1,8,4096]{2,1,0:T(8,128)(2,1)S(1)}, bf16[1,8,4096]{2,1,0:T(8,128)(2,1)}, u32[]{:S(2)}) copy-start(bf16[1,8,4096]{2,1,0:T(8,128)(2,1)} %param.9) | copy-start | bytes 196612

commit v12 on v11

--- a/solution.py
+++ b/solution.py
@@ -123,11 +123,23 @@
 def toeplitz_product(taps_ref, first_group, gsize, outputs, depth, source):
     per = LANES // gsize
     lanes = taps_ref.shape[1]
+    shift = outputs - 1 - lax.broadcasted_iota(jnp.int32, (outputs, LANES), 0)
+    inside = lax.broadcasted_iota(jnp.int32, (outputs, LANES), 1) + shift < LANES
     tiles = []
     for g in range(per):
         line = jnp.broadcast_to(taps_ref[pl.ds(first_group + g, 1), :], (outputs, lanes))
-        line = pltpu.roll(line, lanes - (outputs - 1), 1, stride=1, stride_axis=0)
-        tiles.append(line[:, :depth])
+        if depth % LANES or lanes != depth + LANES or outputs > LANES:
+            line = pltpu.roll(line, lanes - (outputs - 1), 1, stride=1, stride_axis=0)
+            tiles.append(line[:, :depth])
+            continue
+        turned = [
+            pltpu.roll(
+                line[:, at : at + LANES], LANES - (outputs - 1), 1, stride=1, stride_axis=0
+            )
+            for at in range(0, lanes, LANES)
+        ]
+        pieces = [jnp.where(inside, a, b) for a, b in zip(turned[:-1], turned[1:], strict=True)]
+        tiles.append(jnp.concatenate(pieces, axis=1))
     matrix = jnp.concatenate(tiles, axis=0).astype(bf16)
     product = jnp.dot(matrix, source, preferred_element_type=f32)
     group = lax.broadcasted_iota(jnp.int32, (outputs, LANES), 1) // gsize

time: 36.7 us -> 36.7 us (level)
  no operation moved by 1% of the time
where the time goes in v12:
time: 36.7 us; the launch traced here: 36.2 us
  starting transfers between devices  18.3 us (50%)
  waiting for transfers between devices  7.09 us (19%)
  Pallas kernels  6.81 us (19%)
  local copies, waits for them, and re-layouts  2.7 us (7%)
  between operations  1.37 us (4%)
    all_to_all x1, starting transfers between devices, per_device(): lax.all_to_all(send, ('blk', 'tenant'), split_axis=0, concat_axis=0, axis...  7.3 us
    all_to_all x1, starting transfers between devices, per_device(): lax.all_to_all(partial, 'blk', split_axis=0, concat_axis=0, axis_index_gr...  4.85 us
    ppermute x3, starting transfers between devices, per_device(): pages.append(lax.ppermute(inputs, 'blk', turn))  4.45 us
    pallas_call x1, Pallas kernels, per_device(): pl.pallas_call(functools.partial(conv_kernel, fr, n_ten, gsize), out_shap...  2.93 us
    all_to_all x1, waiting for transfers between devices, per_device(): lax.all_to_all(partial, 'blk', split_axis=0, concat_axis=0, axis_index_gr...  2.03 us
    ppermute x3, waiting for transfers between devices, per_device(): pages.append(lax.ppermute(inputs, 'blk', turn))  1.85 us
    pallas_call x1, Pallas kernels, per_device(): pl.pallas_call(functools.partial(pack_kernel, tap_order(n_blk, n_ten), n_...  1.64 us
    slice x1, local copies, waits for them, and re-layouts, per_device(): history[i * piece:(i + 1) * piece]  1.36 us
  transfers between devices with their start and end apart: 11, of which 8 were waited for; matrix products, arithmetic and copies ran while one was open for 4% of the time, Pallas kernels for 12%

profile of v12, /device:TPU:0, one launch (start us, length us, event | category | flops | bytes accessed | tf_op | source)
XLA Modules:
  0.0 36.2 jit_solution(13646328181184807299)
XLA Ops:
  0.6 1.6 %pack.1 = (bf16[32,18,2,128]{3,2,1,0:T(2,128)(2,1)}, f32[8,128]{1,0:T(8,128)}) custom-call(bf16[34,256]{1,0:T(8,128)(2,1)} %taps_hbm.1, bf16[1,128]{1,0:T(2,128)(2,1)} %bitcast.22), custom_call_target="tpu_custom_call" | custom-call | tf_op jit(solution)/shard_map/pack/pallas_call | solution.py:292
  2.3 7.3 %all-to-all-start = ((bf16[32,18,2,128]{3,2,1,0:T(2,128)(2,1)}), bf16[32,18,2,128]{3,2,1,0:T(2,128)(2,1)S(1)}, u32[]{:S(2)}, u32[]{:S(2)}) async-start(bf16[32,18,2,128]{3,2,1,0:T(2,128)(2,1)} %get-tuple-element.13), calls=%async_computation | async-start | bytes 589824 | tf_op jit(solution)/shard_map/all_to_all | solution.py:308
  9.6 0.0 copy-start
  9.6 1.4 %slice_bitcast_fusion = (bf16[32,4096]{1,0:T(8,128)(2,1)S(1)}, bf16[32,4096]{1,0:T(8,128)(2,1)S(1)}, bf16[32,4096]{1,0:T(8,128)(2,1)S(1)}, bf16[32,4096]{1,0:T(8,128)(2,1)S(1)}) fusion(bf16[1,128,4096]{2,1,0:T(8,128)(2,1)} %param.8), kind=kLoop, calls=%fused_computation | loop fusion | bytes 2097152 | tf_op jit(solution)/shard_map/slice | solution.py:319
  11.0 0.3 collective-permute-start
  11.3 0.3 collective-permute-start.1
  11.5 0.3 collective-permute-start.2
  11.8 0.3 collective-permute-start.3
  12.7 0.0 collective-permute-done.refs_0_
  12.7 0.2 collective-permute-done.1.refs_1_
  12.9 0.4 %collective-permute-done.2.refs_2_ = bf16[32,4096]{1,0:T(8,128)(2,1)S(1)} collective-permute-done((bf16[32,4096]{1,0:T(8,128)(2,1)S(1)}, bf16[32,4096]{1,0:T(8,128)(2,1)S(1)}, u32[]{:S(2)}, u32[]{:S(2)}) %collective-permute-start.2) | collective-permute-done | bytes 262176 | tf_op jit(solution)/shard_map/ppermute | solution.py:319
  13.3 0.4 %collective-permute-done.3.refs_3_ = bf16[32,4096]{1,0:T(8,128)(2,1)S(1)} collective-permute-done((bf16[32,4096]{1,0:T(8,128)(2,1)S(1)}, bf16[32,4096]{1,0:T(8,128)(2,1)S(1)}, u32[]{:S(2)}, u32[]{:S(2)}) %collective-permute-start.3) | collective-permute-done | bytes 262176 | tf_op jit(solution)/shard_map/ppermute | solution.py:319
  13.7 0.2 source.1.source_ref._
  13.9 0.6 %copy-done.1 = bf16[1,8,4096]{2,1,0:T(8,128)(2,1)S(1)} copy-done((bf16[1,8,4096]{2,1,0:T(8,128)(2,1)S(1)}, bf16[1,8,4096]{2,1,0:T(8,128)(2,1)}, u32[]{:S(2)}) %copy-start.1) | copy-done | bytes 65560
  14.5 0.0 copy-done.2
  14.6 1.8 %collective-permute-start.4 = (bf16[8,4096]{1,0:T(8,128)(2,1)S(1)}, bf16[8,4096]{1,0:T(8,128)(2,1)S(1)}, u32[]{:S(2)}, u32[]{:S(2)}) collective-permute-start(bf16[8,4096]{1,0:T(8,128)(2,1)S(1)} %inputs.1.refs_0_.input_ref), channel_id=1, source_target_pairs={{0,8},{4,12},{8,0},{12,4},{16,24},{20,28},{24,16},{28,20},{1,9},{5... | collective-permute-start | bytes 196616 | tf_op jit(solution)/shard_map/ppermute | solution.py:351
  16.4 2.4 %collective-permute-start.5 = (bf16[8,4096]{1,0:T(8,128)(2,1)S(1)}, bf16[8,4096]{1,0:T(8,128)(2,1)S(1)}, u32[]{:S(2)}, u32[]{:S(2)}) collective-permute-start(bf16[8,4096]{1,0:T(8,128)(2,1)S(1)} %inputs.1.refs_0_.input_ref), channel_id=1, source_target_pairs={{0,16},{4,20},{8,24},{12,28},{16,0},{20,4},{24,8},{28,12},{1,17},{... | collective-permute-start | bytes 196616 | tf_op jit(solution)/shard_map/ppermute | solution.py:351
  18.8 0.2 collective-permute-start.6
  19.0 1.2 %all-to-all-done.taps_ref = bf16[32,18,2,128]{3,2,1,0:T(2,128)(2,1)S(1)} async-done(((bf16[32,18,2,128]{3,2,1,0:T(2,128)(2,1)}), bf16[32,18,2,128]{3,2,1,0:T(2,128)(2,1)S(1)}, u32[]{:S(2)}, u32[]{:S(2)}) %all-to-all-start) | async-done | bytes 294944 | tf_op jit(solution)/shard_map/all_to_all | solution.py:308
  20.2 2.9 %conv.1._ = bf16[8,8,2048]{2,1,0:T(8,128)(2,1)} custom-call(s32[1]{0:T(128)S(6)} %copy.10.len_ref, bf16[32,18,2,128]{3,2,1,0:T(2,128)(2,1)S(1)} %all-to-all-done.taps_ref, bf16[256,2048]{1,0:T(8,128)(2,1)S(1)} %source.1.source_ref._), custom_call_target="tpu_custom_call" | custom-call | tf_op jit(solution)/shard_map/conv/pallas_call | solution.py:352
  23.1 0.0 collective-permute-done.4.refs_1_
  23.2 0.8 %collective-permute-done.5.refs_2_ = bf16[8,4096]{1,0:T(8,128)(2,1)S(1)} collective-permute-done((bf16[8,4096]{1,0:T(8,128)(2,1)S(1)}, bf16[8,4096]{1,0:T(8,128)(2,1)S(1)}, u32[]{:S(2)}, u32[]{:S(2)}) %collective-permute-start.5) | collective-permute-done | bytes 65568 | tf_op jit(solution)/shard_map/ppermute | solution.py:351
  24.0 1.0 %collective-permute-done.6.refs_3_ = bf16[8,4096]{1,0:T(8,128)(2,1)S(1)} collective-permute-done((bf16[8,4096]{1,0:T(8,128)(2,1)S(1)}, bf16[8,4096]{1,0:T(8,128)(2,1)S(1)}, u32[]{:S(2)}, u32[]{:S(2)}) %collective-permute-start.6) | collective-permute-done | bytes 65568 | tf_op jit(solution)/shard_map/ppermute | solution.py:351
  25.0 4.8 %all-to-all-start.1 = ((bf16[8,8,2048]{2,1,0:T(8,128)(2,1)}), bf16[8,8,2048]{2,1,0:T(8,128)(2,1)S(1)}, u32[]{:S(2)}, u32[]{:S(2)}) async-start(bf16[8,8,2048]{2,1,0:T(8,128)(2,1)} %conv.1._), calls=%async_computation.1 | async-start | bytes 524288 | tf_op jit(solution)/shard_map/all_to_all | solution.py:367
  29.9 0.1 collective-permute-start.7
  30.1 0.4 %collective-permute-start.8 = (bf16[2,36,128]{2,1,0:T(8,128)(2,1)S(1)}, bf16[2,36,128]{2,1,0:T(8,128)(2,1)S(1)}, u32[]{:S(2)}, u32[]{:S(2)}) collective-permute-start(bf16[2,36,128]{2,1,0:T(8,128)(2,1)S(1)} %get-tuple-element.20.own_head_ref), channel_id=1, source_target_pairs={{0,4},{4,0},{8,12},{12,8},{16,20},{20,16},{24,28},{28,24},{1,5},{5... | collective-permute-start | bytes 55304 | tf_op jit(solution)/shard_map/ppermute | solution.py:387
  30.5 1.1 %collective-permute-done.8.peer_head_ref = bf16[2,36,128]{2,1,0:T(8,128)(2,1)S(1)} collective-permute-done((bf16[2,36,128]{2,1,0:T(8,128)(2,1)S(1)}, bf16[2,36,128]{2,1,0:T(8,128)(2,1)S(1)}, u32[]{:S(2)}, u32[]{:S(2)}) %collective-permute-start.8) | collective-permute-done | bytes 18464 | tf_op jit(solution)/shard_map/ppermute | solution.py:387
  31.5 0.0 collective-permute-done.7.peer_stack_ref
  31.5 0.7 %copy-done.4 = s32[1,8,1]{1,2,0:T(1,128)S(1)} copy-done((s32[1,8,1]{1,2,0:T(1,128)S(1)}, s32[1,8,1]{1,2,0:T(1,128)}, u32[]{:S(2)}) %copy-start.4) | copy-done | bytes 56
  32.2 1.3 %span.1 = (f32[8,4096]{1,0:T(8,128)S(1)}, bf16[2,8,4096]{2,1,0:T(8,128)(2,1)}) custom-call(s32[8]{0:T(128)S(1)} %bitcast.20, bf16[4,8,4096]{2,1,0:T(8,128)(2,1)S(1)} %get-tuple-element.19.own_stack_ref, bf16[4,8,4096]{2,1,0:T(8,128)(2,1)S(1)} %collective-permute-done.7.peer_stack_ref, bf16[2,36,128]{2,1,0:T(8,128)(2,1)S(1)} %get-tuple-element.20.own_head_ref, ...), custom_call_target="tpu_custom_call" | custom-call | tf_op jit(solution)/shard_map/span/pallas_call | solution.py:389
  33.5 2.0 %all-to-all-done.1.parts_ref = bf16[8,8,2048]{2,1,0:T(8,128)(2,1)S(1)} async-done(((bf16[8,8,2048]{2,1,0:T(8,128)(2,1)}), bf16[8,8,2048]{2,1,0:T(8,128)(2,1)S(1)}, u32[]{:S(2)}, u32[]{:S(2)}) %all-to-all-start.1) | async-done | bytes 262176 | tf_op jit(solution)/shard_map/all_to_all | solution.py:367
  35.5 0.7 %finish.1 = bf16[8,4096]{1,0:T(8,128)(2,1)} custom-call(bf16[8,8,2048]{2,1,0:T(8,128)(2,1)S(1)} %all-to-all-done.1.parts_ref, bf16[8,4096]{1,0:T(8,128)(2,1)S(1)} %bitcast.19, f32[8,4096]{1,0:T(8,128)S(1)} %get-tuple-element.22.extra_ref), custom_call_target="tpu_custom_call" | custom-call | tf_op jit(solution)/shard_map/finish/pallas_call | solution.py:405
  (8 shorter events, 0.1 us)
Async XLA Ops:
  2.3 17.9 %all-to-all-start = ((bf16[32,18,2,128]{3,2,1,0:T(2,128)(2,1)}), bf16[32,18,2,128]{3,2,1,0:T(2,128)(2,1)S(1)}, u32[]{:S(2)}, u32[]{:S(2)}) async-start(bf16[32,18,2,128]{3,2,1,0:T(2,128)(2,1)} %get-tuple-element.13), calls=%async_computation | async-start | bytes 589824 | tf_op jit(solution)/shard_map/all_to_all | solution.py:308
  9.6 4.1 %copy-start = (bf16[1,128,4096]{2,1,0:T(8,128)(2,1)S(1)}, bf16[1,128,4096]{2,1,0:T(8,128)(2,1)}, u32[]{:S(2)}) copy-start(bf16[1,128,4096]{2,1,0:T(8,128)(2,1)} %param.8) | copy-start | bytes 3145732
  11.0 1.7 %collective-permute-start = (bf16[32,4096]{1,0:T(8,128)(2,1)S(1)}, bf16[32,4096]{1,0:T(8,128)(2,1)S(1)}, u32[]{:S(2)}, u32[]{:S(2)}) collective-permute-start(bf16[32,4096]{1,0:T(8,128)(2,1)S(1)} %get-tuple-element.26), channel_id=1, source_target_pairs={{0,4},{4,0},{8,12},{12,8},{16,20},{20,16},{24,28},{28,24},{1,5},{5... | collective-permute-start | bytes 786440 | tf_op jit(solution)/shard_map/ppermute | solution.py:319
  11.3 1.7 %collective-permute-start.1 = (bf16[32,4096]{1,0:T(8,128)(2,1)S(1)}, bf16[32,4096]{1,0:T(8,128)(2,1)S(1)}, u32[]{:S(2)}, u32[]{:S(2)}) collective-permute-start(bf16[32,4096]{1,0:T(8,128)(2,1)S(1)} %get-tuple-element.25), channel_id=1, source_target_pairs={{0,4},{4,0},{8,12},{12,8},{16,20},{20,16},{24,28},{28,24},{1,5},{5... | collective-permute-start | bytes 786440 | tf_op jit(solution)/shard_map/ppermute | solution.py:319
  11.5 1.8 %collective-permute-start.2 = (bf16[32,4096]{1,0:T(8,128)(2,1)S(1)}, bf16[32,4096]{1,0:T(8,128)(2,1)S(1)}, u32[]{:S(2)}, u32[]{:S(2)}) collective-permute-start(bf16[32,4096]{1,0:T(8,128)(2,1)S(1)} %get-tuple-element.27), channel_id=1, source_target_pairs={{0,4},{4,0},{8,12},{12,8},{16,20},{20,16},{24,28},{28,24},{1,5},{5... | collective-permute-start | bytes 786440 | tf_op jit(solution)/shard_map/ppermute | solution.py:319
  11.8 1.9 %collective-permute-start.3 = (bf16[32,4096]{1,0:T(8,128)(2,1)S(1)}, bf16[32,4096]{1,0:T(8,128)(2,1)S(1)}, u32[]{:S(2)}, u32[]{:S(2)}) collective-permute-start(bf16[32,4096]{1,0:T(8,128)(2,1)S(1)} %get-tuple-element.24), channel_id=1, source_target_pairs={{0,4},{4,0},{8,12},{12,8},{16,20},{20,16},{24,28},{28,24},{1,5},{5... | collective-permute-start | bytes 786440 | tf_op jit(solution)/shard_map/ppermute | solution.py:319
  13.7 0.8 %copy-start.1 = (bf16[1,8,4096]{2,1,0:T(8,128)(2,1)S(1)}, bf16[1,8,4096]{2,1,0:T(8,128)(2,1)}, u32[]{:S(2)}) copy-start(bf16[1,8,4096]{2,1,0:T(8,128)(2,1)} %param.10) | copy-start | bytes 196612
  13.7 0.9 %copy-start.2 = (bf16[1,8,4096]{2,1,0:T(8,128)(2,1)S(1)}, bf16[1,8,4096]{2,1,0:T(8,128)(2,1)}, u32[]{:S(2)}) copy-start(bf16[1,8,4096]{2,1,0:T(8,128)(2,1)} %param.11) | copy-start | bytes 196612
  14.6 8.6 %collective-permute-start.4 = (bf16[8,4096]{1,0:T(8,128)(2,1)S(1)}, bf16[8,4096]{1,0:T(8,128)(2,1)S(1)}, u32[]{:S(2)}, u32[]{:S(2)}) collective-permute-start(bf16[8,4096]{1,0:T(8,128)(2,1)S(1)} %inputs.1.refs_0_.input_ref), channel_id=1, source_target_pairs={{0,8},{4,12},{8,0},{12,4},{16,24},{20,28},{24,16},{28,20},{1,9},{5... | collective-permute-start | bytes 196616 | tf_op jit(solution)/shard_map/ppermute | solution.py:351
  16.4 7.5 %collective-permute-start.5 = (bf16[8,4096]{1,0:T(8,128)(2,1)S(1)}, bf16[8,4096]{1,0:T(8,128)(2,1)S(1)}, u32[]{:S(2)}, u32[]{:S(2)}) collective-permute-start(bf16[8,4096]{1,0:T(8,128)(2,1)S(1)} %inputs.1.refs_0_.input_ref), channel_id=1, source_target_pairs={{0,16},{4,20},{8,24},{12,28},{16,0},{20,4},{24,8},{28,12},{1,17},{... | collective-permute-start | bytes 196616 | tf_op jit(solution)/shard_map/ppermute | solution.py:351
  18.8 6.2 %collective-permute-start.6 = (bf16[8,4096]{1,0:T(8,128)(2,1)S(1)}, bf16[8,4096]{1,0:T(8,128)(2,1)S(1)}, u32[]{:S(2)}, u32[]{:S(2)}) collective-permute-start(bf16[8,4096]{1,0:T(8,128)(2,1)S(1)} %inputs.1.refs_0_.input_ref), channel_id=1, source_target_pairs={{0,24},{4,28},{8,16},{12,20},{16,8},{20,12},{24,0},{28,4},{1,25},{... | collective-permute-start | bytes 196616 | tf_op jit(solution)/shard_map/ppermute | solution.py:351
  25.0 10.5 %all-to-all-start.1 = ((bf16[8,8,2048]{2,1,0:T(8,128)(2,1)}), bf16[8,8,2048]{2,1,0:T(8,128)(2,1)S(1)}, u32[]{:S(2)}, u32[]{:S(2)}) async-start(bf16[8,8,2048]{2,1,0:T(8,128)(2,1)} %conv.1._), calls=%async_computation.1 | async-start | bytes 524288 | tf_op jit(solution)/shard_map/all_to_all | solution.py:367
  29.9 1.6 %collective-permute-start.7 = (bf16[4,8,4096]{2,1,0:T(8,128)(2,1)S(1)}, bf16[4,8,4096]{2,1,0:T(8,128)(2,1)S(1)}, u32[]{:S(2)}, u32[]{:S(2)}) collective-permute-start(bf16[4,8,4096]{2,1,0:T(8,128)(2,1)S(1)} %get-tuple-element.19.own_stack_ref), channel_id=1, source_target_pairs={{0,4},{4,0},{8,12},{12,8},{16,20},{20,16},{24,28},{28,24},{1,5},{5... | collective-permute-start | bytes 786440 | tf_op jit(solution)/shard_map/ppermute | solution.py:386
  30.1 1.5 %collective-permute-start.8 = (bf16[2,36,128]{2,1,0:T(8,128)(2,1)S(1)}, bf16[2,36,128]{2,1,0:T(8,128)(2,1)S(1)}, u32[]{:S(2)}, u32[]{:S(2)}) collective-permute-start(bf16[2,36,128]{2,1,0:T(8,128)(2,1)S(1)} %get-tuple-element.20.own_head_ref), channel_id=1, source_target_pairs={{0,4},{4,0},{8,12},{12,8},{16,20},{20,16},{24,28},{28,24},{1,5},{5... | collective-permute-start | bytes 55304 | tf_op jit(solution)/shard_map/ppermute | solution.py:387
  31.5 0.7 %copy-start.4 = (s32[1,8,1]{1,2,0:T(1,128)S(1)}, s32[1,8,1]{1,2,0:T(1,128)}, u32[]{:S(2)}) copy-start(s32[1,8,1]{1,2,0:T(1,128)} %param.15) | copy-start | bytes 100
  32.2 3.4 %copy-start.3 = (bf16[1,8,4096]{2,1,0:T(8,128)(2,1)S(1)}, bf16[1,8,4096]{2,1,0:T(8,128)(2,1)}, u32[]{:S(2)}) copy-start(bf16[1,8,4096]{2,1,0:T(8,128)(2,1)} %param.9) | copy-start | bytes 196612
